TPU v7x, 32 devices: a whole 2x2x4 slice. The times are simulated.
32 devices in a mesh: row: 4 (over z), col: 8 (over y, x, core).
Axes of the slice: x: 2, y: 2, z: 4, core: 2. Of those that a mesh axis runs over, the one named last changes fastest.
Arguments:
- row_bases: float32 [4, 128, 4096], P('row', 'col'), may hold values from -4 to 4, as said below
- col_bases: float32 [8, 64, 4096], P('col', 'row'), may hold values from -4 to 4, as said below
- row_transfer: float32 [4, 256, 4096], P('row', 'col'), may hold values from -1 to 1, as said below
- col_transfer: float32 [8, 128, 4096], P('col', 'row'), may hold values from -1 to 1, as said below
- row_order: int32 [4, 8, 16], P('row', 'col'), may hold values from 0 to 15, each once within a row
- col_order: int32 [8, 4, 16], P('col', 'row'), may hold values from 0 to 15, each once within a row
- leaf_pattern: int32 [4, 16, 64], P('row', 'col'), may hold values from 0 to 15
- leaf_blocks: bfloat16 [4, 512, 4096], P('row', 'col'), may hold values from -6 to 6
- root_rows: int32 [4, 8, 32], P('row', 'col'), may hold values from 0 to 7
- root_cols: int32 [4, 8, 32], P('row', 'col'), may hold values from 0 to 3
- root_blocks: bfloat16 [4, 256, 4096], P('row', 'col'), may hold values from -6 to 6
Outputs:
- leaf_coupled: float32 [4, 512, 4096], P('row', 'col')
- root_coupled: float32 [4, 256, 4096], P('row', 'col')
- row_upper_r: float32 [4, 8, 4096], P('row', 'col')
- col_upper_r: float32 [8, 4, 4096], P('col', 'row')
Inputs may be any that keep to these rules, and one draw needn't show every extreme that they name: `row_bases`: every leaf basis has full column rank and every Gram matrix of both trees is well conditioned. `col_bases`: every leaf basis has full column rank and every Gram matrix of both trees is well conditioned. `row_transfer`: every transfer matrix is invertible. `col_transfer`: every transfer matrix is invertible.
All inputs are finite; a program needn't handle non-finite values.
Results may differ from a plain program's by a relative error of at most 0.0003.
Values sent between devices are 32-bit elements; how exact they have to be, the bound alone decides.
No kernel may reach another device: no remote copies, remote signals or barrier semaphores. Data moves between devices by JAX's collectives and lax.ppermute only.
A program may use at most 64 MiB of HBM per device.

v0:
```python
import jax
import jax.numpy as jnp
from jax import lax
from jax.sharding import PartitionSpec as P

LEAF = 64
RANK = 64
LEAF_DEV = 16


def from_partner(value, axis, bit):
    return lax.ppermute(value, axis, [(i, i ^ 1 << bit) for i in range(lax.axis_size(axis))])


def matmul_high(first_matrix, second_matrix):
    return jnp.matmul(first_matrix, second_matrix, precision=lax.Precision.HIGHEST)


def flipped(matrix):
    return jnp.swapaxes(matrix, -1, -2)


def sandwich(gram, transfer):
    return matmul_high(flipped(transfer), matmul_high(gram, transfer))


def upper_factor(gram):
    return flipped(jnp.linalg.cholesky(gram))


def as_row(matrix):
    return matrix.reshape(1, RANK * RANK)


def as_square(vector):
    return vector.reshape(-1, RANK, RANK)


def local_tree(bases, transfer, order):
    leaf_basis = bases.reshape(LEAF_DEV, LEAF, RANK)
    leaf_gram = jnp.einsum("pla,plc->pac", leaf_basis, leaf_basis, precision=lax.Precision.HIGHEST)
    matrices = transfer.reshape(2 * LEAF_DEV, RANK, RANK)
    leaf_picks = order.reshape(LEAF_DEV)
    node_gram = leaf_gram[leaf_picks]
    node_up = matrices[leaf_picks]
    node_count = LEAF_DEV
    offset = LEAF_DEV
    while node_count > 1:
        contribution = sandwich(node_gram, node_up)
        node_gram = contribution[0::2] + contribution[1::2]
        node_count = node_count // 2
        node_up = matrices[offset : offset + node_count]
        offset = offset + node_count
    return (upper_factor(leaf_gram), node_gram[0], node_up[0], matrices[2 * LEAF_DEV - 1])


def doubling(
    dev_gram,
    dev_up,
    inner_up,
    inner_size,
    outer_size,
    inner_place,
    outer_place,
    inner_move,
    outer_move,
):
    current_gram = dev_gram
    current_up = dev_up
    first_inner = inner_up
    highest = dev_gram
    inner_depth = inner_size.bit_length() - 1
    outer_depth = outer_size.bit_length() - 1
    place = outer_place * inner_size + inner_place
    for height in range(inner_depth + outer_depth):
        contribution = sandwich(current_gram, current_up)
        if height < inner_depth:
            received, received_first = inner_move(as_row(contribution), as_row(first_inner), height)
        else:
            received, received_first = outer_move(
                as_row(contribution), as_row(first_inner), height - inner_depth
            )
        span = 1 << height
        upper_half = place // span % 2 == 1
        current_gram = contribution + received.reshape(RANK, RANK)
        highest = jnp.where(place % (2 * span) == span, current_gram, highest)
        partner_first = received_first.reshape(RANK, RANK)
        current_up = jnp.where(upper_half, first_inner, partner_first)
        first_inner = jnp.where(upper_half, partner_first, first_inner)
    return jnp.where(place == 0, current_gram, highest)


def couple(left_table, right_table, left_picks, right_picks, blocks):
    squares = blocks.reshape(-1, RANK, RANK).astype(jnp.float32)
    projected = matmul_high(
        matmul_high(left_table[left_picks], squares), flipped(right_table[right_picks])
    )
    return projected.reshape(1, -1, RANK * RANK)


def body(
    row_bases,
    col_bases,
    row_transfer,
    col_transfer,
    row_order,
    col_order,
    leaf_pattern,
    leaf_blocks,
    root_rows,
    root_cols,
    root_blocks,
):
    row_leaf_r, row_gram, row_up, row_inner = local_tree(row_bases, row_transfer, row_order)
    col_leaf_r, col_gram, col_up, col_inner = local_tree(col_bases, col_transfer, col_order)
    leaf_coupled = couple(
        row_leaf_r, col_leaf_r, leaf_pattern[0, 0], leaf_pattern[0, 1], leaf_blocks
    )
    place_row = lax.axis_index("row")
    place_col = lax.axis_index("col")
    row_high = doubling(
        row_gram,
        row_up,
        row_inner,
        lax.axis_size("col"),
        lax.axis_size("row"),
        place_col,
        place_row,
        lambda first_part, second_part, level: from_partner(
            (first_part, second_part), "col", level
        ),
        lambda first_part, second_part, level: from_partner(
            (first_part, second_part), "row", level
        ),
    )
    col_high = doubling(
        col_gram,
        col_up,
        col_inner,
        lax.axis_size("row"),
        lax.axis_size("col"),
        place_row,
        place_col,
        lambda first_part, second_part, level: from_partner(
            (first_part, second_part), "row", level
        ),
        lambda first_part, second_part, level: from_partner(
            (first_part, second_part), "col", level
        ),
    )
    row_root_r = as_square(
        lax.all_gather(as_row(upper_factor(row_gram)), "col", axis=0, tiled=True)
    )
    col_root_r = as_square(
        lax.all_gather(as_row(upper_factor(col_gram)), "row", axis=0, tiled=True)
    )
    root_coupled = couple(row_root_r, col_root_r, root_rows[0, 0], root_cols[0, 0], root_blocks)
    row_upper_r = upper_factor(row_high).reshape(1, 1, RANK * RANK)
    col_upper_r = upper_factor(col_high).reshape(1, 1, RANK * RANK)
    return (leaf_coupled, root_coupled, row_upper_r, col_upper_r)


def solution(mesh):
    return jax.shard_map(
        body,
        mesh=mesh,
        in_specs=(
            P("row", "col", None),
            P("col", "row", None),
            P("row", "col", None),
            P("col", "row", None),
            P("row", "col", None),
            P("col", "row", None),
            P("row", "col", None),
            P("row", "col", None),
            P("row", "col", None),
            P("row", "col", None),
            P("row", "col", None),
        ),
        out_specs=(
            P("row", "col", None),
            P("row", "col", None),
            P("row", "col", None),
            P("col", "row", None),
        ),
        check_vma=False,
    )
```

profile of v0, /device:TPU:0, one launch (start us, length us, event | category | flops | bytes accessed | tf_op | source)
XLA Modules:
  0.0 338.2 jit_solution(11348281205577940296)
XLA Ops:
  0.7 1.8 slice_reduce_fusion
  2.5 3.1 collective-permute-start.9
  5.6 1.5 reshape.398
  7.0 0.9 slice.140
  8.2 1.0 fusion.70
  11.1 1.0 fusion.76
  16.5 1.1 reshape.389
  17.6 1.0 fusion.68
  19.8 0.8 gather_fusion.2
  21.3 1.0 fusion.73
  27.0 5.8 %cholesky.150 = f32[64,64]{1,0:T(8,128)S(1)} custom-call(f32[64,64]{1,0:T(8,128)S(1)} %fusion.26), custom_call_target="Cholesky" | custom-call | tf_op jit(solution)/shard_map/jit(cholesky)/cholesky | solution.py:28
  34.3 13.9 %all-gather.1 = f32[4,1,4096]{2,1,0:T(1,128)S(1)} all-gather(f32[1,1,4096]{2,1,0:T(1,128)S(1)} %reshape.499), channel_id=1, replica_groups=mesh['row'=4,'col'=8] {'row'}, dimensions={0}, use_global_device_ids=true | all-gather | bytes 81920 | tf_op jit(solution)/shard_map/all_gather | solution.py:155
  48.5 5.8 %cholesky.139 = f32[64,64]{1,0:T(8,128)S(1)} custom-call(f32[64,64]{1,0:T(8,128)S(1)} %fusion.27), custom_call_target="Cholesky" | custom-call | tf_op jit(solution)/shard_map/jit(cholesky)/cholesky | solution.py:28
  55.9 9.2 %all-gather = f32[8,1,4096]{2,1,0:T(1,128)S(1)} all-gather(f32[1,1,4096]{2,1,0:T(1,128)S(1)} %reshape.497), channel_id=1, replica_groups=mesh['row'=4,'col'=8] {'col'}, dimensions={0}, use_global_device_ids=true | all-gather | bytes 147456 | tf_op jit(solution)/shard_map/all_gather | solution.py:152
  65.6 1.5 reshape.397
  67.1 0.9 fusion.1
  67.9 94.5 %custom-call.6 = f32[16,64,64]{2,1,0:T(8,128)S(1)} custom-call(f32[16,64,64]{2,1,0:T(8,128)} %fusion.1), custom_call_target="Cholesky" | custom-call | tf_op jit(solution)/shard_map/jit(cholesky)/cholesky | solution.py:28
  162.5 93.8 %custom-call.7 = f32[16,64,64]{2,1,0:T(8,128)S(1)} custom-call(f32[16,64,64]{2,1,0:T(8,128)S(1)} %fusion), custom_call_target="Cholesky" | custom-call | tf_op jit(solution)/shard_map/jit(cholesky)/cholesky | solution.py:28
  256.3 2.8 reshape.390
  259.1 1.6 gather_fusion.7
  261.3 1.6 fusion.74
  264.1 4.4 %fusion.69 = f32[64,64,64]{2,1,0:T(8,128)} fusion(f32[64,64,64]{1,2,0:T(8,128)S(1)} %gather_fusion, bf16[64,64,64]{2,1,0:T(8,128)(2,1)} %reshape.390), kind=kOutput, calls=%fused_computation.155 | convolution fusion | flops 201326592 | bytes 2621440 | tf_op jit(solution)/shard_map/dot_general | solution.py:16
  268.4 2.0 gather_fusion.1
  270.4 4.5 %fusion.71 = f32[64,64,64]{2,1,0:T(8,128)S(1)} fusion(f32[64,64,64]{2,1,0:T(8,128)} %fusion.69, f32[64,64,64]{1,2,0:T(8,128)} %gather_fusion.1), kind=kOutput, calls=%fused_computation.157 | convolution fusion | flops 201326592 | bytes 3145728 | tf_op jit(solution)/shard_map/dot_general | solution.py:16
  275.0 1.8 fusion.77
  277.3 1.2 reshape.402
  278.5 1.6 reshape.392
  280.7 1.5 fusion.62
  283.0 1.5 reduce.93
  284.9 1.5 fusion.65
  288.3 2.4 collective-permute-start.14
  290.7 1.5 collective-permute-start.1
  292.7 0.7 fusion.63
  293.5 1.0 collective-permute-done.1
  294.6 0.7 fusion.66
  295.5 0.7 reduce.94
  296.4 1.4 collective-permute-start.2
  298.8 0.7 fusion.64
  299.6 0.7 collective-permute-start.12
  300.3 0.7 fusion.67
  301.2 1.5 collective-permute-start.3
  306.6 1.4 collective-permute-start.6
  309.3 0.7 collective-permute-start.16
  311.9 1.5 collective-permute-start.7
  314.8 1.4 collective-permute-start.17
  317.8 2.4 collective-permute-start.8
  321.2 5.8 %cholesky.172 = f32[64,64]{1,0:T(8,128)S(1)} custom-call(f32[64,64]{1,0:T(8,128)S(1)} %fusion.28), custom_call_target="Cholesky" | custom-call | tf_op jit(solution)/shard_map/jit(cholesky)/cholesky | solution.py:28
  330.2 5.8 %cholesky.161 = f32[64,64]{1,0:T(8,128)S(1)} custom-call(f32[64,64]{1,0:T(8,128)S(1)} %fusion.29), custom_call_target="Cholesky" | custom-call | tf_op jit(solution)/shard_map/jit(cholesky)/cholesky | solution.py:28
  (231 shorter events, 40.2 us)
Async XLA Ops:
  0.6 7.3 %copy-start.2 = (f32[1,32,4096]{2,1,0:T(8,128)S(1)}, f32[1,32,4096]{2,1,0:T(8,128)}, u32[]{:S(2)}) copy-start(f32[1,32,4096]{2,1,0:T(8,128)} %param.16) | copy-start | bytes 1572868
  0.6 7.3 %copy-start.8 = (s32[1,1,16]{2,1,0:T(1,128)S(1)}, s32[1,1,16]{2,1,0:T(1,128)}, u32[]{:S(2)}) copy-start(s32[1,1,16]{2,1,0:T(1,128)} %param.18) | copy-start | bytes 196
  0.7 7.3 %copy-start.6 = (f32[1,16,4096]{2,1,0:T(8,128)S(1)}, f32[1,16,4096]{2,1,0:T(8,128)}, u32[]{:S(2)}) copy-start(f32[1,16,4096]{2,1,0:T(8,128)} %param.14) | copy-start | bytes 786436
  2.5 277.6 %collective-permute-start.9 = (f32[1,4096]{1,0:T(1,128)}, f32[1,4096]{1,0:T(1,128)}, u32[]{:S(2)}, u32[]{:S(2)}) collective-permute-start(f32[1,4096]{1,0:T(1,128)} %get-tuple-element.18), channel_id=1, source_target_pairs={{0,8},{8,0},{16,24},{24,16},{1,9},{9,1},{17,25},{25,17},{2,10},{10... | collective-permute-start | bytes 49160 | tf_op jit(solution)/shard_map/ppermute | solution.py:12
  9.8 2.3 slice-start
  12.1 3.8 %copy-start.4 = (f32[1,32,4096]{2,1,0:T(8,128)S(1)}, f32[1,32,4096]{2,1,0:T(8,128)}, u32[]{:S(2)}) copy-start(f32[1,32,4096]{2,1,0:T(8,128)} %param.15) | copy-start | bytes 1572868
  13.2 3.2 copy-start.9
  16.0 267.0 %collective-permute-start.13 = (f32[1,4096]{1,0:T(1,128)}, f32[1,4096]{1,0:T(1,128)}, u32[]{:S(2)}, u32[]{:S(2)}) collective-permute-start(f32[1,4096]{1,0:T(1,128)} %reshape.422), channel_id=1, source_target_pairs={{0,8},{8,0},{16,24},{24,16},{1,9},{9,1},{17,25},{25,17},{2,10},{10... | collective-permute-start | bytes 49160 | tf_op jit(solution)/shard_map/ppermute | solution.py:12
  16.0 268.9 %collective-permute-start = (f32[1,4096]{1,0:T(1,128)}, f32[1,4096]{1,0:T(1,128)}, u32[]{:S(2)}, u32[]{:S(2)}) collective-permute-start(f32[1,4096]{1,0:T(1,128)} %get-tuple-element.46), channel_id=1, source_target_pairs={{0,1},{1,0},{2,3},{3,2},{4,5},{5,4},{6,7},{7,6},{8,9},{9,8},{10,11... | collective-permute-start | bytes 49160 | tf_op jit(solution)/shard_map/ppermute | solution.py:12
  19.8 2.5 slice-start.1
  24.0 24.5 %copy-start.10 = (s32[1,1,32]{2,1,0:T(1,128)S(1)}, s32[1,1,32]{2,1,0:T(1,128)}, u32[]{:S(2)}) copy-start(s32[1,1,32]{2,1,0:T(1,128)} %param.22) | copy-start | bytes 388
  25.5 40.1 %copy-start.11 = (s32[1,1,32]{2,1,0:T(1,128)S(1)}, s32[1,1,32]{2,1,0:T(1,128)}, u32[]{:S(2)}) copy-start(s32[1,1,32]{2,1,0:T(1,128)} %param.21) | copy-start | bytes 388
  25.6 261.0 %collective-permute-start.4 = (f32[1,4096]{1,0:T(1,128)S(1)}, f32[1,4096]{1,0:T(1,128)S(1)}, u32[]{:S(2)}, u32[]{:S(2)}) collective-permute-start(f32[1,4096]{1,0:T(1,128)S(1)} %reshape.407), channel_id=1, source_target_pairs={{0,1},{1,0},{2,3},{3,2},{4,5},{5,4},{6,7},{7,6},{8,9},{9,8},{10,11... | collective-permute-start | bytes 49160 | tf_op jit(solution)/shard_map/ppermute | solution.py:12
  65.4 190.8 %copy-start.7 = (s32[1,2,64]{2,1,0:T(2,128)S(1)}, s32[1,2,64]{2,1,0:T(2,128)}, u32[]{:S(2)}) copy-start(s32[1,2,64]{2,1,0:T(2,128)} %param.19) | copy-start | bytes 1540
  270.4 4.5 %copy-start = (f32[32,64,64]{2,1,0:T(8,128)S(1)}, f32[32,64,64]{2,1,0:T(8,128)}, u32[]{:S(2)}) copy-start(f32[32,64,64]{2,1,0:T(8,128)} %gather_fusion.7) | copy-start | bytes 1572868
  270.4 4.6 %copy-start.1 = (f32[32,64,64]{2,1,0:T(8,128)S(1)}, f32[32,64,64]{2,1,0:T(8,128)}, u32[]{:S(2)}) copy-start(f32[32,64,64]{2,1,0:T(8,128)} %fusion.74) | copy-start | bytes 1572868
  278.5 2.2 copy-start.3
  278.5 6.4 %copy-start.5 = (f32[1,32,4096]{2,1,0:T(8,128)S(1)}, f32[1,32,4096]{2,1,0:T(8,128)}, u32[]{:S(2)}) copy-start(f32[1,32,4096]{2,1,0:T(8,128)} %param.15) | copy-start | bytes 1572868
  282.2 10.5 %collective-permute-start.10 = (f32[1,4096]{1,0:T(1,128)S(1)}, f32[1,4096]{1,0:T(1,128)S(1)}, u32[]{:S(2)}, u32[]{:S(2)}) collective-permute-start(f32[1,4096]{1,0:T(1,128)S(1)} %get-tuple-element.21), channel_id=1, source_target_pairs={{0,16},{8,24},{16,0},{24,8},{1,17},{9,25},{17,1},{25,9},{2,18},{10... | collective-permute-start | bytes 49160 | tf_op jit(solution)/shard_map/ppermute | solution.py:12
  288.3 7.2 %collective-permute-start.14 = (f32[1,4096]{1,0:T(1,128)S(1)}, f32[1,4096]{1,0:T(1,128)S(1)}, u32[]{:S(2)}, u32[]{:S(2)}) collective-permute-start(f32[1,4096]{1,0:T(1,128)S(1)} %reshape.424), channel_id=1, source_target_pairs={{0,16},{8,24},{16,0},{24,8},{1,17},{9,25},{17,1},{25,9},{2,18},{10... | collective-permute-start | bytes 49160 | tf_op jit(solution)/shard_map/ppermute | solution.py:12
  290.7 3.9 %collective-permute-start.1 = (f32[1,4096]{1,0:T(1,128)S(1)}, f32[1,4096]{1,0:T(1,128)S(1)}, u32[]{:S(2)}, u32[]{:S(2)}) collective-permute-start(f32[1,4096]{1,0:T(1,128)S(1)} %get-tuple-element.27), channel_id=1, source_target_pairs={{0,2},{1,3},{2,0},{3,1},{4,6},{5,7},{6,4},{7,5},{8,10},{9,11},{10,... | collective-permute-start | bytes 49160 | tf_op jit(solution)/shard_map/ppermute | solution.py:12
  292.2 5.7 %collective-permute-start.5 = (f32[1,4096]{1,0:T(1,128)S(1)}, f32[1,4096]{1,0:T(1,128)S(1)}, u32[]{:S(2)}, u32[]{:S(2)}) collective-permute-start(f32[1,4096]{1,0:T(1,128)S(1)} %reshape.409), channel_id=1, source_target_pairs={{0,2},{1,3},{2,0},{3,1},{4,6},{5,7},{6,4},{7,5},{8,10},{9,11},{10,... | collective-permute-start | bytes 49160 | tf_op jit(solution)/shard_map/ppermute | solution.py:12
  293.5 5.3 %collective-permute-start.11 = (f32[1,4096]{1,0:T(1,128)S(1)}, f32[1,4096]{1,0:T(1,128)S(1)}, u32[]{:S(2)}, u32[]{:S(2)}) collective-permute-start(f32[1,4096]{1,0:T(1,128)S(1)} %get-tuple-element.23), channel_id=1, source_target_pairs={{0,1},{1,0},{2,3},{3,2},{4,5},{5,4},{6,7},{7,6},{8,9},{9,8},{10,11... | collective-permute-start | bytes 49160 | tf_op jit(solution)/shard_map/ppermute | solution.py:12
  296.4 3.9 %collective-permute-start.2 = (f32[1,4096]{1,0:T(1,128)S(1)}, f32[1,4096]{1,0:T(1,128)S(1)}, u32[]{:S(2)}, u32[]{:S(2)}) collective-permute-start(f32[1,4096]{1,0:T(1,128)S(1)} %get-tuple-element.29), channel_id=1, source_target_pairs={{0,4},{1,5},{2,6},{3,7},{4,0},{5,1},{6,2},{7,3},{8,12},{9,13},{10,... | collective-permute-start | bytes 49160 | tf_op jit(solution)/shard_map/ppermute | solution.py:12
  299.6 3.8 %collective-permute-start.12 = (f32[1,4096]{1,0:T(1,128)S(1)}, f32[1,4096]{1,0:T(1,128)S(1)}, u32[]{:S(2)}, u32[]{:S(2)}) collective-permute-start(f32[1,4096]{1,0:T(1,128)S(1)} %get-tuple-element.25), channel_id=1, source_target_pairs={{0,2},{1,3},{2,0},{3,1},{4,6},{5,7},{6,4},{7,5},{8,10},{9,11},{10,... | collective-permute-start | bytes 49160 | tf_op jit(solution)/shard_map/ppermute | solution.py:12
  301.2 3.8 %collective-permute-start.3 = (f32[1,4096]{1,0:T(1,128)S(1)}, f32[1,4096]{1,0:T(1,128)S(1)}, u32[]{:S(2)}, u32[]{:S(2)}) collective-permute-start(f32[1,4096]{1,0:T(1,128)S(1)} %get-tuple-element.31), channel_id=1, source_target_pairs={{0,8},{8,0},{16,24},{24,16},{1,9},{9,1},{17,25},{25,17},{2,10},{10... | collective-permute-start | bytes 49160 | tf_op jit(solution)/shard_map/ppermute | solution.py:12
  304.8 3.2 collective-permute-start.15
  306.6 3.8 %collective-permute-start.6 = (f32[1,4096]{1,0:T(1,128)S(1)}, f32[1,4096]{1,0:T(1,128)S(1)}, u32[]{:S(2)}, u32[]{:S(2)}) collective-permute-start(f32[1,4096]{1,0:T(1,128)S(1)} %reshape.411), channel_id=1, source_target_pairs={{0,4},{1,5},{2,6},{3,7},{4,0},{5,1},{6,2},{7,3},{8,12},{9,13},{10,... | collective-permute-start | bytes 49160 | tf_op jit(solution)/shard_map/ppermute | solution.py:12
  309.3 4.1 %collective-permute-start.16 = (f32[1,4096]{1,0:T(1,128)S(1)}, f32[1,4096]{1,0:T(1,128)S(1)}, u32[]{:S(2)}, u32[]{:S(2)}) collective-permute-start(f32[1,4096]{1,0:T(1,128)S(1)} %reshape.428), channel_id=1, source_target_pairs={{0,2},{1,3},{2,0},{3,1},{4,6},{5,7},{6,4},{7,5},{8,10},{9,11},{10,... | collective-permute-start | bytes 49160 | tf_op jit(solution)/shard_map/ppermute | solution.py:12
  311.9 4.4 %collective-permute-start.7 = (f32[1,4096]{1,0:T(1,128)S(1)}, f32[1,4096]{1,0:T(1,128)S(1)}, u32[]{:S(2)}, u32[]{:S(2)}) collective-permute-start(f32[1,4096]{1,0:T(1,128)S(1)} %reshape.413), channel_id=1, source_target_pairs={{0,8},{8,0},{16,24},{24,16},{1,9},{9,1},{17,25},{25,17},{2,10},{10... | collective-permute-start | bytes 49160 | tf_op jit(solution)/shard_map/ppermute | solution.py:12
  314.8 5.4 %collective-permute-start.17 = (f32[1,4096]{1,0:T(1,128)S(1)}, f32[1,4096]{1,0:T(1,128)S(1)}, u32[]{:S(2)}, u32[]{:S(2)}) collective-permute-start(f32[1,4096]{1,0:T(1,128)S(1)} %reshape.430), channel_id=1, source_target_pairs={{0,4},{1,5},{2,6},{3,7},{4,0},{5,1},{6,2},{7,3},{8,12},{9,13},{10,... | collective-permute-start | bytes 49160 | tf_op jit(solution)/shard_map/ppermute | solution.py:12
  317.8 11.4 %collective-permute-start.8 = (f32[1,4096]{1,0:T(1,128)S(1)}, f32[1,4096]{1,0:T(1,128)S(1)}, u32[]{:S(2)}, u32[]{:S(2)}) collective-permute-start(f32[1,4096]{1,0:T(1,128)S(1)} %reshape.415), channel_id=1, source_target_pairs={{0,16},{8,24},{16,0},{24,8},{1,17},{9,25},{17,1},{25,9},{2,18},{10... | collective-permute-start | bytes 49160 | tf_op jit(solution)/shard_map/ppermute | solution.py:12
where the time goes:
time: 339 us; the launch traced here: 338 us
  other arithmetic  235 us (69%)
  local copies, waits for them, and re-layouts  30.2 us (9%)
  matrix products  26 us (8%)
  blocking collectives  23.1 us (7%)
  starting transfers between devices  20 us (6%)
    another operation x17, other arithmetic, upper_factor(): return flipped(jnp.linalg.cholesky(gram))  215 us
    dot_general x40, matrix products, matmul_high(): jnp.matmul(first_matrix, second_matrix, precision=lax.Precision.HIGHEST)  24 us
    ppermute x18, starting transfers between devices, from_partner(): lax.ppermute(value, axis, [(i, i ^ 1 << bit) for i in range(lax.axis_size...  20 us
    ppermute x18, other arithmetic, from_partner(): lax.ppermute(value, axis, [(i, i ^ 1 << bit) for i in range(lax.axis_size...  15.3 us
    all_gather x1, blocking collectives, body(): lax.all_gather(as_row(upper_factor(col_gram)), 'row', axis=0, tiled=True)  13.9 us
    all_gather x1, blocking collectives, body(): lax.all_gather(as_row(upper_factor(row_gram)), 'col', axis=0, tiled=True)  9.22 us
  transfers between devices with their start and end apart: 18, of which 4 were waited for; matrix products, arithmetic and copies ran while one was open for 83% of the time, Pallas kernels for 0%

commit v1 on v0

v1 whole, which is shorter than its diff:
```python
import functools

import jax
import jax.numpy as jnp
from jax import lax
from jax.experimental import pallas as pl
from jax.experimental.pallas import tpu as pltpu
from jax.sharding import PartitionSpec as P

RANK = 64
WIDE = 2 * RANK
SUB = 8
NB = RANK // SUB
F32 = jnp.float32
BF16 = jnp.bfloat16
VMEM = pl.BlockSpec(memory_space=pltpu.VMEM)
SMEM = pl.BlockSpec(memory_space=pltpu.SMEM)


def split(x):
    high = x.astype(BF16)
    return high, (x - high.astype(F32)).astype(BF16)


def dot(a, b, rhs_dim=0):
    return lax.dot_general(a, b, (((1,), (rhs_dim,)), ((), ())), preferred_element_type=F32)


def dot3(a, b, rhs_dim=0):
    a_high, a_low = split(a)
    b_high, b_low = split(b)
    return dot(a_high, b_high, rhs_dim) + (dot(a_high, b_low, rhs_dim) + dot(a_low, b_high, rhs_dim))


def lane_half(rows):
    return lax.broadcasted_iota(jnp.int32, (rows, WIDE), 1) < RANK


def swapped(x):
    return pltpu.roll(x, RANK, 1)


def beside(left, right):
    return jnp.where(lane_half(left.shape[0]), left, right)


def sandwich_both(gram, transfer):
    t = transfer.T
    x = dot3(t, gram)
    x = jnp.concatenate([x[:RANK], swapped(x[RANK:])], axis=0)[:, :RANK]
    y = dot3(x, transfer)
    return beside(y[:RANK], y[RANK:])


def unpack_both(left_ref, right_ref, out_ref, count):
    for k in range(RANK // 2):
        a = left_ref[0, :, k * WIDE : (k + 1) * WIDE]
        b = right_ref[0, :, k * WIDE : (k + 1) * WIDE]
        out_ref[pl.ds(2 * k, count, stride=RANK), :] = beside(a, swapped(b))
        out_ref[pl.ds(2 * k + 1, count, stride=RANK), :] = beside(swapped(a), b)


def tree_kernel(
    count,
    row_order,
    col_order,
    row_bases,
    col_bases,
    row_transfer,
    col_transfer,
    leaf_gram,
    row_pay,
    col_pay,
    high,
    basis,
    trans,
):
    unpack_both(row_bases, col_bases, basis, count)
    unpack_both(row_transfer, col_transfer, trans, 2 * count)
    for leaf in range(count):
        u = basis[leaf * RANK : (leaf + 1) * RANK, :]
        g = dot3(u.T, u)
        leaf_gram[leaf * RANK : (leaf + 1) * RANK, :] = beside(g[:RANK], g[RANK:])
    nodes = []
    for q in range(count // 2):
        total = None
        for p in (2 * q, 2 * q + 1):
            r = pl.ds(pl.multiple_of(row_order[0, 0, p] * RANK, RANK), RANK)
            c = pl.ds(pl.multiple_of(col_order[0, 0, p] * RANK, RANK), RANK)
            term = sandwich_both(
                beside(leaf_gram[r, :], leaf_gram[c, :]), beside(trans[r, :], trans[c, :])
            )
            total = term if total is None else total + term
        nodes.append(total)
    offset = count
    while len(nodes) > 1:
        terms = []
        for q, gram in enumerate(nodes):
            terms.append(
                sandwich_both(gram, trans[(offset + q) * RANK : (offset + q + 1) * RANK, :])
            )
        offset += len(nodes)
        nodes = [terms[2 * q] + terms[2 * q + 1] for q in range(len(terms) // 2)]
    gram = nodes[0]
    term = sandwich_both(gram, trans[offset * RANK : (offset + 1) * RANK, :])
    first = trans[(offset + 1) * RANK : (offset + 2) * RANK, :]
    high[...] = gram
    row_pay[0:RANK, :] = beside(term, swapped(first))
    row_pay[RANK:WIDE, :] = gram
    col_pay[0:RANK, :] = beside(swapped(term), first)
    col_pay[RANK:WIDE, :] = swapped(gram)


def step_kernel(trees, last, held, extra, flags, own, recv, high_in, *refs):
    refs = list(refs)
    before = refs.pop(0) if extra else None
    pay_out = refs.pop(0) if len(trees) > len(last) or held else None
    high_out = refs.pop(0)
    base = 0
    if extra:
        pay_out[0:RANK, :] = before[0:RANK, :]
        base = RANK
    high = high_in[...]
    for slot, name in enumerate(trees):
        upper = flags[2 * slot] > 0
        take = flags[2 * slot + 1] > 0
        mine = own[slot * RANK : (slot + 1) * RANK, :]
        theirs = recv[slot * RANK : (slot + 1) * RANK, :]
        total = mine + theirs
        picked = beside(total, high) if name == "r" else beside(high, swapped(total))
        high = jnp.where(take, picked, high)
        if name not in last:
            transfer = jnp.where(upper, mine, theirs)
            first = jnp.where(upper, theirs, mine)
            x = dot3(transfer.T[RANK:], total[:, :RANK])
            term = swapped(dot3(x, transfer))
            pay_out[base : base + RANK, :] = beside(term, first)
            base += RANK
    high_out[...] = high
    if extra:
        pay_out[base : base + RANK, :] = before[RANK:WIDE, :]
    elif held:
        upper = flags[0] > 0
        start = len(trees) * RANK
        if held == 1:
            mine = own[start : start + RANK, :]
            theirs = recv[start : start + RANK, :]
            pay_out[base : base + RANK, :] = jnp.where(
                upper, beside(theirs, swapped(mine)), beside(mine, swapped(theirs))
            )
        else:
            rows = held // 2 * RANK
            mine = own[start : start + rows, :]
            theirs = recv[start : start + rows, :]
            pay_out[base : base + rows, :] = jnp.where(upper, theirs, mine)
            pay_out[base + rows : base + 2 * rows, :] = jnp.where(upper, mine, theirs)


def chol_lanes(a_ref, r_ref):
    sub = lax.broadcasted_iota(jnp.int32, (SUB, WIDE), 0)

    def at(q):
        return slice(SUB * q, SUB * (q + 1))

    def spread(i, j):
        return r_ref[i, pl.ds(j, SUB, stride=0), :]

    def less(value, f, row):
        return lax.sub(value, lax.mul(f, row))

    for p in range(NB):
        i0 = SUB * p
        acc = [a_ref[i0 + r, at(p), :] for r in range(SUB)]
        scale = []
        for r in range(SUB):
            inv = lax.rsqrt(jnp.broadcast_to(acc[r][r : r + 1, :], (SUB, WIDE)))
            scale.append(inv)
            row = jnp.where(sub >= r, acc[r] * inv, 0.0)
            r_ref[i0 + r, at(p), :] = row
            for r2 in range(r + 1, SUB):
                acc[r2] = less(acc[r2], jnp.broadcast_to(row[r2 : r2 + 1, :], (SUB, WIDE)), row)
        for q in range(p + 1, NB):
            x = [a_ref[i0 + r, at(q), :] for r in range(SUB)]
            for r in range(SUB):
                x[r] = lax.mul(x[r], scale[r])
                r_ref[i0 + r, at(q), :] = x[r]
                for r2 in range(r + 1, SUB):
                    x[r2] = less(x[r2], spread(i0 + r, i0 + r2), x[r])
        for pi in range(p + 1, NB):
            for q0 in range(pi, NB, 2):
                qs = range(q0, min(q0 + 2, NB))
                acc2 = {(r, q): a_ref[SUB * pi + r, at(q), :] for r in range(SUB) for q in qs}
                for k in range(SUB):
                    rows = {q: r_ref[i0 + k, at(q), :] for q in qs}
                    for r in range(SUB):
                        f = spread(i0 + k, SUB * pi + r)
                        for q in qs:
                            acc2[r, q] = less(acc2[r, q], f, rows[q])
                for (r, q), value in acc2.items():
                    a_ref[SUB * pi + r, at(q), :] = value


def load_lanes(slots_ref, a_ref, count):
    for i in range(RANK):
        b0 = SUB * (i // SUB)
        t = slots_ref[pl.ds(i, count, stride=RANK), :].T
        a_ref[i, b0:RANK, 0 : 2 * count] = jnp.concatenate([t[b0:RANK], t[RANK + b0 :]], axis=1)


def factor_row(r_ref, i, lanes):
    b0 = SUB * (i // SUB)
    t = r_ref[i, b0:RANK, 0:lanes]
    if b0:
        t = jnp.concatenate([jnp.zeros((b0, lanes), F32), t], axis=0)
    return t.T


def chol_table_kernel(count, sources, *refs):
    inputs = refs[: len(sources)]
    table, a_ref, r_ref = refs[len(sources) : len(sources) + 3]
    if len(sources) > 1:
        slots = refs[len(sources) + 3]
        base = 0
        for ref, (start, rows) in zip(inputs, sources):
            slots[base : base + rows, :] = ref[start : start + rows, :]
            base += rows
    else:
        slots = inputs[0]
    load_lanes(slots, a_ref, count)
    chol_lanes(a_ref, r_ref)
    for i in range(RANK):
        table[pl.ds(i, 2 * count, stride=RANK), :] = factor_row(r_ref, i, 2 * count)


def final_kernel(high, row_out, col_out, slots, a_ref, r_ref):
    slots[0:RANK, :] = high[...]
    load_lanes(slots, a_ref, SUB)
    chol_lanes(a_ref, r_ref)
    for k in range(RANK // 2):
        even = factor_row(r_ref, 2 * k, 2 * SUB)
        odd = factor_row(r_ref, 2 * k + 1, 2 * SUB)
        both = jnp.concatenate([even, odd], axis=1)
        row_out[0, 0:1, k * WIDE : (k + 1) * WIDE] = both[0:1]
        col_out[0, 0:1, k * WIDE : (k + 1) * WIDE] = both[SUB : SUB + 1]


def couple_kernel(pairs, left_of, right_of, left_pick, right_pick, table, blocks, out, s_ref, y_ref):
    for k in range(RANK // 2):
        slab = blocks[0, :, k * WIDE : (k + 1) * WIDE].astype(F32)
        s_ref[pl.ds(2 * k, pairs, stride=RANK), :] = slab[:, :RANK]
        s_ref[pl.ds(2 * k + 1, pairs, stride=RANK), :] = swapped(slab)[:, :RANK]

    def one(b, carry):
        t = pl.multiple_of(left_of(left_pick, b) * RANK, RANK)
        s = pl.multiple_of(right_of(right_pick, b) * RANK, RANK)
        at = pl.ds(pl.multiple_of(b * RANK, RANK), RANK)
        left_high, left_low = split(table[pl.ds(t, RANK), :])
        block = s_ref[at, :].astype(BF16)
        x = dot(left_high, block) + dot(left_low, block)
        y_ref[at, :] = dot3(x, table[pl.ds(s, RANK), :], 1)
        return carry

    lax.fori_loop(0, pairs, one, 0, unroll=8)
    for k in range(RANK // 2):
        even = y_ref[pl.ds(2 * k, pairs, stride=RANK), :]
        odd = y_ref[pl.ds(2 * k + 1, pairs, stride=RANK), :]
        out[0, :, k * WIDE : (k + 1) * WIDE] = jnp.concatenate([even, odd], axis=1)


def shape(*dims):
    return jax.ShapeDtypeStruct(dims, F32)


def scratch(rows, lanes=WIDE):
    return pltpu.VMEM((rows, lanes), F32)


def call(kernel, outs, specs, name, scratches=(), flops=0, moved=0):
    return pl.pallas_call(
        kernel,
        out_shape=outs,
        in_specs=specs,
        out_specs=jax.tree.map(lambda _: VMEM, outs),
        scratch_shapes=list(scratches),
        name=name,
        cost_estimate=pl.CostEstimate(flops=flops, bytes_accessed=moved, transcendentals=0),
    )


def partner(value, axis, bit):
    return lax.ppermute(value, axis, [(i, i ^ 1 << bit) for i in range(lax.axis_size(axis))])


def body(
    row_bases,
    col_bases,
    row_transfer,
    col_transfer,
    row_order,
    col_order,
    leaf_pattern,
    leaf_blocks,
    root_rows,
    root_cols,
    root_blocks,
):
    count = row_bases.shape[1]
    leaf_pairs = leaf_blocks.shape[1]
    root_pairs = root_blocks.shape[1]
    nr, nc = lax.axis_size("row"), lax.axis_size("col")
    lr, lc = nr.bit_length() - 1, nc.bit_length() - 1
    i, j = lax.axis_index("row"), lax.axis_index("col")
    place = {"r": i * nc + j, "c": j * nr + i}

    leaf_gram, row_pay, col_pay, high = call(
        functools.partial(tree_kernel, count),
        [shape(count * RANK, WIDE), shape(WIDE, WIDE), shape(WIDE, WIDE), shape(RANK, WIDE)],
        [SMEM, SMEM, VMEM, VMEM, VMEM, VMEM],
        "local_tree",
        [scratch(count * RANK), scratch(2 * count * RANK)],
    )(row_order, col_order, row_bases, col_bases, row_transfer, col_transfer)

    def flags(levels):
        values = []
        for name, level in levels:
            span = 1 << level
            d = place[name]
            take = d % (2 * span) == span
            if level == lr + lc - 1:
                take = take | (d == 0)
            values += [(d // span) % 2, take.astype(jnp.int32)]
        return jnp.stack(values)

    def step(levels, pay, axis, bit, high, held=0, extra=None):
        trees = tuple(name for name, _ in levels)
        last = tuple(name for name, level in levels if level == lr + lc - 1)
        recv = partner(pay, axis, bit)
        rows = (len(trees) - len(last)) * RANK + held * RANK
        if extra is not None:
            rows = (len(trees) - len(last)) * RANK + WIDE
        outs = [shape(RANK, WIDE)]
        if rows:
            outs = [shape(rows, WIDE)] + outs
        args = [flags(levels), pay, recv, high] + ([] if extra is None else [extra])
        result = call(
            functools.partial(step_kernel, trees, last, held, extra is not None),
            outs,
            [SMEM] + [VMEM] * (len(args) - 1),
            "step",
        )(*args)
        return list(result) if rows else [None, *result]

    pay = col_pay
    for h in range(lr):
        pay, high = step([("c", h)], pay, "row", h, high, held=1 << h)
    col_roots = pay
    pay = jnp.concatenate([row_pay[:RANK], pay[:RANK], row_pay[RANK:]], axis=0)
    for h in range(lc):
        pay, high = step([("r", h), ("c", lr + h)], pay, "col", h, high, held=1 << h)
    row_roots = pay
    pay = pay[:RANK]
    for h in range(lr):
        pay, high = step([("r", lc + h)], pay, "row", h, high)

    big = [pltpu.VMEM((RANK, RANK, WIDE), F32)] * 2
    leaf_table = call(
        functools.partial(chol_table_kernel, count, ((0, count * RANK),)),
        shape(2 * count * RANK, RANK),
        [VMEM],
        "leaf_factors",
        big,
    )(leaf_gram)
    leaf_coupled = call(
        functools.partial(
            couple_kernel,
            leaf_pairs,
            lambda ref, b: ref[0, 0, b],
            lambda ref, b: ref[0, 1, b] + count,
        ),
        shape(1, leaf_pairs, RANK * RANK),
        [SMEM, SMEM, VMEM, VMEM],
        "leaf_couple",
        [scratch(leaf_pairs * RANK, RANK), scratch(leaf_pairs * RANK, RANK)],
    )(leaf_pattern, leaf_pattern, leaf_table, leaf_blocks)

    row_slots, col_slots = nc // 2, nr // 2
    slots = -(-(row_slots + col_slots) // SUB) * SUB
    root_table = call(
        functools.partial(
            chol_table_kernel,
            slots,
            ((row_roots.shape[0] - row_slots * RANK, row_slots * RANK), (RANK, col_slots * RANK)),
        ),
        shape(2 * slots * RANK, RANK),
        [VMEM, VMEM],
        "root_factors",
        big + [scratch(slots * RANK)],
    )(row_roots, col_roots)
    root_coupled = call(
        functools.partial(
            couple_kernel,
            root_pairs,
            lambda ref, b: (ref[0, 0, b] & 1) * slots + (ref[0, 0, b] >> 1),
            lambda ref, b: (ref[0, 0, b] & 1) * slots + (ref[0, 0, b] >> 1) + row_slots,
        ),
        shape(1, root_pairs, RANK * RANK),
        [SMEM, SMEM, VMEM, VMEM],
        "root_couple",
        [scratch(root_pairs * RANK, RANK), scratch(root_pairs * RANK, RANK)],
    )(root_rows, root_cols, root_table, root_blocks)

    row_upper_r, col_upper_r = call(
        final_kernel,
        [shape(1, 1, RANK * RANK), shape(1, 1, RANK * RANK)],
        [VMEM],
        "upper_factors",
        [scratch(SUB * RANK)] + big,
    )(high)
    return (leaf_coupled, root_coupled, row_upper_r, col_upper_r)


def solution(mesh):
    return jax.shard_map(
        body,
        mesh=mesh,
        in_specs=(
            P("row", "col", None),
            P("col", "row", None),
            P("row", "col", None),
            P("col", "row", None),
            P("row", "col", None),
            P("col", "row", None),
            P("row", "col", None),
            P("row", "col", None),
            P("row", "col", None),
            P("row", "col", None),
            P("row", "col", None),
        ),
        out_specs=(
            P("row", "col", None),
            P("row", "col", None),
            P("row", "col", None),
            P("col", "row", None),
        ),
        check_vma=False,
    )
```

time: 339 us -> 96.4 us (0.28)
  other arithmetic: 235 us -> 4.5 us
  Pallas kernels: 0 us -> 58.7 us
  matrix products: 26 us -> 0 us
  local copies, waits for them, and re-layouts: 30.2 us -> 6.75 us
  blocking collectives: 23.1 us -> 0 us
  waiting for transfers between devices: 1.9 us -> 10.3 us
  starting transfers between devices: 20 us -> 14.6 us
    another operation x17 -> x7, other arithmetic: 215 us -> 4.49 us  [flags(): return jnp.stack(values)]
    pallas_call x0 -> x13, Pallas kernels: none -> 58.7 us  [the longest x7 13.4 us: step(): call(functools.partial(step_kernel, trees, last, held, extra is not None)...]
    dot_general x42 -> x0, matrix products: 26 us -> none  [the longest x40 24 us: matmul_high(): jnp.matmul(first_matrix, second_matrix, precision=lax.Precision.HIGHEST)]
    all_gather x2 -> x0, blocking collectives: 23.1 us -> none  [the longest x1 13.9 us: body(): lax.all_gather(as_row(upper_factor(col_gram)), 'row', axis=0, tiled=True)]
    reshape x58 -> x0, local copies, waits for them, and re-layouts: 16 us -> none  [the longest x2 4.23 us: couple(): squares = blocks.reshape(-1, RANK, RANK).astype(jnp.float32)]
    ppermute x18 -> x0, other arithmetic: 15.3 us -> none  [from_partner(): lax.ppermute(value, axis, [(i, i ^ 1 << bit) for i in range(lax.axis_size...]
    ppermute x18 -> x7, waiting for transfers between devices: 1.9 us -> 10.3 us  [partner(): lax.ppermute(value, axis, [(i, i ^ 1 << bit) for i in range(lax.axis_size...]
    gather x8 -> x0, local copies, waits for them, and re-layouts: 7.48 us -> none  [the longest x2 3.6 us: couple(): right_table[right_picks]]
  transfers between devices with their start and end apart: 18 -> 7, of which waited for: 4 -> 6; matrix products, arithmetic and copies ran while one was open for 83% -> 5% of each run, Pallas kernels for 0% -> 34%
where the time goes in v1:
time: 96.4 us; the launch traced here: 95.6 us
  Pallas kernels  58.7 us (61%)
  starting transfers between devices  14.6 us (15%)
  waiting for transfers between devices  10.3 us (11%)
  local copies, waits for them, and re-layouts  6.75 us (7%)
  other arithmetic  4.5 us (5%)
    ppermute x7, starting transfers between devices, partner(): lax.ppermute(value, axis, [(i, i ^ 1 << bit) for i in range(lax.axis_size...  14.6 us
    pallas_call x7, Pallas kernels, step(): call(functools.partial(step_kernel, trees, last, held, extra is not None)...  13.4 us
    pallas_call x1, Pallas kernels, body(): call(functools.partial(couple_kernel, leaf_pairs, lambda ref, b: ref[0, 0...  12.3 us
    ppermute x7, waiting for transfers between devices, partner(): lax.ppermute(value, axis, [(i, i ^ 1 << bit) for i in range(lax.axis_size...  10.3 us
    pallas_call x1, Pallas kernels, body(): call(functools.partial(tree_kernel, count), [shape(count * RANK, WIDE), s...  7.13 us
    pallas_call x1, Pallas kernels, body(): call(functools.partial(chol_table_kernel, count, ((0, count * RANK),)), s...  6.75 us
    pallas_call x1, Pallas kernels, body(): call(functools.partial(couple_kernel, root_pairs, lambda ref, b: (ref[0,...  6.75 us
    pallas_call x1, Pallas kernels, body(): call(functools.partial(chol_table_kernel, slots, ((row_roots.shape[0] - r...  6.38 us
  transfers between devices with their start and end apart: 7, of which 6 were waited for; matrix products, arithmetic and copies ran while one was open for 5% of the time, Pallas kernels for 34%

profile of v1, /device:TPU:0, one launch (start us, length us, event | category | flops | bytes accessed | tf_op | source)
XLA Modules:
  0.0 95.6 jit_solution(232953146479414160)
XLA Ops:
  0.6 7.1 %local_tree.1 = (f32[1024,128]{1,0:T(8,128)}, f32[128,128]{1,0:T(8,128)}, f32[128,128]{1,0:T(8,128)}, f32[64,128]{1,0:T(8,128)}) custom-call(s32[1,1,16]{2,1,0:T(1,128)} %row_order.1, s32[1,1,16]{2,1,0:T(1,128)} %col_order.1, f32[1,16,4096]{2,1,0:T(8,128)} %row_bases.1, f32[1,16,4096]{2,1,0:T(8,128)} %col_bases.1, f32[1,32,4096]{2,1,0:T(8,128)} %row_transfer.1, ...), custom_call_target="tpu_custom_call" | custom-call | tf_op jit(solution)/shard_map/local_tree/pallas_call | solution.py:315
  7.8 3.0 %collective-permute-start = (f32[128,128]{1,0:T(8,128)}, f32[128,128]{1,0:T(8,128)S(1)}, u32[]{:S(2)}, u32[]{:S(2)}) collective-permute-start(f32[128,128]{1,0:T(8,128)} %get-tuple-element.24.own), channel_id=1, source_target_pairs={{0,8},{8,0},{16,24},{24,16},{1,9},{9,1},{17,25},{25,17},{2,10},{10... | collective-permute-start | bytes 196616 | tf_op jit(solution)/shard_map/ppermute | solution.py:291
  10.8 0.0 copy-start.6
  10.8 0.8 copy-done.6
  11.7 0.6 pad_add_fusion.4.flags
  12.3 1.0 %collective-permute-done.recv = f32[128,128]{1,0:T(8,128)S(1)} collective-permute-done((f32[128,128]{1,0:T(8,128)}, f32[128,128]{1,0:T(8,128)S(1)}, u32[]{:S(2)}, u32[]{:S(2)}) %collective-permute-start) | collective-permute-done | bytes 65568 | tf_op jit(solution)/shard_map/ppermute | solution.py:291
  13.3 0.6 copy-done.5
  13.9 1.9 %step.7 = (f32[128,128]{1,0:T(8,128)}, f32[64,128]{1,0:T(8,128)}) custom-call(s32[2]{0:T(128)} %pad_add_fusion.4.flags, f32[128,128]{1,0:T(8,128)} %get-tuple-element.24.own, f32[128,128]{1,0:T(8,128)} %copy-done.5, f32[64,128]{1,0:T(8,128)} %get-tuple-element.25.high_in), custom_call_target="tpu_custom_call" | custom-call | tf_op jit(solution)/shard_map/step/pallas_call | solution.py:345
  15.8 3.0 %collective-permute-start.1 = (f32[128,128]{1,0:T(8,128)}, f32[128,128]{1,0:T(8,128)S(1)}, u32[]{:S(2)}, u32[]{:S(2)}) collective-permute-start(f32[128,128]{1,0:T(8,128)} %get-tuple-element.26.own), channel_id=1, source_target_pairs={{0,16},{8,24},{16,0},{24,8},{1,17},{9,25},{17,1},{25,9},{2,18},{10... | collective-permute-start | bytes 196616 | tf_op jit(solution)/shard_map/ppermute | solution.py:291
  18.9 0.7 pad_add_fusion.3.flags
  19.5 1.8 %collective-permute-done.1.recv = f32[128,128]{1,0:T(8,128)S(1)} collective-permute-done((f32[128,128]{1,0:T(8,128)}, f32[128,128]{1,0:T(8,128)S(1)}, u32[]{:S(2)}, u32[]{:S(2)}) %collective-permute-start.1) | collective-permute-done | bytes 65568 | tf_op jit(solution)/shard_map/ppermute | solution.py:291
  21.3 0.6 copy-done.7
  22.0 2.0 %step.8 = (f32[192,128]{1,0:T(8,128)}, f32[64,128]{1,0:T(8,128)}) custom-call(s32[2]{0:T(128)} %pad_add_fusion.3.flags, f32[128,128]{1,0:T(8,128)} %get-tuple-element.26.own, f32[128,128]{1,0:T(8,128)} %copy-done.7, f32[64,128]{1,0:T(8,128)} %get-tuple-element.27.high_in), custom_call_target="tpu_custom_call" | custom-call | tf_op jit(solution)/shard_map/step/pallas_call | solution.py:345
  23.9 0.8 slice.13
  24.7 0.0 copy-start
  24.7 0.1 collective-permute-start.2
  24.8 0.7 pad_add_fusion.2.flags
  25.5 0.6 collective-permute-done.2.recv
  26.1 0.0 copy-done
  26.1 0.6 copy-done.3
  26.7 2.1 %step.9 = (f32[192,128]{1,0:T(8,128)}, f32[64,128]{1,0:T(8,128)}) custom-call(s32[4]{0:T(128)} %pad_add_fusion.2.flags, f32[192,128]{1,0:T(8,128)} %copy-done, f32[192,128]{1,0:T(8,128)} %copy-done.3, f32[64,128]{1,0:T(8,128)} %get-tuple-element.29.high_in), custom_call_target="tpu_custom_call" | custom-call | tf_op jit(solution)/shard_map/step/pallas_call | solution.py:345
  28.8 1.8 %collective-permute-start.3 = (f32[192,128]{1,0:T(8,128)}, f32[192,128]{1,0:T(8,128)S(1)}, u32[]{:S(2)}, u32[]{:S(2)}) collective-permute-start(f32[192,128]{1,0:T(8,128)} %get-tuple-element.30.own), channel_id=1, source_target_pairs={{0,2},{1,3},{2,0},{3,1},{4,6},{5,7},{6,4},{7,5},{8,10},{9,11},{10,... | collective-permute-start | bytes 294920 | tf_op jit(solution)/shard_map/ppermute | solution.py:291
  30.6 0.6 pad_add_fusion.1.flags
  31.2 2.7 %collective-permute-done.3.recv = f32[192,128]{1,0:T(8,128)S(1)} collective-permute-done((f32[192,128]{1,0:T(8,128)}, f32[192,128]{1,0:T(8,128)S(1)}, u32[]{:S(2)}, u32[]{:S(2)}) %collective-permute-start.3) | collective-permute-done | bytes 98336 | tf_op jit(solution)/shard_map/ppermute | solution.py:291
  33.9 0.6 copy-done.4
  34.6 2.1 %step.10 = (f32[256,128]{1,0:T(8,128)}, f32[64,128]{1,0:T(8,128)}) custom-call(s32[4]{0:T(128)} %pad_add_fusion.1.flags, f32[192,128]{1,0:T(8,128)} %get-tuple-element.30.own, f32[192,128]{1,0:T(8,128)} %copy-done.4, f32[64,128]{1,0:T(8,128)} %get-tuple-element.31.high_in), custom_call_target="tpu_custom_call" | custom-call | tf_op jit(solution)/shard_map/step/pallas_call | solution.py:345
  36.7 1.8 %collective-permute-start.4 = (f32[256,128]{1,0:T(8,128)}, f32[256,128]{1,0:T(8,128)S(1)}, u32[]{:S(2)}, u32[]{:S(2)}) collective-permute-start(f32[256,128]{1,0:T(8,128)} %get-tuple-element.32.own), channel_id=1, source_target_pairs={{0,4},{1,5},{2,6},{3,7},{4,0},{5,1},{6,2},{7,3},{8,12},{9,13},{10,... | collective-permute-start | bytes 393224 | tf_op jit(solution)/shard_map/ppermute | solution.py:291
  38.4 0.6 pad_add_fusion.flags
  39.0 2.8 %collective-permute-done.4.recv = f32[256,128]{1,0:T(8,128)S(1)} collective-permute-done((f32[256,128]{1,0:T(8,128)}, f32[256,128]{1,0:T(8,128)S(1)}, u32[]{:S(2)}, u32[]{:S(2)}) %collective-permute-start.4) | collective-permute-done | bytes 131104 | tf_op jit(solution)/shard_map/ppermute | solution.py:291
  41.8 0.6 copy-done.2
  42.5 2.1 %step.11 = (f32[320,128]{1,0:T(8,128)}, f32[64,128]{1,0:T(8,128)}) custom-call(s32[4]{0:T(128)} %pad_add_fusion.flags, f32[256,128]{1,0:T(8,128)} %get-tuple-element.32.own, f32[256,128]{1,0:T(8,128)} %copy-done.2, f32[64,128]{1,0:T(8,128)} %get-tuple-element.33.high_in), custom_call_target="tpu_custom_call" | custom-call | tf_op jit(solution)/shard_map/step/pallas_call | solution.py:345
  44.6 0.8 slice.15.own
  45.3 1.8 %collective-permute-start.5 = (f32[64,128]{1,0:T(8,128)S(1)}, f32[64,128]{1,0:T(8,128)S(1)}, u32[]{:S(2)}, u32[]{:S(2)}) collective-permute-start(f32[64,128]{1,0:T(8,128)S(1)} %slice.15.own), channel_id=1, source_target_pairs={{0,8},{8,0},{16,24},{24,16},{1,9},{9,1},{17,25},{25,17},{2,10},{10... | collective-permute-start | bytes 98312 | tf_op jit(solution)/shard_map/ppermute | solution.py:291
  47.2 0.6 pad_add_fusion.6.flags
  47.8 1.4 %collective-permute-done.5.recv = f32[64,128]{1,0:T(8,128)S(1)} collective-permute-done((f32[64,128]{1,0:T(8,128)S(1)}, f32[64,128]{1,0:T(8,128)S(1)}, u32[]{:S(2)}, u32[]{:S(2)}) %collective-permute-start.5) | collective-permute-done | bytes 32800 | tf_op jit(solution)/shard_map/ppermute | solution.py:291
  49.3 0.0 copy-done.1
  49.3 0.6 copy-done.8
  49.9 1.9 %step.12 = (f32[64,128]{1,0:T(8,128)}, f32[64,128]{1,0:T(8,128)}) custom-call(s32[2]{0:T(128)} %pad_add_fusion.6.flags, f32[64,128]{1,0:T(8,128)} %copy-done.1, f32[64,128]{1,0:T(8,128)} %copy-done.8, f32[64,128]{1,0:T(8,128)} %get-tuple-element.35.high_in), custom_call_target="tpu_custom_call" | custom-call | tf_op jit(solution)/shard_map/step/pallas_call | solution.py:345
  51.7 3.0 %collective-permute-start.6 = (f32[64,128]{1,0:T(8,128)}, f32[64,128]{1,0:T(8,128)S(1)}, u32[]{:S(2)}, u32[]{:S(2)}) collective-permute-start(f32[64,128]{1,0:T(8,128)} %get-tuple-element.36.own), channel_id=1, source_target_pairs={{0,16},{8,24},{16,0},{24,8},{1,17},{9,25},{17,1},{25,9},{2,18},{10... | collective-permute-start | bytes 98312 | tf_op jit(solution)/shard_map/ppermute | solution.py:291
  54.7 0.7 pad_add_fusion.5.flags
  55.4 6.7 %leaf_factors.1.table = f32[2048,64]{1,0:T(8,128)} custom-call(f32[1024,128]{1,0:T(8,128)} %get-tuple-element.22.refs_0_), custom_call_target="tpu_custom_call" | custom-call | tf_op jit(solution)/shard_map/leaf_factors/pallas_call | solution.py:366
  62.1 12.3 %leaf_couple.1 = f32[1,64,4096]{2,1,0:T(8,128)} custom-call(s32[1,2,64]{2,1,0:T(2,128)} %right_pick.2, s32[1,2,64]{2,1,0:T(2,128)} %right_pick.2, f32[2048,64]{1,0:T(8,128)} %leaf_factors.1.table, bf16[1,64,4096]{2,1,0:T(8,128)(2,1)} %blocks.2), custom_call_target="tpu_custom_call" | custom-call | tf_op jit(solution)/shard_map/leaf_couple/pallas_call | solution.py:373
  74.5 6.4 %root_factors.1.table = f32[1024,64]{1,0:T(8,128)} custom-call(f32[320,128]{1,0:T(8,128)} %get-tuple-element.34.refs_0_, f32[192,128]{1,0:T(8,128)} %get-tuple-element.28.refs_1_), custom_call_target="tpu_custom_call" | custom-call | tf_op jit(solution)/shard_map/root_factors/pallas_call | solution.py:388
  80.9 6.7 %root_couple.1 = f32[1,32,4096]{2,1,0:T(8,128)} custom-call(s32[1,1,32]{2,1,0:T(1,128)} %left_pick.3, s32[1,1,32]{2,1,0:T(1,128)} %right_pick.3, f32[1024,64]{1,0:T(8,128)} %root_factors.1.table, bf16[1,32,4096]{2,1,0:T(8,128)(2,1)} %blocks.3), custom_call_target="tpu_custom_call" | custom-call | tf_op jit(solution)/shard_map/root_couple/pallas_call | solution.py:399
  87.6 0.0 collective-permute-done.6.recv
  87.6 0.6 copy-done.9
  88.2 1.4 %step.13.high = f32[64,128]{1,0:T(8,128)} custom-call(s32[2]{0:T(128)} %pad_add_fusion.5.flags, f32[64,128]{1,0:T(8,128)} %get-tuple-element.36.own, f32[64,128]{1,0:T(8,128)} %copy-done.9, f32[64,128]{1,0:T(8,128)} %get-tuple-element.37.high_in), custom_call_target="tpu_custom_call" | custom-call | tf_op jit(solution)/shard_map/step/pallas_call | solution.py:345
  89.6 5.9 %upper_factors.1 = (f32[1,1,4096]{2,1,0:T(1,128)}, f32[1,1,4096]{2,1,0:T(1,128)}) custom-call(f32[64,128]{1,0:T(8,128)} %step.13.high), custom_call_target="tpu_custom_call" | custom-call | tf_op jit(solution)/shard_map/upper_factors/pallas_call | solution.py:412
  (10 shorter events, 0.0 us)
Async XLA Ops:
  7.8 5.5 %collective-permute-start = (f32[128,128]{1,0:T(8,128)}, f32[128,128]{1,0:T(8,128)S(1)}, u32[]{:S(2)}, u32[]{:S(2)}) collective-permute-start(f32[128,128]{1,0:T(8,128)} %get-tuple-element.24.own), channel_id=1, source_target_pairs={{0,8},{8,0},{16,24},{24,16},{1,9},{9,1},{17,25},{25,17},{2,10},{10... | collective-permute-start | bytes 196616 | tf_op jit(solution)/shard_map/ppermute | solution.py:291
  10.8 0.8 copy-start.6
  13.3 0.6 copy-start.5
  15.8 5.5 %collective-permute-start.1 = (f32[128,128]{1,0:T(8,128)}, f32[128,128]{1,0:T(8,128)S(1)}, u32[]{:S(2)}, u32[]{:S(2)}) collective-permute-start(f32[128,128]{1,0:T(8,128)} %get-tuple-element.26.own), channel_id=1, source_target_pairs={{0,16},{8,24},{16,0},{24,8},{1,17},{9,25},{17,1},{25,9},{2,18},{10... | collective-permute-start | bytes 196616 | tf_op jit(solution)/shard_map/ppermute | solution.py:291
  21.3 0.6 copy-start.7
  24.7 1.4 %copy-start = (f32[192,128]{1,0:T(8,128)}, f32[192,128]{1,0:T(8,128)S(1)}, u32[]{:S(2)}) copy-start(f32[192,128]{1,0:T(8,128)S(1)} %pad_maximum_fusion.own) | copy-start | bytes 294916
  24.7 1.4 %collective-permute-start.2 = (f32[192,128]{1,0:T(8,128)S(1)}, f32[192,128]{1,0:T(8,128)S(1)}, u32[]{:S(2)}, u32[]{:S(2)}) collective-permute-start(f32[192,128]{1,0:T(8,128)S(1)} %pad_maximum_fusion.own), channel_id=1, source_target_pairs={{0,1},{1,0},{2,3},{3,2},{4,5},{5,4},{6,7},{7,6},{8,9},{9,8},{10,11... | collective-permute-start | bytes 294920 | tf_op jit(solution)/shard_map/ppermute | solution.py:291
  26.1 0.6 copy-start.3
  28.8 5.1 %collective-permute-start.3 = (f32[192,128]{1,0:T(8,128)}, f32[192,128]{1,0:T(8,128)S(1)}, u32[]{:S(2)}, u32[]{:S(2)}) collective-permute-start(f32[192,128]{1,0:T(8,128)} %get-tuple-element.30.own), channel_id=1, source_target_pairs={{0,2},{1,3},{2,0},{3,1},{4,6},{5,7},{6,4},{7,5},{8,10},{9,11},{10,... | collective-permute-start | bytes 294920 | tf_op jit(solution)/shard_map/ppermute | solution.py:291
  33.9 0.6 copy-start.4
  36.7 5.2 %collective-permute-start.4 = (f32[256,128]{1,0:T(8,128)}, f32[256,128]{1,0:T(8,128)S(1)}, u32[]{:S(2)}, u32[]{:S(2)}) collective-permute-start(f32[256,128]{1,0:T(8,128)} %get-tuple-element.32.own), channel_id=1, source_target_pairs={{0,4},{1,5},{2,6},{3,7},{4,0},{5,1},{6,2},{7,3},{8,12},{9,13},{10,... | collective-permute-start | bytes 393224 | tf_op jit(solution)/shard_map/ppermute | solution.py:291
  41.8 0.6 copy-start.2
  45.3 3.9 %copy-start.1 = (f32[64,128]{1,0:T(8,128)}, f32[64,128]{1,0:T(8,128)S(1)}, u32[]{:S(2)}) copy-start(f32[64,128]{1,0:T(8,128)S(1)} %slice.15.own) | copy-start | bytes 98308
  45.3 3.9 %collective-permute-start.5 = (f32[64,128]{1,0:T(8,128)S(1)}, f32[64,128]{1,0:T(8,128)S(1)}, u32[]{:S(2)}, u32[]{:S(2)}) collective-permute-start(f32[64,128]{1,0:T(8,128)S(1)} %slice.15.own), channel_id=1, source_target_pairs={{0,8},{8,0},{16,24},{24,16},{1,9},{9,1},{17,25},{25,17},{2,10},{10... | collective-permute-start | bytes 98312 | tf_op jit(solution)/shard_map/ppermute | solution.py:291
  49.3 0.6 copy-start.8
  51.7 35.9 %collective-permute-start.6 = (f32[64,128]{1,0:T(8,128)}, f32[64,128]{1,0:T(8,128)S(1)}, u32[]{:S(2)}, u32[]{:S(2)}) collective-permute-start(f32[64,128]{1,0:T(8,128)} %get-tuple-element.36.own), channel_id=1, source_target_pairs={{0,16},{8,24},{16,0},{24,8},{1,17},{9,25},{17,1},{25,9},{2,18},{10... | collective-permute-start | bytes 98312 | tf_op jit(solution)/shard_map/ppermute | solution.py:291
  87.6 0.6 copy-start.9

commit v2 on v1

v2 whole, which is shorter than its diff:
```python
import functools

import jax
import jax.numpy as jnp
from jax import lax
from jax.experimental import pallas as pl
from jax.experimental.pallas import tpu as pltpu
from jax.sharding import PartitionSpec as P


RANK = 64
WIDE = 2 * RANK
SUB = 8
NB = RANK // SUB
F32 = jnp.float32
BF16 = jnp.bfloat16
VMEM = pl.BlockSpec(memory_space=pltpu.VMEM)
SMEM = pl.BlockSpec(memory_space=pltpu.SMEM)


def split(x):
    high = x.astype(BF16)
    return high, (x - high.astype(F32)).astype(BF16)


def dot(a, b, rhs_dim=0):
    return lax.dot_general(a, b, (((1,), (rhs_dim,)), ((), ())), preferred_element_type=F32)


def dot3(a, b):
    a_high, a_low = split(a)
    b_high, b_low = split(b)
    return dot(a_high, b_high) + (dot(a_high, b_low) + dot(a_low, b_high))


def stacked(x, axis=0):
    return jnp.concatenate(split(x), axis=axis)


def lane_half(rows):
    return lax.broadcasted_iota(jnp.int32, (rows, WIDE), 1) < RANK


def swapped(x):
    return pltpu.roll(x, RANK, 1)


def beside(left, right):
    return jnp.where(lane_half(left.shape[0]), left, right)


def dot_both(a, b):
    y = dot(stacked(a), stacked(b))
    return beside(y[:RANK], y[RANK:WIDE]) + beside(y[WIDE : WIDE + RANK], y[WIDE + RANK :])


def sandwich_both(gram, transfer):
    x = dot(stacked(jnp.concatenate([transfer, transfer], axis=0).T), stacked(gram))
    x = x[:WIDE] + x[WIDE:]
    top, low = x[:RANK], x[RANK:]
    return dot_both(
        jnp.concatenate([beside(top, swapped(top)), beside(swapped(low), low)], axis=0), transfer
    )


def unpack_both(left_ref, right_ref, out_ref, count):
    for k in range(RANK // 2):
        a = left_ref[0, :, k * WIDE : (k + 1) * WIDE]
        b = right_ref[0, :, k * WIDE : (k + 1) * WIDE]
        out_ref[pl.ds(2 * k, count, stride=RANK), :] = beside(a, swapped(b))
        out_ref[pl.ds(2 * k + 1, count, stride=RANK), :] = beside(swapped(a), b)


def tree_kernel(
    count,
    row_order,
    col_order,
    row_bases,
    col_bases,
    row_transfer,
    col_transfer,
    leaf_gram,
    row_pay,
    col_pay,
    high,
    basis,
    trans,
):
    unpack_both(row_bases, col_bases, basis, count)
    unpack_both(row_transfer, col_transfer, trans, 2 * count)
    for leaf in range(count):
        u = basis[leaf * RANK : (leaf + 1) * RANK, :]
        leaf_gram[leaf * RANK : (leaf + 1) * RANK, :] = dot_both(
            jnp.concatenate([u, u], axis=0).T, u
        )
    nodes = []
    for q in range(count // 2):
        total = None
        for p in (2 * q, 2 * q + 1):
            r = pl.ds(pl.multiple_of(row_order[0, 0, p] * RANK, RANK), RANK)
            c = pl.ds(pl.multiple_of(col_order[0, 0, p] * RANK, RANK), RANK)
            term = sandwich_both(
                beside(leaf_gram[r, :], leaf_gram[c, :]), beside(trans[r, :], trans[c, :])
            )
            total = term if total is None else total + term
        nodes.append(total)
    offset = count
    while len(nodes) > 1:
        terms = []
        for q, gram in enumerate(nodes):
            terms.append(
                sandwich_both(gram, trans[(offset + q) * RANK : (offset + q + 1) * RANK, :])
            )
        offset += len(nodes)
        nodes = [terms[2 * q] + terms[2 * q + 1] for q in range(len(terms) // 2)]
    gram = nodes[0]
    term = sandwich_both(gram, trans[offset * RANK : (offset + 1) * RANK, :])
    first = trans[(offset + 1) * RANK : (offset + 2) * RANK, :]
    high[...] = gram
    row_pay[0:RANK, :] = beside(term, swapped(first))
    row_pay[RANK:WIDE, :] = gram
    col_pay[0:RANK, :] = beside(swapped(term), first)
    col_pay[RANK:WIDE, :] = swapped(gram)


def step_kernel(levels, top, sizes, held, apart, extra, own, recv, high_in, *refs):
    refs = list(refs)
    before = refs.pop(0) if extra else None
    high_out = refs.pop(0)
    roots_out = refs.pop() if apart else None
    pay_out = refs.pop(0) if refs else None
    nr, nc = sizes
    i, j = lax.axis_index("row"), lax.axis_index("col")
    base = 0
    if extra:
        pay_out[0:RANK, :] = before[0:RANK, :]
        base = RANK
    high = high_in[...]
    uppers = []
    for slot, (name, level) in enumerate(levels):
        d = i * nc + j if name == "r" else j * nr + i
        span = 1 << level
        upper = lax.rem(lax.div(d, span), 2) == 1
        uppers.append(upper)
        take = lax.rem(d, 2 * span) == span
        if level == top:
            take = jnp.logical_or(take, d == 0)
        mine = own[slot * RANK : (slot + 1) * RANK, :]
        theirs = recv[slot * RANK : (slot + 1) * RANK, :]
        total = mine + theirs
        if level < top:
            transfer = jnp.where(upper, mine, theirs)
            first = jnp.where(upper, theirs, mine)
            x = dot3(transfer.T[RANK:], total[:, :RANK])
            pay_out[base : base + RANK, :] = beside(swapped(dot3(x, transfer)), first)
            base += RANK
        picked = beside(total, high) if name == "r" else beside(high, swapped(total))
        high = jnp.where(take, picked, high)
    high_out[...] = high
    if extra:
        pay_out[base : base + RANK, :] = before[RANK:WIDE, :]
    if held:
        upper = uppers[0]
        start = len(levels) * RANK
        if roots_out is None:
            roots_out = pay_out.at[base:, :]
        if held == 1:
            mine = own[start : start + RANK, :]
            theirs = recv[start : start + RANK, :]
            roots_out[0:RANK, :] = jnp.where(
                upper, beside(theirs, swapped(mine)), beside(mine, swapped(theirs))
            )
        else:
            rows = held // 2 * RANK
            mine = own[start : start + rows, :]
            theirs = recv[start : start + rows, :]
            roots_out[0:rows, :] = jnp.where(upper, theirs, mine)
            roots_out[rows : 2 * rows, :] = jnp.where(upper, mine, theirs)


def chol_lanes(a_ref, r_ref):
    sub = lax.broadcasted_iota(jnp.int32, (SUB, WIDE), 0)

    def at(q):
        return slice(SUB * q, SUB * (q + 1))

    def spread(i, j):
        return r_ref[i, pl.ds(j, SUB, stride=0), :]

    def less(value, f, row):
        return lax.sub(value, lax.mul(f, row))

    for p in range(NB):
        i0 = SUB * p
        acc = [a_ref[i0 + r, at(p), :] for r in range(SUB)]
        scale = []
        for r in range(SUB):
            inv = lax.rsqrt(jnp.broadcast_to(acc[r][r : r + 1, :], (SUB, WIDE)))
            scale.append(inv)
            row = jnp.where(sub >= r, acc[r] * inv, 0.0)
            r_ref[i0 + r, at(p), :] = row
            for r2 in range(r + 1, SUB):
                acc[r2] = less(acc[r2], jnp.broadcast_to(row[r2 : r2 + 1, :], (SUB, WIDE)), row)
        for q in range(p + 1, NB):
            x = [a_ref[i0 + r, at(q), :] for r in range(SUB)]
            for r in range(SUB):
                x[r] = lax.mul(x[r], scale[r])
                r_ref[i0 + r, at(q), :] = x[r]
                for r2 in range(r + 1, SUB):
                    x[r2] = less(x[r2], spread(i0 + r, i0 + r2), x[r])
        for pi in range(p + 1, NB):
            for q0 in range(pi, NB, 2):
                qs = range(q0, min(q0 + 2, NB))
                acc2 = {(r, q): a_ref[SUB * pi + r, at(q), :] for r in range(SUB) for q in qs}
                for k in range(SUB):
                    rows = {q: r_ref[i0 + k, at(q), :] for q in qs}
                    for r in range(SUB):
                        f = spread(i0 + k, SUB * pi + r)
                        for q in qs:
                            acc2[r, q] = less(acc2[r, q], f, rows[q])
                for (r, q), value in acc2.items():
                    a_ref[SUB * pi + r, at(q), :] = value


def load_lanes(slots_ref, a_ref, count):
    for i in range(RANK):
        b0 = SUB * (i // SUB)
        t = slots_ref[pl.ds(i, count, stride=RANK), :].T
        a_ref[i, b0:RANK, 0 : 2 * count] = jnp.concatenate([t[b0:RANK], t[RANK + b0 :]], axis=1)


def factor_row(r_ref, i, lanes):
    b0 = SUB * (i // SUB)
    t = r_ref[i, b0:RANK, 0:lanes]
    if b0:
        t = jnp.concatenate([jnp.zeros((b0, lanes), F32), t], axis=0)
    return t.T


def chol_table_kernel(count, sources, *refs):
    inputs = refs[: len(sources)]
    table, a_ref, r_ref, factor = refs[len(sources) : len(sources) + 4]
    if len(sources) > 1:
        slots = refs[len(sources) + 4]
        base = 0
        for ref in inputs:
            slots[base : base + ref.shape[0], :] = ref[...]
            base += ref.shape[0]
    else:
        slots = inputs[0]
    load_lanes(slots, a_ref, count)
    chol_lanes(a_ref, r_ref)
    for i in range(RANK):
        factor[pl.ds(i, 2 * count, stride=RANK), :] = factor_row(r_ref, i, 2 * count)
    for b in range(2 * count):
        table[b * WIDE : (b + 1) * WIDE, :] = stacked(factor[b * RANK : (b + 1) * RANK, :])


def final_kernel(high, row_out, col_out, slots, a_ref, r_ref):
    slots[0:RANK, :] = high[...]
    load_lanes(slots, a_ref, SUB)
    chol_lanes(a_ref, r_ref)
    for k in range(RANK // 2):
        even = factor_row(r_ref, 2 * k, 2 * SUB)
        odd = factor_row(r_ref, 2 * k + 1, 2 * SUB)
        both = jnp.concatenate([even, odd], axis=1)
        row_out[0, 0:1, k * WIDE : (k + 1) * WIDE] = both[0:1]
        col_out[0, 0:1, k * WIDE : (k + 1) * WIDE] = both[SUB : SUB + 1]


def couple_kernel(start, pairs, left_of, right_of, left_pick, right_pick, table, blocks, y_ref, s_ref):
    for k in range(RANK // 2):
        slab = blocks[0, start : start + pairs, k * WIDE : (k + 1) * WIDE].astype(F32)
        s_ref[pl.ds(2 * k, pairs, stride=RANK), :] = slab[:, :RANK]
        s_ref[pl.ds(2 * k + 1, pairs, stride=RANK), :] = swapped(slab)[:, :RANK]

    def one(b, carry):
        t = pl.multiple_of(left_of(left_pick, start + b) * WIDE, WIDE)
        s = pl.multiple_of(right_of(right_pick, start + b) * WIDE, WIDE)
        at = pl.ds(pl.multiple_of(b * RANK, RANK), RANK)
        x = dot(table[pl.ds(t, WIDE), :], s_ref[at, :].astype(BF16))
        y = dot(stacked(x[:RANK] + x[RANK:]), table[pl.ds(s, WIDE), :], 1)
        y = y[:RANK] + y[RANK:]
        y_ref[at, :] = y + swapped(y)
        return carry

    lax.fori_loop(0, pairs, one, 0, unroll=8)


def pack_kernel(sizes, *refs):
    inputs, out = refs[: len(sizes)], refs[len(sizes)]
    for k in range(RANK // 2):
        base = 0
        for pairs, y_ref in zip(sizes, inputs):
            out[0, base : base + pairs, k * WIDE : (k + 1) * WIDE] = beside(
                y_ref[pl.ds(2 * k, pairs, stride=RANK), :],
                y_ref[pl.ds(2 * k + 1, pairs, stride=RANK), :],
            )
            base += pairs


def shape(*dims):
    return jax.ShapeDtypeStruct(dims, F32)


def scratch(rows, lanes=WIDE):
    return pltpu.VMEM((rows, lanes), F32)


def call(kernel, outs, specs, scratches=(), limit=8):
    return pl.pallas_call(
        kernel,
        out_shape=outs,
        in_specs=specs,
        out_specs=jax.tree.map(lambda _: VMEM, outs),
        scratch_shapes=list(scratches),
        compiler_params=pltpu.CompilerParams(vmem_limit_bytes=limit << 20),
    )


def partner(value, axis, bit):
    return lax.ppermute(value, axis, [(i, i ^ 1 << bit) for i in range(lax.axis_size(axis))])


def body(
    row_bases,
    col_bases,
    row_transfer,
    col_transfer,
    row_order,
    col_order,
    leaf_pattern,
    leaf_blocks,
    root_rows,
    root_cols,
    root_blocks,
):
    count = row_bases.shape[1]
    leaf_pairs = leaf_blocks.shape[1]
    root_pairs = root_blocks.shape[1]
    nr, nc = lax.axis_size("row"), lax.axis_size("col")
    lr, lc = nr.bit_length() - 1, nc.bit_length() - 1
    top = lr + lc - 1

    leaf_gram, row_pay, col_pay, high = call(
        functools.partial(tree_kernel, count),
        [shape(count * RANK, WIDE), shape(WIDE, WIDE), shape(WIDE, WIDE), shape(RANK, WIDE)],
        [SMEM, SMEM, VMEM, VMEM, VMEM, VMEM],
        [scratch(count * RANK), scratch(2 * count * RANK)],
    )(row_order, col_order, row_bases, col_bases, row_transfer, col_transfer)

    def step(levels, pay, axis, bit, high, held=0, apart=False, extra=None):
        recv = partner(pay, axis, bit)
        rows = sum(level < top for _, level in levels) * RANK
        rows += 0 if apart else held * RANK
        rows += 0 if extra is None else WIDE
        outs = [shape(RANK, WIDE)]
        if rows:
            outs.append(shape(rows, WIDE))
        if apart:
            outs.append(shape(held * RANK, WIDE))
        args = [pay, recv, high] + ([] if extra is None else [extra])
        result = call(
            functools.partial(step_kernel, levels, top, (nr, nc), held, apart, extra is not None),
            outs,
            [VMEM] * len(args),
            limit=2 + held // 4,
        )(*args)
        return result

    pay = col_pay
    for h in range(lr):
        done = h == lr - 1
        high, pay, *rest = step(
            [("c", h)],
            pay,
            "row",
            h,
            high,
            held=1 << h,
            apart=done,
            extra=row_pay if done else None,
        )
    col_roots = rest[0]
    for h in range(lc):
        done = h == lc - 1
        high, pay, *rest = step(
            [("r", h), ("c", lr + h)], pay, "col", h, high, held=1 << h, apart=done
        )
    row_roots = rest[0]
    for h in range(lr):
        high, *rest = step([("r", lc + h)], pay, "row", h, high)
        pay = rest[0] if rest else None

    big = [pltpu.VMEM((RANK, RANK, WIDE), F32)] * 2

    def table(count, *sources):
        return call(
            functools.partial(chol_table_kernel, count, [x.shape for x in sources]),
            jax.ShapeDtypeStruct((2 * count * WIDE, RANK), BF16),
            [VMEM] * len(sources),
            big
            + [scratch(2 * count * RANK, RANK)]
            + ([scratch(count * RANK)] if len(sources) > 1 else []),
            limit=5 + count // 3,
        )(*sources)

    def couple(parts, total, left_of, right_of, left_pick, right_pick, table, blocks):
        pieces, start = [], 0
        for pairs in parts:
            pieces.append(
                call(
                    functools.partial(couple_kernel, start, pairs, left_of, right_of),
                    shape(pairs * RANK, WIDE),
                    [SMEM, SMEM, VMEM, VMEM],
                    [scratch(pairs * RANK, RANK)],
                )(left_pick, right_pick, table, blocks)
            )
            start += pairs
        return call(
            functools.partial(pack_kernel, parts), shape(1, total, RANK * RANK), [VMEM] * len(parts)
        )(*pieces)

    quarter = leaf_pairs // 4
    leaf_coupled = couple(
        (quarter, quarter, 2 * quarter),
        leaf_pairs,
        lambda ref, b: ref[0, 0, b],
        lambda ref, b: ref[0, 1, b] + count,
        leaf_pattern,
        leaf_pattern,
        table(count, leaf_gram),
        leaf_blocks,
    )
    row_slots, col_slots = nc // 2, nr // 2
    slots = -(-(row_slots + col_slots) // SUB) * SUB
    root_coupled = couple(
        (root_pairs,),
        root_pairs,
        lambda ref, b: (ref[0, 0, b] & 1) * slots + (ref[0, 0, b] >> 1),
        lambda ref, b: (ref[0, 0, b] & 1) * slots + (ref[0, 0, b] >> 1) + row_slots,
        root_rows,
        root_cols,
        table(slots, row_roots, col_roots),
        root_blocks,
    )
    row_upper_r, col_upper_r = call(
        final_kernel,
        [shape(1, 1, RANK * RANK), shape(1, 1, RANK * RANK)],
        [VMEM],
        [scratch(SUB * RANK)] + big,
    )(high)
    return (leaf_coupled, root_coupled, row_upper_r, col_upper_r)


def solution(mesh):
    return jax.shard_map(
        body,
        mesh=mesh,
        in_specs=(
            P("row", "col", None),
            P("col", "row", None),
            P("row", "col", None),
            P("col", "row", None),
            P("row", "col", None),
            P("col", "row", None),
            P("row", "col", None),
            P("row", "col", None),
            P("row", "col", None),
            P("row", "col", None),
            P("row", "col", None),
        ),
        out_specs=(
            P("row", "col", None),
            P("row", "col", None),
            P("row", "col", None),
            P("col", "row", None),
        ),
        check_vma=False,
    )
```

time: 96.4 us -> 77.6 us (0.80)
  Pallas kernels: 58.7 us -> 42 us
  other arithmetic: 4.5 us -> 0 us
  waiting for transfers between devices: 10.3 us -> 14.2 us
  local copies, waits for them, and re-layouts: 6.75 us -> 5.3 us
    pallas_call x11 -> x15, Pallas kernels: 45.7 us -> 31.4 us  [the longest x4 15.2 us: couple(): call(functools.partial(couple_kernel, start, pairs, left_of, right_of), s...]
    another operation x7 -> x0, other arithmetic: 4.49 us -> none  [flags(): return jnp.stack(values)]
    ppermute x7, waiting for transfers between devices: 10.3 us -> 14.2 us  [partner(): lax.ppermute(value, axis, [(i, i ^ 1 << bit) for i in range(lax.axis_size...]
    pallas_call x1, Pallas kernels: 7.13 us -> 5.23 us  [body(): call(functools.partial(tree_kernel, count), [shape(count * RANK, WIDE), s...]
    slice x3 -> x0, local copies, waits for them, and re-layouts: 1.53 us -> none  [the longest x2 0.77 us: body(): pay = jnp.concatenate([row_pay[:RANK], pay[:RANK], row_pay[RANK:]], axis=0)]
    unnamed x20 -> x22, local copies, waits for them, and re-layouts: 5.22 us -> 5.3 us
  transfers between devices with their start and end apart: 7 -> 7, of which waited for: 6 -> 6; matrix products, arithmetic and copies ran while one was open for 5% -> 0% of each run, Pallas kernels for 34% -> 37%
where the time goes in v2:
time: 77.6 us; the launch traced here: 77.3 us
  Pallas kernels  42 us (54%)
  starting transfers between devices  14.9 us (19%)
  waiting for transfers between devices  14.2 us (18%)
  local copies, waits for them, and re-layouts  5.3 us (7%)
  between operations  0.81 us (1%)
    pallas_call x4, Pallas kernels, couple(): call(functools.partial(couple_kernel, start, pairs, left_of, right_of), s...  15.2 us
    ppermute x7, starting transfers between devices, partner(): lax.ppermute(value, axis, [(i, i ^ 1 << bit) for i in range(lax.axis_size...  14.9 us
    ppermute x7, waiting for transfers between devices, partner(): lax.ppermute(value, axis, [(i, i ^ 1 << bit) for i in range(lax.axis_size...  14.2 us
    pallas_call x2, Pallas kernels, table(): call(functools.partial(chol_table_kernel, count, [x.shape for x in source...  9.91 us
    pallas_call x1, Pallas kernels, body(): call(final_kernel, [shape(1, 1, RANK * RANK), shape(1, 1, RANK * RANK)],...  5.35 us
    unnamed x22, local copies, waits for them, and re-layouts  5.3 us
    pallas_call x1, Pallas kernels, body(): call(functools.partial(tree_kernel, count), [shape(count * RANK, WIDE), s...  5.23 us
    pallas_call x2, Pallas kernels, couple(): call(functools.partial(pack_kernel, parts), shape(1, total, RANK * RANK),...  3.5 us
  transfers between devices with their start and end apart: 7, of which 6 were waited for; matrix products, arithmetic and copies ran while one was open for 0% of the time, Pallas kernels for 37%

profile of v2, /device:TPU:0, one launch (start us, length us, event | category | flops | bytes accessed | tf_op | source)
XLA Modules:
  0.0 77.3 jit_solution(12088500595938038000)
XLA Ops:
  0.6 0.0 copy-start.1
  0.6 1.0 %copy-done.1 = f32[1,32,4096]{2,1,0:T(8,128)S(1)} copy-done((f32[1,32,4096]{2,1,0:T(8,128)S(1)}, f32[1,32,4096]{2,1,0:T(8,128)}, u32[]{:S(2)}) %copy-start.1) | copy-done | bytes 524312
  1.7 0.0 copy-start.2
  1.7 1.0 %copy-done.2 = f32[1,32,4096]{2,1,0:T(8,128)S(1)} copy-done((f32[1,32,4096]{2,1,0:T(8,128)S(1)}, f32[1,32,4096]{2,1,0:T(8,128)}, u32[]{:S(2)}) %copy-start.2) | copy-done | bytes 524312
  2.7 0.0 copy-start.4
  2.7 0.9 %copy-done.4 = f32[1,16,4096]{2,1,0:T(8,128)S(1)} copy-done((f32[1,16,4096]{2,1,0:T(8,128)S(1)}, f32[1,16,4096]{2,1,0:T(8,128)}, u32[]{:S(2)}) %copy-start.4) | copy-done | bytes 262168
  3.7 0.0 copy-start.5
  3.7 0.9 %copy-done.5 = f32[1,16,4096]{2,1,0:T(8,128)S(1)} copy-done((f32[1,16,4096]{2,1,0:T(8,128)S(1)}, f32[1,16,4096]{2,1,0:T(8,128)}, u32[]{:S(2)}) %copy-start.5) | copy-done | bytes 262168
  4.6 0.0 copy-start.7
  4.6 0.7 copy-done.7
  5.3 0.0 copy-start.8
  5.3 0.7 copy-done.8
  5.9 5.2 %shard_map.138 = (f32[1024,128]{1,0:T(8,128)S(1)}, f32[128,128]{1,0:T(8,128)S(1)}, f32[128,128]{1,0:T(8,128)S(1)}, f32[64,128]{1,0:T(8,128)S(1)}) custom-call(s32[1,1,16]{2,1,0:T(1,128)S(1)} %copy-done.7, s32[1,1,16]{2,1,0:T(1,128)S(1)} %copy-done.8, f32[1,16,4096]{2,1,0:T(8,128)S(1)} %copy-done.4, f32[1,16,4096]{2,1,0:T(8,128)S(1)} %copy-done.5, ...), custom_call_target="tpu_custom_call" | custom-call | tf_op jit(solution)/shard_map/pallas_call | solution.py:345
  11.2 3.1 %collective-permute-start = (f32[128,128]{1,0:T(8,128)S(1)}, f32[128,128]{1,0:T(8,128)S(1)}, u32[]{:S(2)}, u32[]{:S(2)}) collective-permute-start(f32[128,128]{1,0:T(8,128)S(1)} %get-tuple-element.25.own), channel_id=1, source_target_pairs={{0,8},{8,0},{16,24},{24,16},{1,9},{9,1},{17,25},{25,17},{2,10},{10... | collective-permute-start | bytes 196616 | tf_op jit(solution)/shard_map/ppermute | solution.py:322
  14.3 2.2 %collective-permute-done.recv = f32[128,128]{1,0:T(8,128)S(1)} collective-permute-done((f32[128,128]{1,0:T(8,128)S(1)}, f32[128,128]{1,0:T(8,128)S(1)}, u32[]{:S(2)}, u32[]{:S(2)}) %collective-permute-start) | collective-permute-done | bytes 65568 | tf_op jit(solution)/shard_map/ppermute | solution.py:322
  16.5 0.5 shard_map.144
  17.0 3.1 %collective-permute-start.1 = (f32[128,128]{1,0:T(8,128)S(1)}, f32[128,128]{1,0:T(8,128)S(1)}, u32[]{:S(2)}, u32[]{:S(2)}) collective-permute-start(f32[128,128]{1,0:T(8,128)S(1)} %get-tuple-element.27.own), channel_id=1, source_target_pairs={{0,16},{8,24},{16,0},{24,8},{1,17},{9,25},{17,1},{25,9},{2,18},{10... | collective-permute-start | bytes 196616 | tf_op jit(solution)/shard_map/ppermute | solution.py:322
  20.1 2.2 %collective-permute-done.1.recv = f32[128,128]{1,0:T(8,128)S(1)} collective-permute-done((f32[128,128]{1,0:T(8,128)S(1)}, f32[128,128]{1,0:T(8,128)S(1)}, u32[]{:S(2)}, u32[]{:S(2)}) %collective-permute-start.1) | collective-permute-done | bytes 65568 | tf_op jit(solution)/shard_map/ppermute | solution.py:322
  22.3 0.5 shard_map.145
  22.8 0.1 collective-permute-start.2
  22.9 1.3 %collective-permute-done.2.recv = f32[192,128]{1,0:T(8,128)S(1)} collective-permute-done((f32[192,128]{1,0:T(8,128)S(1)}, f32[192,128]{1,0:T(8,128)S(1)}, u32[]{:S(2)}, u32[]{:S(2)}) %collective-permute-start.2) | collective-permute-done | bytes 98336 | tf_op jit(solution)/shard_map/ppermute | solution.py:322
  24.2 0.5 shard_map.146
  24.7 1.9 %collective-permute-start.3 = (f32[192,128]{1,0:T(8,128)S(1)}, f32[192,128]{1,0:T(8,128)S(1)}, u32[]{:S(2)}, u32[]{:S(2)}) collective-permute-start(f32[192,128]{1,0:T(8,128)S(1)} %get-tuple-element.32.own), channel_id=1, source_target_pairs={{0,2},{1,3},{2,0},{3,1},{4,6},{5,7},{6,4},{7,5},{8,10},{9,11},{10,... | collective-permute-start | bytes 294920 | tf_op jit(solution)/shard_map/ppermute | solution.py:322
  26.5 3.1 %collective-permute-done.3.recv = f32[192,128]{1,0:T(8,128)S(1)} collective-permute-done((f32[192,128]{1,0:T(8,128)S(1)}, f32[192,128]{1,0:T(8,128)S(1)}, u32[]{:S(2)}, u32[]{:S(2)}) %collective-permute-start.3) | collective-permute-done | bytes 98336 | tf_op jit(solution)/shard_map/ppermute | solution.py:322
  29.7 0.5 shard_map.147
  30.1 1.8 %collective-permute-start.4 = (f32[256,128]{1,0:T(8,128)S(1)}, f32[256,128]{1,0:T(8,128)S(1)}, u32[]{:S(2)}, u32[]{:S(2)}) collective-permute-start(f32[256,128]{1,0:T(8,128)S(1)} %get-tuple-element.34.own), channel_id=1, source_target_pairs={{0,4},{1,5},{2,6},{3,7},{4,0},{5,1},{6,2},{7,3},{8,12},{9,13},{10,... | collective-permute-start | bytes 393224 | tf_op jit(solution)/shard_map/ppermute | solution.py:322
  32.0 3.2 %collective-permute-done.4.recv = f32[256,128]{1,0:T(8,128)S(1)} collective-permute-done((f32[256,128]{1,0:T(8,128)S(1)}, f32[256,128]{1,0:T(8,128)S(1)}, u32[]{:S(2)}, u32[]{:S(2)}) %collective-permute-start.4) | collective-permute-done | bytes 131104 | tf_op jit(solution)/shard_map/ppermute | solution.py:322
  35.2 0.5 shard_map.148
  35.6 1.9 %collective-permute-start.5 = (f32[64,128]{1,0:T(8,128)S(1)}, f32[64,128]{1,0:T(8,128)S(1)}, u32[]{:S(2)}, u32[]{:S(2)}) collective-permute-start(f32[64,128]{1,0:T(8,128)S(1)} %get-tuple-element.38.own), channel_id=1, source_target_pairs={{0,8},{8,0},{16,24},{24,16},{1,9},{9,1},{17,25},{25,17},{2,10},{10... | collective-permute-start | bytes 98312 | tf_op jit(solution)/shard_map/ppermute | solution.py:322
  37.5 2.1 %collective-permute-done.5.recv = f32[64,128]{1,0:T(8,128)S(1)} collective-permute-done((f32[64,128]{1,0:T(8,128)S(1)}, f32[64,128]{1,0:T(8,128)S(1)}, u32[]{:S(2)}, u32[]{:S(2)}) %collective-permute-start.5) | collective-permute-done | bytes 32800 | tf_op jit(solution)/shard_map/ppermute | solution.py:322
  39.6 0.5 shard_map.152
  40.1 3.0 %collective-permute-start.6 = (f32[64,128]{1,0:T(8,128)S(1)}, f32[64,128]{1,0:T(8,128)S(1)}, u32[]{:S(2)}, u32[]{:S(2)}) collective-permute-start(f32[64,128]{1,0:T(8,128)S(1)} %get-tuple-element.40.own), channel_id=1, source_target_pairs={{0,16},{8,24},{16,0},{24,8},{1,17},{9,25},{17,1},{25,9},{2,18},{10... | collective-permute-start | bytes 98312 | tf_op jit(solution)/shard_map/ppermute | solution.py:322
  43.1 0.0 copy-start
  43.1 5.1 %shard_map.139.table = bf16[4096,64]{1,0:T(8,128)(2,1)S(1)} custom-call(f32[1024,128]{1,0:T(8,128)S(1)} %get-tuple-element.24.refs_0_), custom_call_target="tpu_custom_call" | custom-call | tf_op jit(solution)/shard_map/pallas_call | solution.py:398
  48.2 0.0 copy-done
  48.2 0.0 copy-done.6
  48.2 2.8 %shard_map.140.refs_0_ = f32[1024,128]{1,0:T(8,128)S(1)} custom-call(s32[1,2,64]{2,1,0:T(2,128)S(1)} %copy-done.6, s32[1,2,64]{2,1,0:T(2,128)S(1)} %copy-done.6, bf16[4096,64]{1,0:T(8,128)(2,1)S(1)} %shard_map.139.table, bf16[1,64,4096]{2,1,0:T(8,128)(2,1)S(1)} %copy-done), custom_call_target="tpu_custom_call" | custom-call | tf_op jit(solution)/shard_map/pallas_call | solution.py:412
  51.0 2.6 %shard_map.141.refs_1_ = f32[1024,128]{1,0:T(8,128)S(1)} custom-call(s32[1,2,64]{2,1,0:T(2,128)S(1)} %copy-done.6, s32[1,2,64]{2,1,0:T(2,128)S(1)} %copy-done.6, bf16[4096,64]{1,0:T(8,128)(2,1)S(1)} %shard_map.139.table, bf16[1,64,4096]{2,1,0:T(8,128)(2,1)S(1)} %copy-done), custom_call_target="tpu_custom_call" | custom-call | tf_op jit(solution)/shard_map/pallas_call | solution.py:412
  53.6 4.8 %shard_map.142.refs_2_ = f32[2048,128]{1,0:T(8,128)S(1)} custom-call(s32[1,2,64]{2,1,0:T(2,128)S(1)} %copy-done.6, s32[1,2,64]{2,1,0:T(2,128)S(1)} %copy-done.6, bf16[4096,64]{1,0:T(8,128)(2,1)S(1)} %shard_map.139.table, bf16[1,64,4096]{2,1,0:T(8,128)(2,1)S(1)} %copy-done), custom_call_target="tpu_custom_call" | custom-call | tf_op jit(solution)/shard_map/pallas_call | solution.py:412
  58.5 2.1 %shard_map.143 = f32[1,64,4096]{2,1,0:T(8,128)} custom-call(f32[1024,128]{1,0:T(8,128)S(1)} %shard_map.140.refs_0_, f32[1024,128]{1,0:T(8,128)S(1)} %shard_map.141.refs_1_, f32[2048,128]{1,0:T(8,128)S(1)} %shard_map.142.refs_2_), custom_call_target="tpu_custom_call" | custom-call | tf_op jit(solution)/shard_map/pallas_call | solution.py:420
  60.6 4.9 %shard_map.149.table = bf16[2048,64]{1,0:T(8,128)(2,1)S(1)} custom-call(f32[256,128]{1,0:T(8,128)S(1)} %get-tuple-element.36.refs_0_, f32[128,128]{1,0:T(8,128)S(1)} %get-tuple-element.37.refs_1_), custom_call_target="tpu_custom_call" | custom-call | tf_op jit(solution)/shard_map/pallas_call | solution.py:398
  65.5 0.0 copy-done.3
  65.5 0.0 copy-done.9
  65.5 0.0 copy-done.10
  65.5 5.0 %shard_map.150.refs_0_ = f32[2048,128]{1,0:T(8,128)S(1)} custom-call(s32[1,1,32]{2,1,0:T(1,128)S(1)} %copy-done.9, s32[1,1,32]{2,1,0:T(1,128)S(1)} %copy-done.10, bf16[2048,64]{1,0:T(8,128)(2,1)S(1)} %shard_map.149.table, bf16[1,32,4096]{2,1,0:T(8,128)(2,1)S(1)} %copy-done.3), custom_call_target="tpu_custom_call" | custom-call | tf_op jit(solution)/shard_map/pallas_call | solution.py:412
  70.5 1.4 %shard_map.151 = f32[1,32,4096]{2,1,0:T(8,128)} custom-call(f32[2048,128]{1,0:T(8,128)S(1)} %shard_map.150.refs_0_), custom_call_target="tpu_custom_call" | custom-call | tf_op jit(solution)/shard_map/pallas_call | solution.py:420
  71.9 0.0 collective-permute-done.6.recv
  71.9 5.4 %shard_map.154 = (f32[1,1,4096]{2,1,0:T(1,128)}, f32[1,1,4096]{2,1,0:T(1,128)}) custom-call(f32[64,128]{1,0:T(8,128)S(1)} %shard_map.153.high), custom_call_target="tpu_custom_call" | custom-call | tf_op jit(solution)/shard_map/pallas_call | solution.py:447
  (5 shorter events, 0.0 us)
Async XLA Ops:
  0.6 1.0 %copy-start.1 = (f32[1,32,4096]{2,1,0:T(8,128)S(1)}, f32[1,32,4096]{2,1,0:T(8,128)}, u32[]{:S(2)}) copy-start(f32[1,32,4096]{2,1,0:T(8,128)} %row_transfer.1) | copy-start | bytes 1572868
  1.7 1.0 %copy-start.2 = (f32[1,32,4096]{2,1,0:T(8,128)S(1)}, f32[1,32,4096]{2,1,0:T(8,128)}, u32[]{:S(2)}) copy-start(f32[1,32,4096]{2,1,0:T(8,128)} %col_transfer.1) | copy-start | bytes 1572868
  2.7 0.9 %copy-start.4 = (f32[1,16,4096]{2,1,0:T(8,128)S(1)}, f32[1,16,4096]{2,1,0:T(8,128)}, u32[]{:S(2)}) copy-start(f32[1,16,4096]{2,1,0:T(8,128)} %row_bases.1) | copy-start | bytes 786436
  3.7 0.9 %copy-start.5 = (f32[1,16,4096]{2,1,0:T(8,128)S(1)}, f32[1,16,4096]{2,1,0:T(8,128)}, u32[]{:S(2)}) copy-start(f32[1,16,4096]{2,1,0:T(8,128)} %col_bases.1) | copy-start | bytes 786436
  4.6 0.7 copy-start.7
  5.3 0.7 copy-start.8
  11.2 5.4 %collective-permute-start = (f32[128,128]{1,0:T(8,128)S(1)}, f32[128,128]{1,0:T(8,128)S(1)}, u32[]{:S(2)}, u32[]{:S(2)}) collective-permute-start(f32[128,128]{1,0:T(8,128)S(1)} %get-tuple-element.25.own), channel_id=1, source_target_pairs={{0,8},{8,0},{16,24},{24,16},{1,9},{9,1},{17,25},{25,17},{2,10},{10... | collective-permute-start | bytes 196616 | tf_op jit(solution)/shard_map/ppermute | solution.py:322
  17.0 5.3 %collective-permute-start.1 = (f32[128,128]{1,0:T(8,128)S(1)}, f32[128,128]{1,0:T(8,128)S(1)}, u32[]{:S(2)}, u32[]{:S(2)}) collective-permute-start(f32[128,128]{1,0:T(8,128)S(1)} %get-tuple-element.27.own), channel_id=1, source_target_pairs={{0,16},{8,24},{16,0},{24,8},{1,17},{9,25},{17,1},{25,9},{2,18},{10... | collective-permute-start | bytes 196616 | tf_op jit(solution)/shard_map/ppermute | solution.py:322
  22.8 1.4 %collective-permute-start.2 = (f32[192,128]{1,0:T(8,128)S(1)}, f32[192,128]{1,0:T(8,128)S(1)}, u32[]{:S(2)}, u32[]{:S(2)}) collective-permute-start(f32[192,128]{1,0:T(8,128)S(1)} %get-tuple-element.30.own), channel_id=1, source_target_pairs={{0,1},{1,0},{2,3},{3,2},{4,5},{5,4},{6,7},{7,6},{8,9},{9,8},{10,11... | collective-permute-start | bytes 294920 | tf_op jit(solution)/shard_map/ppermute | solution.py:322
  24.7 5.0 %collective-permute-start.3 = (f32[192,128]{1,0:T(8,128)S(1)}, f32[192,128]{1,0:T(8,128)S(1)}, u32[]{:S(2)}, u32[]{:S(2)}) collective-permute-start(f32[192,128]{1,0:T(8,128)S(1)} %get-tuple-element.32.own), channel_id=1, source_target_pairs={{0,2},{1,3},{2,0},{3,1},{4,6},{5,7},{6,4},{7,5},{8,10},{9,11},{10,... | collective-permute-start | bytes 294920 | tf_op jit(solution)/shard_map/ppermute | solution.py:322
  30.1 5.0 %collective-permute-start.4 = (f32[256,128]{1,0:T(8,128)S(1)}, f32[256,128]{1,0:T(8,128)S(1)}, u32[]{:S(2)}, u32[]{:S(2)}) collective-permute-start(f32[256,128]{1,0:T(8,128)S(1)} %get-tuple-element.34.own), channel_id=1, source_target_pairs={{0,4},{1,5},{2,6},{3,7},{4,0},{5,1},{6,2},{7,3},{8,12},{9,13},{10,... | collective-permute-start | bytes 393224 | tf_op jit(solution)/shard_map/ppermute | solution.py:322
  35.6 4.0 %collective-permute-start.5 = (f32[64,128]{1,0:T(8,128)S(1)}, f32[64,128]{1,0:T(8,128)S(1)}, u32[]{:S(2)}, u32[]{:S(2)}) collective-permute-start(f32[64,128]{1,0:T(8,128)S(1)} %get-tuple-element.38.own), channel_id=1, source_target_pairs={{0,8},{8,0},{16,24},{24,16},{1,9},{9,1},{17,25},{25,17},{2,10},{10... | collective-permute-start | bytes 98312 | tf_op jit(solution)/shard_map/ppermute | solution.py:322
  40.1 31.8 %collective-permute-start.6 = (f32[64,128]{1,0:T(8,128)S(1)}, f32[64,128]{1,0:T(8,128)S(1)}, u32[]{:S(2)}, u32[]{:S(2)}) collective-permute-start(f32[64,128]{1,0:T(8,128)S(1)} %get-tuple-element.40.own), channel_id=1, source_target_pairs={{0,16},{8,24},{16,0},{24,8},{1,17},{9,25},{17,1},{25,9},{2,18},{10... | collective-permute-start | bytes 98312 | tf_op jit(solution)/shard_map/ppermute | solution.py:322
  43.1 5.1 %copy-start = (bf16[1,64,4096]{2,1,0:T(8,128)(2,1)S(1)}, bf16[1,64,4096]{2,1,0:T(8,128)(2,1)}, u32[]{:S(2)}) copy-start(bf16[1,64,4096]{2,1,0:T(8,128)(2,1)} %blocks.6) | copy-start | bytes 1572868
  43.1 5.1 %copy-start.6 = (s32[1,2,64]{2,1,0:T(2,128)S(1)}, s32[1,2,64]{2,1,0:T(2,128)}, u32[]{:S(2)}) copy-start(s32[1,2,64]{2,1,0:T(2,128)} %right_pick.6) | copy-start | bytes 1540
  60.6 4.9 %copy-start.3 = (bf16[1,32,4096]{2,1,0:T(8,128)(2,1)S(1)}, bf16[1,32,4096]{2,1,0:T(8,128)(2,1)}, u32[]{:S(2)}) copy-start(bf16[1,32,4096]{2,1,0:T(8,128)(2,1)} %blocks.7) | copy-start | bytes 786436
  60.6 4.9 %copy-start.9 = (s32[1,1,32]{2,1,0:T(1,128)S(1)}, s32[1,1,32]{2,1,0:T(1,128)}, u32[]{:S(2)}) copy-start(s32[1,1,32]{2,1,0:T(1,128)} %left_pick.7) | copy-start | bytes 388
  60.6 4.9 %copy-start.10 = (s32[1,1,32]{2,1,0:T(1,128)S(1)}, s32[1,1,32]{2,1,0:T(1,128)}, u32[]{:S(2)}) copy-start(s32[1,1,32]{2,1,0:T(1,128)} %right_pick.7) | copy-start | bytes 388

commit v3 on v2

--- a/solution.py
+++ b/solution.py
@@ -63,36 +63,99 @@
     )
 
 
-def unpack_both(left_ref, right_ref, out_ref, count):
-    for k in range(RANK // 2):
-        a = left_ref[0, :, k * WIDE : (k + 1) * WIDE]
-        b = right_ref[0, :, k * WIDE : (k + 1) * WIDE]
-        out_ref[pl.ds(2 * k, count, stride=RANK), :] = beside(a, swapped(b))
-        out_ref[pl.ds(2 * k + 1, count, stride=RANK), :] = beside(swapped(a), b)
+def swap8(tiles):
+    tiles = list(tiles)
+    sub = lax.broadcasted_iota(jnp.int32, tiles[0].shape, 0)
+    for d in (4, 2, 1):
+        keep = (sub & d) == 0
+        for i in range(SUB):
+            if not i & d:
+                a, b = tiles[i], tiles[i + d]
+                tiles[i] = jnp.where(keep, a, pltpu.roll(b, d, 0))
+                tiles[i + d] = jnp.where(keep, pltpu.roll(a, SUB - d, 0), b)
+    return tiles
+
+
+def eight(n):
+    return slice(SUB * n, SUB * (n + 1))
+
+
+def unpack_both(left, right, store):
+    for q in range(NB):
+        rows = []
+        for k in range(SUB // 2 * q, SUB // 2 * (q + 1)):
+            a, b = left(k), right(k)
+            rows += [beside(a, swapped(b)), beside(swapped(a), b)]
+        for b, tile in enumerate(swap8(rows)):
+            store(b, q, tile)
+
+
+def lanes_of(k):
+    return slice(k * WIDE, (k + 1) * WIDE)
+
+
+def unpack_trees(left_ref, right_ref, out_ref, count):
+    for g in range(count // SUB):
+
+        def store(b, q, tile):
+            at = (SUB * g + b) * RANK + SUB * q
+            out_ref[at : at + SUB, :] = tile
+
+        unpack_both(
+            lambda k: left_ref[0, eight(g), lanes_of(k)],
+            lambda k: right_ref[0, eight(g), lanes_of(k)],
+            store,
+        )
 
 
 def tree_kernel(
     count,
-    row_order,
-    col_order,
+    row_order_in,
+    col_order_in,
+    row_bases_in,
+    col_bases_in,
+    row_transfer_in,
+    col_transfer_in,
+    leaf_gram,
+    row_pay,
+    col_pay,
+    high,
     row_bases,
     col_bases,
     row_transfer,
     col_transfer,
-    leaf_gram,
-    row_pay,
-    col_pay,
-    high,
+    row_order,
+    col_order,
     basis,
     trans,
+    sems,
 ):
-    unpack_both(row_bases, col_bases, basis, count)
-    unpack_both(row_transfer, col_transfer, trans, 2 * count)
+    copies = [
+        pltpu.make_async_copy(source, target, sems.at[n])
+        for n, (source, target) in enumerate(
+            (
+                (row_bases_in, row_bases),
+                (col_bases_in, col_bases),
+                (row_transfer_in, row_transfer),
+                (col_transfer_in, col_transfer),
+                (row_order_in, row_order),
+                (col_order_in, col_order),
+            )
+        )
+    ]
+    for copy in copies:
+        copy.start()
+    copies[0].wait()
+    copies[1].wait()
+    unpack_trees(row_bases, col_bases, basis, count)
     for leaf in range(count):
         u = basis[leaf * RANK : (leaf + 1) * RANK, :]
         leaf_gram[leaf * RANK : (leaf + 1) * RANK, :] = dot_both(
             jnp.concatenate([u, u], axis=0).T, u
         )
+    for copy in copies[2:]:
+        copy.wait()
+    unpack_trees(row_transfer, col_transfer, trans, 2 * count)
     nodes = []
     for q in range(count // 2):
         total = None
@@ -222,81 +285,121 @@
                     a_ref[SUB * pi + r, at(q), :] = value
 
 
-def load_lanes(slots_ref, a_ref, count):
+def put_row(a_ref, i, rows):
+    b0 = SUB * (i // SUB)
+    t = rows.T
+    a_ref[i, b0:RANK, 0 : 2 * rows.shape[0]] = jnp.concatenate([t[b0:RANK], t[RANK + b0 :]], axis=1)
+
+
+def get_row(r_ref, i, count):
+    b0 = SUB * (i // SUB)
+    parts = []
+    for half in range(2):
+        if b0:
+            parts.append(jnp.zeros((b0, count), F32))
+        parts.append(r_ref[i, b0:RANK, half * count : (half + 1) * count])
+    return jnp.concatenate(parts, axis=0).T
+
+
+def chol_table_kernel(count, shapes, *refs):
+    inputs = refs[: len(shapes)]
+    left, right, a_ref, r_ref = refs[len(shapes) : len(shapes) + 4]
+    slots = [(ref, s) for ref in inputs for s in range(ref.shape[0] // RANK)]
+    slots += [slots[-1]] * (count - len(slots))
+    for q in range(NB):
+        groups = []
+        for g in range(count // SUB):
+            groups.append(
+                swap8(
+                    [
+                        ref[s * RANK + SUB * q : s * RANK + SUB * (q + 1), :]
+                        for ref, s in slots[SUB * g : SUB * (g + 1)]
+                    ]
+                )
+            )
+        for r in range(SUB):
+            put_row(a_ref, SUB * q + r, jnp.concatenate([tiles[r] for tiles in groups], axis=0))
+    chol_lanes(a_ref, r_ref)
+    keep = lane_half(2 * SUB)
+    for q in range(0, NB, 2):
+        rows = [get_row(r_ref, SUB * q + r, count) for r in range(2 * SUB)]
+        for g in range(count // SUB):
+            upper = swap8([row[eight(g)] for row in rows[:SUB]])
+            lower = swap8([row[eight(g)] for row in rows[SUB:]])
+            for b in range(SUB):
+                both = jnp.concatenate([upper[b], lower[b]], axis=0)
+                other = swapped(both)
+                for n, here, there in (
+                    (SUB * g + b, both, other),
+                    (count + SUB * g + b, other, both),
+                ):
+                    at = n * WIDE + SUB * q
+                    for table, value in (
+                        (left, jnp.where(keep, here, 0.0)),
+                        (right, jnp.where(keep, 0.0, there)),
+                    ):
+                        high, low = split(value)
+                        table[at : at + 2 * SUB, :] = high
+                        table[at + RANK : at + RANK + 2 * SUB, :] = low
+
+
+def final_kernel(high, row_out, col_out, a_ref, r_ref):
     for i in range(RANK):
-        b0 = SUB * (i // SUB)
-        t = slots_ref[pl.ds(i, count, stride=RANK), :].T
-        a_ref[i, b0:RANK, 0 : 2 * count] = jnp.concatenate([t[b0:RANK], t[RANK + b0 :]], axis=1)
-
-
-def factor_row(r_ref, i, lanes):
-    b0 = SUB * (i // SUB)
-    t = r_ref[i, b0:RANK, 0:lanes]
-    if b0:
-        t = jnp.concatenate([jnp.zeros((b0, lanes), F32), t], axis=0)
-    return t.T
-
-
-def chol_table_kernel(count, sources, *refs):
-    inputs = refs[: len(sources)]
-    table, a_ref, r_ref, factor = refs[len(sources) : len(sources) + 4]
-    if len(sources) > 1:
-        slots = refs[len(sources) + 4]
-        base = 0
-        for ref in inputs:
-            slots[base : base + ref.shape[0], :] = ref[...]
-            base += ref.shape[0]
-    else:
-        slots = inputs[0]
-    load_lanes(slots, a_ref, count)
-    chol_lanes(a_ref, r_ref)
-    for i in range(RANK):
-        factor[pl.ds(i, 2 * count, stride=RANK), :] = factor_row(r_ref, i, 2 * count)
-    for b in range(2 * count):
-        table[b * WIDE : (b + 1) * WIDE, :] = stacked(factor[b * RANK : (b + 1) * RANK, :])
-
-
-def final_kernel(high, row_out, col_out, slots, a_ref, r_ref):
-    slots[0:RANK, :] = high[...]
-    load_lanes(slots, a_ref, SUB)
+        put_row(a_ref, i, jnp.broadcast_to(high[i : i + 1, :], (SUB, WIDE)))
     chol_lanes(a_ref, r_ref)
     for k in range(RANK // 2):
-        even = factor_row(r_ref, 2 * k, 2 * SUB)
-        odd = factor_row(r_ref, 2 * k + 1, 2 * SUB)
-        both = jnp.concatenate([even, odd], axis=1)
-        row_out[0, 0:1, k * WIDE : (k + 1) * WIDE] = both[0:1]
-        col_out[0, 0:1, k * WIDE : (k + 1) * WIDE] = both[SUB : SUB + 1]
-
-
-def couple_kernel(start, pairs, left_of, right_of, left_pick, right_pick, table, blocks, y_ref, s_ref):
-    for k in range(RANK // 2):
-        slab = blocks[0, start : start + pairs, k * WIDE : (k + 1) * WIDE].astype(F32)
-        s_ref[pl.ds(2 * k, pairs, stride=RANK), :] = slab[:, :RANK]
-        s_ref[pl.ds(2 * k + 1, pairs, stride=RANK), :] = swapped(slab)[:, :RANK]
-
-    def one(b, carry):
-        t = pl.multiple_of(left_of(left_pick, start + b) * WIDE, WIDE)
-        s = pl.multiple_of(right_of(right_pick, start + b) * WIDE, WIDE)
-        at = pl.ds(pl.multiple_of(b * RANK, RANK), RANK)
-        x = dot(table[pl.ds(t, WIDE), :], s_ref[at, :].astype(BF16))
-        y = dot(stacked(x[:RANK] + x[RANK:]), table[pl.ds(s, WIDE), :], 1)
-        y = y[:RANK] + y[RANK:]
-        y_ref[at, :] = y + swapped(y)
+        even = get_row(r_ref, 2 * k, SUB)
+        odd = get_row(r_ref, 2 * k + 1, SUB)
+        row_out[0, 0:1, lanes_of(k)] = beside(even, swapped(odd))[0:1]
+        col_out[0, 0:1, lanes_of(k)] = beside(swapped(even), odd)[0:1]
+
+
+def couple_kernel(pairs, left_of, right_of, left_pick, right_pick, left, right, blocks, out, s_ref, y_ref):
+    def group(g, carry):
+        start = pl.multiple_of(g * 2 * SUB, 2 * SUB)
+
+        def slab(k):
+            return blocks[0, pl.ds(start, 2 * SUB), lanes_of(k)].astype(F32)
+
+        def keep(b, q, tile):
+            s_ref[b * RANK + SUB * q : b * RANK + SUB * (q + 1), :] = tile
+
+        unpack_both(lambda k: slab(k)[:SUB], lambda k: slab(k)[SUB:], keep)
+
+        def entry(table, pick, ref, b):
+            return table[pl.ds(pl.multiple_of(pick(ref, start + b) * WIDE, WIDE), WIDE), :]
+
+        for b in range(SUB):
+            block = s_ref[b * RANK : (b + 1) * RANK, :].astype(BF16)
+            rows = jnp.concatenate(
+                [entry(left, left_of, left_pick, n)[:, :RANK] for n in (b, b + SUB)], axis=0
+            )
+            x = dot(rows, block)
+            x = beside(x[:RANK], x[WIDE : WIDE + RANK]) + beside(
+                x[RANK:WIDE], x[WIDE + RANK :]
+            )
+            first = entry(left, right_of, right_pick, b)
+            second = entry(right, right_of, right_pick, b + SUB)
+            weights = jnp.concatenate(
+                [first[:RANK], second[:RANK], first[RANK:], second[RANK:]], axis=0
+            )
+            y = dot(stacked(x), weights, 1)
+            y = y[:RANK] + y[RANK:]
+            y_ref[b * RANK : (b + 1) * RANK, :] = y[:, :WIDE] + y[:, WIDE:]
+        for q in range(NB):
+            rows = swap8(
+                [y_ref[b * RANK + SUB * q : b * RANK + SUB * (q + 1), :] for b in range(SUB)]
+            )
+            for k in range(SUB // 2):
+                even, odd = rows[2 * k], rows[2 * k + 1]
+                at = lanes_of(SUB // 2 * q + k)
+                out[0, pl.ds(start, SUB), at] = beside(even, swapped(odd))
+                out[0, pl.ds(pl.multiple_of(start + SUB, SUB), SUB), at] = beside(
+                    swapped(even), odd
+                )
         return carry
 
-    lax.fori_loop(0, pairs, one, 0, unroll=8)
-
-
-def pack_kernel(sizes, *refs):
-    inputs, out = refs[: len(sizes)], refs[len(sizes)]
-    for k in range(RANK // 2):
-        base = 0
-        for pairs, y_ref in zip(sizes, inputs):
-            out[0, base : base + pairs, k * WIDE : (k + 1) * WIDE] = beside(
-                y_ref[pl.ds(2 * k, pairs, stride=RANK), :],
-                y_ref[pl.ds(2 * k + 1, pairs, stride=RANK), :],
-            )
-            base += pairs
+    lax.fori_loop(0, pairs // (2 * SUB), group, 0)
 
 
 def shape(*dims):
@@ -336,8 +439,6 @@
     root_blocks,
 ):
     count = row_bases.shape[1]
-    leaf_pairs = leaf_blocks.shape[1]
-    root_pairs = root_blocks.shape[1]
     nr, nc = lax.axis_size("row"), lax.axis_size("col")
     lr, lc = nr.bit_length() - 1, nc.bit_length() - 1
     top = lr + lc - 1
@@ -345,8 +446,10 @@
     leaf_gram, row_pay, col_pay, high = call(
         functools.partial(tree_kernel, count),
         [shape(count * RANK, WIDE), shape(WIDE, WIDE), shape(WIDE, WIDE), shape(RANK, WIDE)],
-        [SMEM, SMEM, VMEM, VMEM, VMEM, VMEM],
-        [scratch(count * RANK), scratch(2 * count * RANK)],
+        [pl.BlockSpec(memory_space=pltpu.HBM)] * 6,
+        [pltpu.VMEM(x.shape, F32) for x in (row_bases, col_bases, row_transfer, col_transfer)]
+        + [pltpu.SMEM(x.shape, jnp.int32) for x in (row_order, col_order)]
+        + [scratch(count * RANK), scratch(2 * count * RANK), pltpu.SemaphoreType.DMA((6,))],
     )(row_order, col_order, row_bases, col_bases, row_transfer, col_transfer)
 
     def step(levels, pay, axis, bit, high, held=0, apart=False, extra=None):
@@ -394,61 +497,45 @@
 
     big = [pltpu.VMEM((RANK, RANK, WIDE), F32)] * 2
 
-    def table(count, *sources):
+    def tables(count, *sources):
+        out = jax.ShapeDtypeStruct((2 * count * WIDE, WIDE), BF16)
         return call(
             functools.partial(chol_table_kernel, count, [x.shape for x in sources]),
-            jax.ShapeDtypeStruct((2 * count * WIDE, RANK), BF16),
+            [out, out],
             [VMEM] * len(sources),
-            big
-            + [scratch(2 * count * RANK, RANK)]
-            + ([scratch(count * RANK)] if len(sources) > 1 else []),
+            big,
             limit=5 + count // 3,
         )(*sources)
 
-    def couple(parts, total, left_of, right_of, left_pick, right_pick, table, blocks):
-        pieces, start = [], 0
-        for pairs in parts:
-            pieces.append(
-                call(
-                    functools.partial(couple_kernel, start, pairs, left_of, right_of),
-                    shape(pairs * RANK, WIDE),
-                    [SMEM, SMEM, VMEM, VMEM],
-                    [scratch(pairs * RANK, RANK)],
-                )(left_pick, right_pick, table, blocks)
-            )
-            start += pairs
+    def couple(left_of, right_of, left_pick, right_pick, factors, blocks):
+        pairs = blocks.shape[1]
         return call(
-            functools.partial(pack_kernel, parts), shape(1, total, RANK * RANK), [VMEM] * len(parts)
-        )(*pieces)
-
-    quarter = leaf_pairs // 4
+            functools.partial(couple_kernel, pairs, left_of, right_of),
+            shape(1, pairs, RANK * RANK),
+            [SMEM, SMEM, VMEM, VMEM, VMEM],
+            [scratch(SUB * RANK), scratch(SUB * RANK)],
+        )(left_pick, right_pick, *factors, blocks)
+
     leaf_coupled = couple(
-        (quarter, quarter, 2 * quarter),
-        leaf_pairs,
         lambda ref, b: ref[0, 0, b],
         lambda ref, b: ref[0, 1, b] + count,
         leaf_pattern,
         leaf_pattern,
-        table(count, leaf_gram),
+        tables(count, leaf_gram),
         leaf_blocks,
     )
     row_slots, col_slots = nc // 2, nr // 2
     slots = -(-(row_slots + col_slots) // SUB) * SUB
     root_coupled = couple(
-        (root_pairs,),
-        root_pairs,
         lambda ref, b: (ref[0, 0, b] & 1) * slots + (ref[0, 0, b] >> 1),
         lambda ref, b: (ref[0, 0, b] & 1) * slots + (ref[0, 0, b] >> 1) + row_slots,
         root_rows,
         root_cols,
-        table(slots, row_roots, col_roots),
+        tables(slots, row_roots, col_roots),
         root_blocks,
     )
     row_upper_r, col_upper_r = call(
-        final_kernel,
-        [shape(1, 1, RANK * RANK), shape(1, 1, RANK * RANK)],
-        [VMEM],
-        [scratch(SUB * RANK)] + big,
+        final_kernel, [shape(1, 1, RANK * RANK), shape(1, 1, RANK * RANK)], [VMEM], big
     )(high)
     return (leaf_coupled, root_coupled, row_upper_r, col_upper_r)
 

time: 77.6 us -> 71 us (0.915)
  Pallas kernels: 42 us -> 34.2 us
  local copies, waits for them, and re-layouts: 5.3 us -> 6.6 us
    pallas_call x8 -> x4, Pallas kernels: 28.6 us -> 19 us  [the longest x2 11.3 us: tables(): call(functools.partial(chol_table_kernel, count, [x.shape for x in source...]
    pallas_call x1, Pallas kernels: 5.35 us -> 8.23 us  [body(): call(final_kernel, [shape(1, 1, RANK * RANK), shape(1, 1, RANK * RANK)],...]
    unnamed x22, local copies, waits for them, and re-layouts: 5.3 us -> 6.6 us
    pallas_call x1, Pallas kernels: 5.23 us -> 4.15 us  [body(): call(functools.partial(tree_kernel, count), [shape(count * RANK, WIDE), s...]
  transfers between devices with their start and end apart: 7 -> 7, of which waited for: 6 -> 6; matrix products, arithmetic and copies ran while one was open for 0% -> 0% of each run, Pallas kernels for 37% -> 27%
where the time goes in v3:
time: 71 us; the launch traced here: 70.7 us
  Pallas kernels  34.2 us (48%)
  starting transfers between devices  14.9 us (21%)
  waiting for transfers between devices  14.2 us (20%)
  local copies, waits for them, and re-layouts  6.6 us (9%)
  between operations  0.78 us (1%)
    ppermute x7, starting transfers between devices, partner(): lax.ppermute(value, axis, [(i, i ^ 1 << bit) for i in range(lax.axis_size...  14.9 us
    ppermute x7, waiting for transfers between devices, partner(): lax.ppermute(value, axis, [(i, i ^ 1 << bit) for i in range(lax.axis_size...  14.2 us
    pallas_call x2, Pallas kernels, tables(): call(functools.partial(chol_table_kernel, count, [x.shape for x in source...  11.3 us
    pallas_call x1, Pallas kernels, body(): call(final_kernel, [shape(1, 1, RANK * RANK), shape(1, 1, RANK * RANK)],...  8.23 us
    pallas_call x2, Pallas kernels, couple(): call(functools.partial(couple_kernel, pairs, left_of, right_of), shape(1,...  7.72 us
    unnamed x22, local copies, waits for them, and re-layouts  6.6 us
    pallas_call x1, Pallas kernels, body(): call(functools.partial(tree_kernel, count), [shape(count * RANK, WIDE), s...  4.15 us
    pallas_call x7, Pallas kernels, step(): call(functools.partial(step_kernel, levels, top, (nr, nc), held, apart, e...  2.8 us
  transfers between devices with their start and end apart: 7, of which 6 were waited for; matrix products, arithmetic and copies ran while one was open for 0% of the time, Pallas kernels for 27%

profile of v3, /device:TPU:0, one launch (start us, length us, event | category | flops | bytes accessed | tf_op | source)
XLA Modules:
  0.0 70.7 jit_solution(3506199724322128629)
XLA Ops:
  0.6 0.0 copy-start.1
  0.6 1.0 %copy-done.1 = f32[1,32,4096]{2,1,0:T(8,128)S(1)} copy-done((f32[1,32,4096]{2,1,0:T(8,128)S(1)}, f32[1,32,4096]{2,1,0:T(8,128)}, u32[]{:S(2)}) %copy-start.1) | copy-done | bytes 524312
  1.7 0.0 copy-start.2
  1.7 1.0 %copy-done.2 = f32[1,32,4096]{2,1,0:T(8,128)S(1)} copy-done((f32[1,32,4096]{2,1,0:T(8,128)S(1)}, f32[1,32,4096]{2,1,0:T(8,128)}, u32[]{:S(2)}) %copy-start.2) | copy-done | bytes 524312
  2.7 0.0 copy-start.4
  2.7 0.9 %copy-done.4 = f32[1,16,4096]{2,1,0:T(8,128)S(1)} copy-done((f32[1,16,4096]{2,1,0:T(8,128)S(1)}, f32[1,16,4096]{2,1,0:T(8,128)}, u32[]{:S(2)}) %copy-start.4) | copy-done | bytes 262168
  3.7 0.0 copy-start.5
  3.7 0.9 %copy-done.5 = f32[1,16,4096]{2,1,0:T(8,128)S(1)} copy-done((f32[1,16,4096]{2,1,0:T(8,128)S(1)}, f32[1,16,4096]{2,1,0:T(8,128)}, u32[]{:S(2)}) %copy-start.5) | copy-done | bytes 262168
  4.6 0.0 copy-start.7
  4.6 0.7 copy-done.7
  5.3 0.0 copy-start.8
  5.3 0.7 copy-done.8
  5.9 4.1 %shard_map.138 = (f32[1024,128]{1,0:T(8,128)S(1)}, f32[128,128]{1,0:T(8,128)S(1)}, f32[128,128]{1,0:T(8,128)S(1)}, f32[64,128]{1,0:T(8,128)S(1)}) custom-call(s32[1,1,16]{2,1,0:T(1,128)S(1)} %copy-done.7, s32[1,1,16]{2,1,0:T(1,128)S(1)} %copy-done.8, f32[1,16,4096]{2,1,0:T(8,128)S(1)} %copy-done.4, f32[1,16,4096]{2,1,0:T(8,128)S(1)} %copy-done.5, ...), custom_call_target="tpu_custom_call" | custom-call | tf_op jit(solution)/shard_map/pallas_call | solution.py:446
  10.1 3.1 %collective-permute-start = (f32[128,128]{1,0:T(8,128)S(1)}, f32[128,128]{1,0:T(8,128)S(1)}, u32[]{:S(2)}, u32[]{:S(2)}) collective-permute-start(f32[128,128]{1,0:T(8,128)S(1)} %get-tuple-element.31.own), channel_id=1, source_target_pairs={{0,8},{8,0},{16,24},{24,16},{1,9},{9,1},{17,25},{25,17},{2,10},{10... | collective-permute-start | bytes 196616 | tf_op jit(solution)/shard_map/ppermute | solution.py:425
  13.2 2.2 %collective-permute-done.recv = f32[128,128]{1,0:T(8,128)S(1)} collective-permute-done((f32[128,128]{1,0:T(8,128)S(1)}, f32[128,128]{1,0:T(8,128)S(1)}, u32[]{:S(2)}, u32[]{:S(2)}) %collective-permute-start) | collective-permute-done | bytes 65568 | tf_op jit(solution)/shard_map/ppermute | solution.py:425
  15.4 0.5 shard_map.141
  15.9 3.1 %collective-permute-start.1 = (f32[128,128]{1,0:T(8,128)S(1)}, f32[128,128]{1,0:T(8,128)S(1)}, u32[]{:S(2)}, u32[]{:S(2)}) collective-permute-start(f32[128,128]{1,0:T(8,128)S(1)} %get-tuple-element.33.own), channel_id=1, source_target_pairs={{0,16},{8,24},{16,0},{24,8},{1,17},{9,25},{17,1},{25,9},{2,18},{10... | collective-permute-start | bytes 196616 | tf_op jit(solution)/shard_map/ppermute | solution.py:425
  19.0 2.2 %collective-permute-done.1.recv = f32[128,128]{1,0:T(8,128)S(1)} collective-permute-done((f32[128,128]{1,0:T(8,128)S(1)}, f32[128,128]{1,0:T(8,128)S(1)}, u32[]{:S(2)}, u32[]{:S(2)}) %collective-permute-start.1) | collective-permute-done | bytes 65568 | tf_op jit(solution)/shard_map/ppermute | solution.py:425
  21.3 0.5 shard_map.142
  21.7 0.1 collective-permute-start.2
  21.8 1.3 %collective-permute-done.2.recv = f32[192,128]{1,0:T(8,128)S(1)} collective-permute-done((f32[192,128]{1,0:T(8,128)S(1)}, f32[192,128]{1,0:T(8,128)S(1)}, u32[]{:S(2)}, u32[]{:S(2)}) %collective-permute-start.2) | collective-permute-done | bytes 98336 | tf_op jit(solution)/shard_map/ppermute | solution.py:425
  23.1 0.5 shard_map.143
  23.6 1.9 %collective-permute-start.3 = (f32[192,128]{1,0:T(8,128)S(1)}, f32[192,128]{1,0:T(8,128)S(1)}, u32[]{:S(2)}, u32[]{:S(2)}) collective-permute-start(f32[192,128]{1,0:T(8,128)S(1)} %get-tuple-element.38.own), channel_id=1, source_target_pairs={{0,2},{1,3},{2,0},{3,1},{4,6},{5,7},{6,4},{7,5},{8,10},{9,11},{10,... | collective-permute-start | bytes 294920 | tf_op jit(solution)/shard_map/ppermute | solution.py:425
  25.5 3.1 %collective-permute-done.3.recv = f32[192,128]{1,0:T(8,128)S(1)} collective-permute-done((f32[192,128]{1,0:T(8,128)S(1)}, f32[192,128]{1,0:T(8,128)S(1)}, u32[]{:S(2)}, u32[]{:S(2)}) %collective-permute-start.3) | collective-permute-done | bytes 98336 | tf_op jit(solution)/shard_map/ppermute | solution.py:425
  28.6 0.0 copy-start
  28.6 0.5 shard_map.144
  29.1 1.8 %collective-permute-start.4 = (f32[256,128]{1,0:T(8,128)S(1)}, f32[256,128]{1,0:T(8,128)S(1)}, u32[]{:S(2)}, u32[]{:S(2)}) collective-permute-start(f32[256,128]{1,0:T(8,128)S(1)} %get-tuple-element.40.own), channel_id=1, source_target_pairs={{0,4},{1,5},{2,6},{3,7},{4,0},{5,1},{6,2},{7,3},{8,12},{9,13},{10,... | collective-permute-start | bytes 393224 | tf_op jit(solution)/shard_map/ppermute | solution.py:425
  30.9 3.2 %collective-permute-done.4.recv = f32[256,128]{1,0:T(8,128)S(1)} collective-permute-done((f32[256,128]{1,0:T(8,128)S(1)}, f32[256,128]{1,0:T(8,128)S(1)}, u32[]{:S(2)}, u32[]{:S(2)}) %collective-permute-start.4) | collective-permute-done | bytes 131104 | tf_op jit(solution)/shard_map/ppermute | solution.py:425
  34.1 0.5 shard_map.145
  34.6 1.9 %collective-permute-start.5 = (f32[64,128]{1,0:T(8,128)S(1)}, f32[64,128]{1,0:T(8,128)S(1)}, u32[]{:S(2)}, u32[]{:S(2)}) collective-permute-start(f32[64,128]{1,0:T(8,128)S(1)} %get-tuple-element.46.own), channel_id=1, source_target_pairs={{0,8},{8,0},{16,24},{24,16},{1,9},{9,1},{17,25},{25,17},{2,10},{10... | collective-permute-start | bytes 98312 | tf_op jit(solution)/shard_map/ppermute | solution.py:425
  36.4 2.1 %collective-permute-done.5.recv = f32[64,128]{1,0:T(8,128)S(1)} collective-permute-done((f32[64,128]{1,0:T(8,128)S(1)}, f32[64,128]{1,0:T(8,128)S(1)}, u32[]{:S(2)}, u32[]{:S(2)}) %collective-permute-start.5) | collective-permute-done | bytes 32800 | tf_op jit(solution)/shard_map/ppermute | solution.py:425
  38.5 0.5 shard_map.148
  39.0 3.1 %collective-permute-start.6 = (f32[64,128]{1,0:T(8,128)S(1)}, f32[64,128]{1,0:T(8,128)S(1)}, u32[]{:S(2)}, u32[]{:S(2)}) collective-permute-start(f32[64,128]{1,0:T(8,128)S(1)} %get-tuple-element.48.own), channel_id=1, source_target_pairs={{0,16},{8,24},{16,0},{24,8},{1,17},{9,25},{17,1},{25,9},{2,18},{10... | collective-permute-start | bytes 98312 | tf_op jit(solution)/shard_map/ppermute | solution.py:425
  42.1 5.6 %shard_map.139 = (bf16[4096,128]{1,0:T(8,128)(2,1)S(1)}, bf16[4096,128]{1,0:T(8,128)(2,1)S(1)}) custom-call(f32[1024,128]{1,0:T(8,128)S(1)} %get-tuple-element.28.refs_0_), custom_call_target="tpu_custom_call" | custom-call | tf_op jit(solution)/shard_map/pallas_call | solution.py:502
  47.7 0.0 copy-start.6
  47.7 0.0 copy-done
  47.7 0.7 copy-done.6
  48.4 0.0 copy-start.3
  48.4 4.8 %shard_map.140 = f32[1,64,4096]{2,1,0:T(8,128)} custom-call(s32[1,2,64]{2,1,0:T(2,128)S(1)} %copy-done.6, s32[1,2,64]{2,1,0:T(2,128)S(1)} %copy-done.6, bf16[4096,128]{1,0:T(8,128)(2,1)S(1)} %get-tuple-element.29.left, bf16[4096,128]{1,0:T(8,128)(2,1)S(1)} %get-tuple-element.30.right, bf16[1,64,4096]{2,1,0:T(8,128)(2,1)S(1)} %copy-done), custom_call_target="tpu_custom_call" | custom-call | tf_op jit(solution)/shard_map/pallas_call | solution.py:512
  53.2 5.7 %shard_map.146 = (bf16[2048,128]{1,0:T(8,128)(2,1)S(1)}, bf16[2048,128]{1,0:T(8,128)(2,1)S(1)}) custom-call(f32[256,128]{1,0:T(8,128)S(1)} %get-tuple-element.42.refs_0_, f32[128,128]{1,0:T(8,128)S(1)} %get-tuple-element.43.refs_1_), custom_call_target="tpu_custom_call" | custom-call | tf_op jit(solution)/shard_map/pallas_call | solution.py:502
  58.9 0.0 copy-start.9
  58.9 0.0 copy-start.10
  58.9 0.0 copy-done.3
  58.9 0.6 copy-done.9
  59.5 0.0 copy-done.10
  59.5 2.9 %shard_map.147 = f32[1,32,4096]{2,1,0:T(8,128)} custom-call(s32[1,1,32]{2,1,0:T(1,128)S(1)} %copy-done.9, s32[1,1,32]{2,1,0:T(1,128)S(1)} %copy-done.10, bf16[2048,128]{1,0:T(8,128)(2,1)S(1)} %get-tuple-element.44.left, bf16[2048,128]{1,0:T(8,128)(2,1)S(1)} %get-tuple-element.45.right, bf16[1,32,4096]{2,1,0:T(8,128)(2,1)S(1)} %copy-done.3), custom_call_target="tpu_custom_call" | custom-call | tf_op jit(solution)/shard_map/pallas_call | solution.py:512
  62.4 0.0 collective-permute-done.6.recv
  62.5 8.2 %shard_map.150 = (f32[1,1,4096]{2,1,0:T(1,128)}, f32[1,1,4096]{2,1,0:T(1,128)}) custom-call(f32[64,128]{1,0:T(8,128)S(1)} %shard_map.149.high), custom_call_target="tpu_custom_call" | custom-call | tf_op jit(solution)/shard_map/pallas_call | solution.py:537
  (1 shorter events, 0.0 us)
Async XLA Ops:
  0.6 1.0 %copy-start.1 = (f32[1,32,4096]{2,1,0:T(8,128)S(1)}, f32[1,32,4096]{2,1,0:T(8,128)}, u32[]{:S(2)}) copy-start(f32[1,32,4096]{2,1,0:T(8,128)} %row_transfer_in.1) | copy-start | bytes 1572868
  1.7 1.0 %copy-start.2 = (f32[1,32,4096]{2,1,0:T(8,128)S(1)}, f32[1,32,4096]{2,1,0:T(8,128)}, u32[]{:S(2)}) copy-start(f32[1,32,4096]{2,1,0:T(8,128)} %col_transfer_in.1) | copy-start | bytes 1572868
  2.7 0.9 %copy-start.4 = (f32[1,16,4096]{2,1,0:T(8,128)S(1)}, f32[1,16,4096]{2,1,0:T(8,128)}, u32[]{:S(2)}) copy-start(f32[1,16,4096]{2,1,0:T(8,128)} %row_bases_in.1) | copy-start | bytes 786436
  3.7 0.9 %copy-start.5 = (f32[1,16,4096]{2,1,0:T(8,128)S(1)}, f32[1,16,4096]{2,1,0:T(8,128)}, u32[]{:S(2)}) copy-start(f32[1,16,4096]{2,1,0:T(8,128)} %col_bases_in.1) | copy-start | bytes 786436
  4.6 0.7 copy-start.7
  5.3 0.7 copy-start.8
  10.1 5.4 %collective-permute-start = (f32[128,128]{1,0:T(8,128)S(1)}, f32[128,128]{1,0:T(8,128)S(1)}, u32[]{:S(2)}, u32[]{:S(2)}) collective-permute-start(f32[128,128]{1,0:T(8,128)S(1)} %get-tuple-element.31.own), channel_id=1, source_target_pairs={{0,8},{8,0},{16,24},{24,16},{1,9},{9,1},{17,25},{25,17},{2,10},{10... | collective-permute-start | bytes 196616 | tf_op jit(solution)/shard_map/ppermute | solution.py:425
  15.9 5.3 %collective-permute-start.1 = (f32[128,128]{1,0:T(8,128)S(1)}, f32[128,128]{1,0:T(8,128)S(1)}, u32[]{:S(2)}, u32[]{:S(2)}) collective-permute-start(f32[128,128]{1,0:T(8,128)S(1)} %get-tuple-element.33.own), channel_id=1, source_target_pairs={{0,16},{8,24},{16,0},{24,8},{1,17},{9,25},{17,1},{25,9},{2,18},{10... | collective-permute-start | bytes 196616 | tf_op jit(solution)/shard_map/ppermute | solution.py:425
  21.7 1.4 %collective-permute-start.2 = (f32[192,128]{1,0:T(8,128)S(1)}, f32[192,128]{1,0:T(8,128)S(1)}, u32[]{:S(2)}, u32[]{:S(2)}) collective-permute-start(f32[192,128]{1,0:T(8,128)S(1)} %get-tuple-element.36.own), channel_id=1, source_target_pairs={{0,1},{1,0},{2,3},{3,2},{4,5},{5,4},{6,7},{7,6},{8,9},{9,8},{10,11... | collective-permute-start | bytes 294920 | tf_op jit(solution)/shard_map/ppermute | solution.py:425
  23.6 5.0 %collective-permute-start.3 = (f32[192,128]{1,0:T(8,128)S(1)}, f32[192,128]{1,0:T(8,128)S(1)}, u32[]{:S(2)}, u32[]{:S(2)}) collective-permute-start(f32[192,128]{1,0:T(8,128)S(1)} %get-tuple-element.38.own), channel_id=1, source_target_pairs={{0,2},{1,3},{2,0},{3,1},{4,6},{5,7},{6,4},{7,5},{8,10},{9,11},{10,... | collective-permute-start | bytes 294920 | tf_op jit(solution)/shard_map/ppermute | solution.py:425
  28.6 19.1 %copy-start = (bf16[1,64,4096]{2,1,0:T(8,128)(2,1)S(1)}, bf16[1,64,4096]{2,1,0:T(8,128)(2,1)}, u32[]{:S(2)}) copy-start(bf16[1,64,4096]{2,1,0:T(8,128)(2,1)} %blocks.2) | copy-start | bytes 1572868
  29.1 5.0 %collective-permute-start.4 = (f32[256,128]{1,0:T(8,128)S(1)}, f32[256,128]{1,0:T(8,128)S(1)}, u32[]{:S(2)}, u32[]{:S(2)}) collective-permute-start(f32[256,128]{1,0:T(8,128)S(1)} %get-tuple-element.40.own), channel_id=1, source_target_pairs={{0,4},{1,5},{2,6},{3,7},{4,0},{5,1},{6,2},{7,3},{8,12},{9,13},{10,... | collective-permute-start | bytes 393224 | tf_op jit(solution)/shard_map/ppermute | solution.py:425
  34.6 4.0 %collective-permute-start.5 = (f32[64,128]{1,0:T(8,128)S(1)}, f32[64,128]{1,0:T(8,128)S(1)}, u32[]{:S(2)}, u32[]{:S(2)}) collective-permute-start(f32[64,128]{1,0:T(8,128)S(1)} %get-tuple-element.46.own), channel_id=1, source_target_pairs={{0,8},{8,0},{16,24},{24,16},{1,9},{9,1},{17,25},{25,17},{2,10},{10... | collective-permute-start | bytes 98312 | tf_op jit(solution)/shard_map/ppermute | solution.py:425
  39.0 23.4 %collective-permute-start.6 = (f32[64,128]{1,0:T(8,128)S(1)}, f32[64,128]{1,0:T(8,128)S(1)}, u32[]{:S(2)}, u32[]{:S(2)}) collective-permute-start(f32[64,128]{1,0:T(8,128)S(1)} %get-tuple-element.48.own), channel_id=1, source_target_pairs={{0,16},{8,24},{16,0},{24,8},{1,17},{9,25},{17,1},{25,9},{2,18},{10... | collective-permute-start | bytes 98312 | tf_op jit(solution)/shard_map/ppermute | solution.py:425
  47.7 0.7 copy-start.6
  48.4 10.5 %copy-start.3 = (bf16[1,32,4096]{2,1,0:T(8,128)(2,1)S(1)}, bf16[1,32,4096]{2,1,0:T(8,128)(2,1)}, u32[]{:S(2)}) copy-start(bf16[1,32,4096]{2,1,0:T(8,128)(2,1)} %blocks.3) | copy-start | bytes 786436
  58.9 0.7 copy-start.9
  58.9 0.7 copy-start.10

commit v4 on v3

--- a/solution.py
+++ b/solution.py
@@ -16,6 +16,7 @@
 BF16 = jnp.bfloat16
 VMEM = pl.BlockSpec(memory_space=pltpu.VMEM)
 SMEM = pl.BlockSpec(memory_space=pltpu.SMEM)
+HBM = pl.BlockSpec(memory_space=pltpu.HBM)
 
 
 def split(x):
@@ -241,11 +242,9 @@
             roots_out[rows : 2 * rows, :] = jnp.where(upper, mine, theirs)
 
 
-def chol_lanes(a_ref, r_ref):
+def chol_lanes(a_ref, r_ref, scale_ref):
     sub = lax.broadcasted_iota(jnp.int32, (SUB, WIDE), 0)
-
-    def at(q):
-        return slice(SUB * q, SUB * (q + 1))
+    here = lax.axis_index("row") >= 0
 
     def spread(i, j):
         return r_ref[i, pl.ds(j, SUB, stride=0), :]
@@ -253,36 +252,49 @@
     def less(value, f, row):
         return lax.sub(value, lax.mul(f, row))
 
-    for p in range(NB):
-        i0 = SUB * p
-        acc = [a_ref[i0 + r, at(p), :] for r in range(SUB)]
-        scale = []
+    def reduced(p, qs):
+        acc = {(r, q): a_ref[SUB * p + r, eight(q), :] for r in range(SUB) for q in qs}
+        for k in range(SUB * p):
+            rows = [r_ref[k, eight(q), :] for q in qs]
+            for r in range(SUB):
+                f = spread(k, SUB * p + r)
+                for q, row in zip(qs, rows):
+                    acc[r, q] = less(acc[r, q], f, row)
+        return acc
+
+    def diagonal(p):
+        acc = reduced(p, [p])
         for r in range(SUB):
-            inv = lax.rsqrt(jnp.broadcast_to(acc[r][r : r + 1, :], (SUB, WIDE)))
-            scale.append(inv)
-            row = jnp.where(sub >= r, acc[r] * inv, 0.0)
-            r_ref[i0 + r, at(p), :] = row
+            inv = lax.rsqrt(jnp.broadcast_to(acc[r, p][r : r + 1, :], (SUB, WIDE)))
+            scale_ref[SUB * p + r] = inv
+            row = jnp.where(sub >= r, lax.mul(acc[r, p], inv), 0.0)
+            r_ref[SUB * p + r, eight(p), :] = row
             for r2 in range(r + 1, SUB):
-                acc[r2] = less(acc[r2], jnp.broadcast_to(row[r2 : r2 + 1, :], (SUB, WIDE)), row)
-        for q in range(p + 1, NB):
-            x = [a_ref[i0 + r, at(q), :] for r in range(SUB)]
-            for r in range(SUB):
-                x[r] = lax.mul(x[r], scale[r])
-                r_ref[i0 + r, at(q), :] = x[r]
-                for r2 in range(r + 1, SUB):
-                    x[r2] = less(x[r2], spread(i0 + r, i0 + r2), x[r])
-        for pi in range(p + 1, NB):
-            for q0 in range(pi, NB, 2):
-                qs = range(q0, min(q0 + 2, NB))
-                acc2 = {(r, q): a_ref[SUB * pi + r, at(q), :] for r in range(SUB) for q in qs}
-                for k in range(SUB):
-                    rows = {q: r_ref[i0 + k, at(q), :] for q in qs}
-                    for r in range(SUB):
-                        f = spread(i0 + k, SUB * pi + r)
-                        for q in qs:
-                            acc2[r, q] = less(acc2[r, q], f, rows[q])
-                for (r, q), value in acc2.items():
-                    a_ref[SUB * pi + r, at(q), :] = value
+                f = jnp.broadcast_to(row[r2 : r2 + 1, :], (SUB, WIDE))
+                acc[r2, p] = less(acc[r2, p], f, row)
+
+    def beyond(p, qs):
+        acc = reduced(p, qs)
+        for r in range(SUB):
+            inv = scale_ref[SUB * p + r]
+            for q in qs:
+                acc[r, q] = lax.mul(acc[r, q], inv)
+                r_ref[SUB * p + r, eight(q), :] = acc[r, q]
+            for r2 in range(r + 1, SUB):
+                f = spread(SUB * p + r, SUB * p + r2)
+                for q in qs:
+                    acc[r2, q] = less(acc[r2, q], f, acc[r, q])
+
+    for p in range(-1, NB - 1):
+
+        @pl.when(here)
+        def _():
+            if p >= 0:
+                beyond(p, [p + 1])
+            diagonal(p + 1)
+            for q in range(p + 2, NB, 2):
+                if p >= 0:
+                    beyond(p, list(range(q, min(q + 2, NB))))
 
 
 def put_row(a_ref, i, rows):
@@ -303,7 +315,7 @@
 
 def chol_table_kernel(count, shapes, *refs):
     inputs = refs[: len(shapes)]
-    left, right, a_ref, r_ref = refs[len(shapes) : len(shapes) + 4]
+    left, right, a_ref, r_ref, scale_ref = refs[len(shapes) : len(shapes) + 5]
     slots = [(ref, s) for ref in inputs for s in range(ref.shape[0] // RANK)]
     slots += [slots[-1]] * (count - len(slots))
     for q in range(NB):
@@ -319,7 +331,7 @@
             )
         for r in range(SUB):
             put_row(a_ref, SUB * q + r, jnp.concatenate([tiles[r] for tiles in groups], axis=0))
-    chol_lanes(a_ref, r_ref)
+    chol_lanes(a_ref, r_ref, scale_ref)
     keep = lane_half(2 * SUB)
     for q in range(0, NB, 2):
         rows = [get_row(r_ref, SUB * q + r, count) for r in range(2 * SUB)]
@@ -343,20 +355,40 @@
                         table[at + RANK : at + RANK + 2 * SUB, :] = low
 
 
-def final_kernel(high, row_out, col_out, a_ref, r_ref):
+def final_kernel(high, row_out, col_out, a_ref, r_ref, scale_ref):
     for i in range(RANK):
-        put_row(a_ref, i, jnp.broadcast_to(high[i : i + 1, :], (SUB, WIDE)))
-    chol_lanes(a_ref, r_ref)
-    for k in range(RANK // 2):
-        even = get_row(r_ref, 2 * k, SUB)
-        odd = get_row(r_ref, 2 * k + 1, SUB)
-        row_out[0, 0:1, lanes_of(k)] = beside(even, swapped(odd))[0:1]
-        col_out[0, 0:1, lanes_of(k)] = beside(swapped(even), odd)[0:1]
-
-
-def couple_kernel(pairs, left_of, right_of, left_pick, right_pick, left, right, blocks, out, s_ref, y_ref):
+        b0 = SUB * (i // SUB)
+        value = high[b0:RANK, :]
+        a_ref[i, b0:RANK, :] = pltpu.roll(value, WIDE - i, 1) if i else value
+    chol_lanes(a_ref, r_ref, scale_ref)
+    lane = lax.broadcasted_iota(jnp.int32, (SUB, WIDE), 1) % RANK
+    columns = []
+    for q in range(NB):
+        tile = jnp.zeros((SUB, WIDE), F32)
+        for i in range(SUB * (q + 1)):
+            value = r_ref[i, eight(q), :]
+            tile = jnp.where(lane == i, pltpu.roll(value, i, 1) if i else value, tile)
+        columns.append(tile)
+    columns = jnp.concatenate(columns, axis=0)
+    rows = jnp.concatenate([columns, columns], axis=0).T
+    for out, half in ((row_out, rows[:RANK]), (col_out, rows[RANK:])):
+        for k in range(RANK // 2):
+            out[0, 0:1, lanes_of(k)] = beside(half[2 * k : 2 * k + 1], half[2 * k + 1 : 2 * k + 2])
+
+
+def couple_kernel(
+    first_group, groups, left_of, right_of, left_pick, right_pick, left, right, blocks, *refs
+):
+    target, s_ref, y_ref, out, sem = refs[-5:]
+
+    def copy(g):
+        at = pl.ds(pl.multiple_of(g * 2 * SUB, 2 * SUB), 2 * SUB)
+        to = pl.ds(pl.multiple_of((first_group + g) * 2 * SUB, 2 * SUB), 2 * SUB)
+        return pltpu.make_async_copy(out.at[at, :], target.at[0, to, :], sem.at[g])
+
     def group(g, carry):
-        start = pl.multiple_of(g * 2 * SUB, 2 * SUB)
+        local = pl.multiple_of(g * 2 * SUB, 2 * SUB)
+        start = pl.multiple_of((first_group + g) * 2 * SUB, 2 * SUB)
 
         def slab(k):
             return blocks[0, pl.ds(start, 2 * SUB), lanes_of(k)].astype(F32)
@@ -393,13 +425,16 @@
             for k in range(SUB // 2):
                 even, odd = rows[2 * k], rows[2 * k + 1]
                 at = lanes_of(SUB // 2 * q + k)
-                out[0, pl.ds(start, SUB), at] = beside(even, swapped(odd))
-                out[0, pl.ds(pl.multiple_of(start + SUB, SUB), SUB), at] = beside(
+                out[pl.ds(local, SUB), at] = beside(even, swapped(odd))
+                out[pl.ds(pl.multiple_of(local + SUB, SUB), SUB), at] = beside(
                     swapped(even), odd
                 )
+        copy(g).start()
         return carry
 
-    lax.fori_loop(0, pairs // (2 * SUB), group, 0)
+    lax.fori_loop(0, groups, group, 0)
+    for g in range(groups):
+        copy(g).wait()
 
 
 def shape(*dims):
@@ -446,11 +481,16 @@
     leaf_gram, row_pay, col_pay, high = call(
         functools.partial(tree_kernel, count),
         [shape(count * RANK, WIDE), shape(WIDE, WIDE), shape(WIDE, WIDE), shape(RANK, WIDE)],
-        [pl.BlockSpec(memory_space=pltpu.HBM)] * 6,
+        [HBM] * 6,
         [pltpu.VMEM(x.shape, F32) for x in (row_bases, col_bases, row_transfer, col_transfer)]
         + [pltpu.SMEM(x.shape, jnp.int32) for x in (row_order, col_order)]
         + [scratch(count * RANK), scratch(2 * count * RANK), pltpu.SemaphoreType.DMA((6,))],
-    )(row_order, col_order, row_bases, col_bases, row_transfer, col_transfer)
+    )(
+        *(
+            pltpu.with_memory_space_constraint(x, pltpu.HBM)
+            for x in (row_order, col_order, row_bases, col_bases, row_transfer, col_transfer)
+        )
+    )
 
     def step(levels, pay, axis, bit, high, held=0, apart=False, extra=None):
         recv = partner(pay, axis, bit)
@@ -495,7 +535,7 @@
         high, *rest = step([("r", lc + h)], pay, "row", h, high)
         pay = rest[0] if rest else None
 
-    big = [pltpu.VMEM((RANK, RANK, WIDE), F32)] * 2
+    big = [pltpu.VMEM((RANK, RANK, WIDE), F32)] * 2 + [pltpu.VMEM((RANK, SUB, WIDE), F32)]
 
     def tables(count, *sources):
         out = jax.ShapeDtypeStruct((2 * count * WIDE, WIDE), BF16)
@@ -507,16 +547,33 @@
             limit=5 + count // 3,
         )(*sources)
 
-    def couple(left_of, right_of, left_pick, right_pick, factors, blocks):
-        pairs = blocks.shape[1]
-        return call(
-            functools.partial(couple_kernel, pairs, left_of, right_of),
-            shape(1, pairs, RANK * RANK),
-            [SMEM, SMEM, VMEM, VMEM, VMEM],
-            [scratch(SUB * RANK), scratch(SUB * RANK)],
-        )(left_pick, right_pick, *factors, blocks)
-
+    def couple(parts, left_of, right_of, left_pick, right_pick, factors, blocks):
+        result, first = [], 0
+        for groups in parts:
+            pairs = groups * 2 * SUB
+            result = [
+                pl.pallas_call(
+                    functools.partial(couple_kernel, first, groups, left_of, right_of),
+                    out_shape=shape(1, blocks.shape[1], RANK * RANK),
+                    in_specs=[SMEM, SMEM, VMEM, VMEM, VMEM] + [HBM] * len(result),
+                    out_specs=HBM,
+                    scratch_shapes=[
+                        scratch(SUB * RANK),
+                        scratch(SUB * RANK),
+                        scratch(pairs, RANK * RANK),
+                        pltpu.SemaphoreType.DMA((groups,)),
+                    ],
+                    input_output_aliases={5: 0} if result else {},
+                    compiler_params=pltpu.CompilerParams(vmem_limit_bytes=6 << 20),
+                )(left_pick, right_pick, *factors, blocks, *result)
+            ]
+            first += groups
+        return result[0]
+
+    leaf_groups = leaf_blocks.shape[1] // (2 * SUB)
+    root_groups = root_blocks.shape[1] // (2 * SUB)
     leaf_coupled = couple(
+        (leaf_groups // 2, leaf_groups - leaf_groups // 2),
         lambda ref, b: ref[0, 0, b],
         lambda ref, b: ref[0, 1, b] + count,
         leaf_pattern,
@@ -527,6 +584,7 @@
     row_slots, col_slots = nc // 2, nr // 2
     slots = -(-(row_slots + col_slots) // SUB) * SUB
     root_coupled = couple(
+        (root_groups,),
         lambda ref, b: (ref[0, 0, b] & 1) * slots + (ref[0, 0, b] >> 1),
         lambda ref, b: (ref[0, 0, b] & 1) * slots + (ref[0, 0, b] >> 1) + row_slots,
         root_rows,

time: 71 us -> 61.7 us (0.87)
  local copies, waits for them, and re-layouts: 6.6 us -> 1.32 us
  Pallas kernels: 34.2 us -> 30.3 us
    unnamed x22 -> x10, local copies, waits for them, and re-layouts: 6.6 us -> 1.32 us
    pallas_call x1, Pallas kernels: 8.23 us -> 3.33 us  [body(): call(final_kernel, [shape(1, 1, RANK * RANK), shape(1, 1, RANK * RANK)],...]
    pallas_call x1, Pallas kernels: 4.15 us -> 5.07 us  [body(): call(functools.partial(tree_kernel, count), [shape(count * RANK, WIDE), s...]
    pallas_call x2 -> x3, Pallas kernels: 7.72 us -> 8.5 us  [couple(): pl.pallas_call(functools.partial(couple_kernel, first, groups, left_of, r...]
  transfers between devices with their start and end apart: 7 -> 7, of which waited for: 6 -> 6; matrix products, arithmetic and copies ran while one was open for 0% -> 0% of each run, Pallas kernels for 27% -> 31%
where the time goes in v4:
time: 61.7 us; the launch traced here: 61.6 us
  Pallas kernels  30.3 us (49%)
  starting transfers between devices  14.9 us (24%)
  waiting for transfers between devices  14.2 us (23%)
  local copies, waits for them, and re-layouts  1.32 us (2%)
  between operations  0.8 us (1%)
    ppermute x7, starting transfers between devices, partner(): lax.ppermute(value, axis, [(i, i ^ 1 << bit) for i in range(lax.axis_size...  14.9 us
    ppermute x7, waiting for transfers between devices, partner(): lax.ppermute(value, axis, [(i, i ^ 1 << bit) for i in range(lax.axis_size...  14.2 us
    pallas_call x2, Pallas kernels, tables(): call(functools.partial(chol_table_kernel, count, [x.shape for x in source...  10.6 us
    pallas_call x3, Pallas kernels, couple(): pl.pallas_call(functools.partial(couple_kernel, first, groups, left_of, r...  8.5 us
    pallas_call x1, Pallas kernels, body(): call(functools.partial(tree_kernel, count), [shape(count * RANK, WIDE), s...  5.07 us
    pallas_call x1, Pallas kernels, body(): call(final_kernel, [shape(1, 1, RANK * RANK), shape(1, 1, RANK * RANK)],...  3.33 us
    pallas_call x7, Pallas kernels, step(): call(functools.partial(step_kernel, levels, top, (nr, nc), held, apart, e...  2.8 us
    unnamed x10, local copies, waits for them, and re-layouts  1.32 us
  transfers between devices with their start and end apart: 7, of which 6 were waited for; matrix products, arithmetic and copies ran while one was open for 0% of the time, Pallas kernels for 31%

profile of v4, /device:TPU:0, one launch (start us, length us, event | category | flops | bytes accessed | tf_op | source)
XLA Modules:
  0.0 61.6 jit_solution(17119095406594653028)
XLA Ops:
  0.6 5.1 %shard_map.138 = (f32[1024,128]{1,0:T(8,128)S(1)}, f32[128,128]{1,0:T(8,128)S(1)}, f32[128,128]{1,0:T(8,128)S(1)}, f32[64,128]{1,0:T(8,128)S(1)}) custom-call(s32[1,1,16]{2,1,0:T(1,128)} %row_order_in.1, s32[1,1,16]{2,1,0:T(1,128)} %col_order_in.1, f32[1,16,4096]{2,1,0:T(8,128)} %row_bases_in.1, f32[1,16,4096]{2,1,0:T(8,128)} %col_bases_in.1, ...), custom_call_target="tpu_custom_call" | custom-call | tf_op jit(solution)/shard_map/pallas_call | solution.py:481
  5.7 3.1 %collective-permute-start = (f32[128,128]{1,0:T(8,128)S(1)}, f32[128,128]{1,0:T(8,128)S(1)}, u32[]{:S(2)}, u32[]{:S(2)}) collective-permute-start(f32[128,128]{1,0:T(8,128)S(1)} %get-tuple-element.31.own), channel_id=1, source_target_pairs={{0,8},{8,0},{16,24},{24,16},{1,9},{9,1},{17,25},{25,17},{2,10},{10... | collective-permute-start | bytes 196616 | tf_op jit(solution)/shard_map/ppermute | solution.py:460
  8.8 2.2 %collective-permute-done.recv = f32[128,128]{1,0:T(8,128)S(1)} collective-permute-done((f32[128,128]{1,0:T(8,128)S(1)}, f32[128,128]{1,0:T(8,128)S(1)}, u32[]{:S(2)}, u32[]{:S(2)}) %collective-permute-start) | collective-permute-done | bytes 65568 | tf_op jit(solution)/shard_map/ppermute | solution.py:460
  11.1 0.5 shard_map.142
  11.5 3.1 %collective-permute-start.1 = (f32[128,128]{1,0:T(8,128)S(1)}, f32[128,128]{1,0:T(8,128)S(1)}, u32[]{:S(2)}, u32[]{:S(2)}) collective-permute-start(f32[128,128]{1,0:T(8,128)S(1)} %get-tuple-element.33.own), channel_id=1, source_target_pairs={{0,16},{8,24},{16,0},{24,8},{1,17},{9,25},{17,1},{25,9},{2,18},{10... | collective-permute-start | bytes 196616 | tf_op jit(solution)/shard_map/ppermute | solution.py:460
  14.6 2.2 %collective-permute-done.1.recv = f32[128,128]{1,0:T(8,128)S(1)} collective-permute-done((f32[128,128]{1,0:T(8,128)S(1)}, f32[128,128]{1,0:T(8,128)S(1)}, u32[]{:S(2)}, u32[]{:S(2)}) %collective-permute-start.1) | collective-permute-done | bytes 65568 | tf_op jit(solution)/shard_map/ppermute | solution.py:460
  16.9 0.5 shard_map.143
  17.3 0.1 collective-permute-start.2
  17.4 1.3 %collective-permute-done.2.recv = f32[192,128]{1,0:T(8,128)S(1)} collective-permute-done((f32[192,128]{1,0:T(8,128)S(1)}, f32[192,128]{1,0:T(8,128)S(1)}, u32[]{:S(2)}, u32[]{:S(2)}) %collective-permute-start.2) | collective-permute-done | bytes 98336 | tf_op jit(solution)/shard_map/ppermute | solution.py:460
  18.7 0.5 shard_map.144
  19.2 1.9 %collective-permute-start.3 = (f32[192,128]{1,0:T(8,128)S(1)}, f32[192,128]{1,0:T(8,128)S(1)}, u32[]{:S(2)}, u32[]{:S(2)}) collective-permute-start(f32[192,128]{1,0:T(8,128)S(1)} %get-tuple-element.38.own), channel_id=1, source_target_pairs={{0,2},{1,3},{2,0},{3,1},{4,6},{5,7},{6,4},{7,5},{8,10},{9,11},{10,... | collective-permute-start | bytes 294920 | tf_op jit(solution)/shard_map/ppermute | solution.py:460
  21.1 3.1 %collective-permute-done.3.recv = f32[192,128]{1,0:T(8,128)S(1)} collective-permute-done((f32[192,128]{1,0:T(8,128)S(1)}, f32[192,128]{1,0:T(8,128)S(1)}, u32[]{:S(2)}, u32[]{:S(2)}) %collective-permute-start.3) | collective-permute-done | bytes 98336 | tf_op jit(solution)/shard_map/ppermute | solution.py:460
  24.2 0.0 copy-start
  24.2 0.5 shard_map.145
  24.7 1.8 %collective-permute-start.4 = (f32[256,128]{1,0:T(8,128)S(1)}, f32[256,128]{1,0:T(8,128)S(1)}, u32[]{:S(2)}, u32[]{:S(2)}) collective-permute-start(f32[256,128]{1,0:T(8,128)S(1)} %get-tuple-element.40.own), channel_id=1, source_target_pairs={{0,4},{1,5},{2,6},{3,7},{4,0},{5,1},{6,2},{7,3},{8,12},{9,13},{10,... | collective-permute-start | bytes 393224 | tf_op jit(solution)/shard_map/ppermute | solution.py:460
  26.5 3.2 %collective-permute-done.4.recv = f32[256,128]{1,0:T(8,128)S(1)} collective-permute-done((f32[256,128]{1,0:T(8,128)S(1)}, f32[256,128]{1,0:T(8,128)S(1)}, u32[]{:S(2)}, u32[]{:S(2)}) %collective-permute-start.4) | collective-permute-done | bytes 131104 | tf_op jit(solution)/shard_map/ppermute | solution.py:460
  29.7 0.5 shard_map.146
  30.2 1.9 %collective-permute-start.5 = (f32[64,128]{1,0:T(8,128)S(1)}, f32[64,128]{1,0:T(8,128)S(1)}, u32[]{:S(2)}, u32[]{:S(2)}) collective-permute-start(f32[64,128]{1,0:T(8,128)S(1)} %get-tuple-element.46.own), channel_id=1, source_target_pairs={{0,8},{8,0},{16,24},{24,16},{1,9},{9,1},{17,25},{25,17},{2,10},{10... | collective-permute-start | bytes 98312 | tf_op jit(solution)/shard_map/ppermute | solution.py:460
  32.1 2.1 %collective-permute-done.5.recv = f32[64,128]{1,0:T(8,128)S(1)} collective-permute-done((f32[64,128]{1,0:T(8,128)S(1)}, f32[64,128]{1,0:T(8,128)S(1)}, u32[]{:S(2)}, u32[]{:S(2)}) %collective-permute-start.5) | collective-permute-done | bytes 32800 | tf_op jit(solution)/shard_map/ppermute | solution.py:460
  34.2 0.5 shard_map.149
  34.6 3.1 %collective-permute-start.6 = (f32[64,128]{1,0:T(8,128)S(1)}, f32[64,128]{1,0:T(8,128)S(1)}, u32[]{:S(2)}, u32[]{:S(2)}) collective-permute-start(f32[64,128]{1,0:T(8,128)S(1)} %get-tuple-element.48.own), channel_id=1, source_target_pairs={{0,16},{8,24},{16,0},{24,8},{1,17},{9,25},{17,1},{25,9},{2,18},{10... | collective-permute-start | bytes 98312 | tf_op jit(solution)/shard_map/ppermute | solution.py:460
  37.7 5.3 %shard_map.139 = (bf16[4096,128]{1,0:T(8,128)(2,1)S(1)}, bf16[4096,128]{1,0:T(8,128)(2,1)S(1)}) custom-call(f32[1024,128]{1,0:T(8,128)S(1)} %get-tuple-element.28.refs_0_), custom_call_target="tpu_custom_call" | custom-call | tf_op jit(solution)/shard_map/pallas_call | solution.py:542
  43.0 0.0 copy-start.2
  43.0 0.0 copy-done
  43.0 0.7 %copy-done.2 = s32[1,2,64]{2,1,0:T(2,128)S(1)} copy-done((s32[1,2,64]{2,1,0:T(2,128)S(1)}, s32[1,2,64]{2,1,0:T(2,128)}, u32[]{:S(2)}) %copy-start.2) | copy-done | bytes 536
  43.7 2.8 %shard_map.140.refs_0_ = f32[1,64,4096]{2,1,0:T(8,128)} custom-call(s32[1,2,64]{2,1,0:T(2,128)S(1)} %copy-done.2, s32[1,2,64]{2,1,0:T(2,128)S(1)} %copy-done.2, bf16[4096,128]{1,0:T(8,128)(2,1)S(1)} %get-tuple-element.29.left, bf16[4096,128]{1,0:T(8,128)(2,1)S(1)} %get-tuple-element.30.right, bf16[1,64,4096]{2,1,0:T(8,128)(2,1)S(1)} %copy-done), custom_call_target="tpu_custom_call" | custom-call | tf_op jit(solution)/shard_map/pallas_call | solution.py:555
  46.5 0.0 copy-start.1
  46.5 2.8 %shard_map.141 = f32[1,64,4096]{2,1,0:T(8,128)} custom-call(s32[1,2,64]{2,1,0:T(2,128)S(1)} %copy-done.2, s32[1,2,64]{2,1,0:T(2,128)S(1)} %copy-done.2, bf16[4096,128]{1,0:T(8,128)(2,1)S(1)} %get-tuple-element.29.left, bf16[4096,128]{1,0:T(8,128)(2,1)S(1)} %get-tuple-element.30.right, ...), custom_call_target="tpu_custom_call", output_to_operand_aliasing={{}: (5, {})} | custom-call | tf_op jit(solution)/shard_map/pallas_call | solution.py:555
  49.4 5.3 %shard_map.147 = (bf16[2048,128]{1,0:T(8,128)(2,1)S(1)}, bf16[2048,128]{1,0:T(8,128)(2,1)S(1)}) custom-call(f32[256,128]{1,0:T(8,128)S(1)} %get-tuple-element.42.refs_0_, f32[128,128]{1,0:T(8,128)S(1)} %get-tuple-element.43.refs_1_), custom_call_target="tpu_custom_call" | custom-call | tf_op jit(solution)/shard_map/pallas_call | solution.py:542
  54.7 0.0 copy-start.3
  54.7 0.0 copy-start.4
  54.7 0.0 copy-done.1
  54.7 0.6 %copy-done.3 = s32[1,1,32]{2,1,0:T(1,128)S(1)} copy-done((s32[1,1,32]{2,1,0:T(1,128)S(1)}, s32[1,1,32]{2,1,0:T(1,128)}, u32[]{:S(2)}) %copy-start.3) | copy-done | bytes 152
  55.3 0.0 copy-done.4
  55.4 2.8 %shard_map.148 = f32[1,32,4096]{2,1,0:T(8,128)} custom-call(s32[1,1,32]{2,1,0:T(1,128)S(1)} %copy-done.3, s32[1,1,32]{2,1,0:T(1,128)S(1)} %copy-done.4, bf16[2048,128]{1,0:T(8,128)(2,1)S(1)} %get-tuple-element.44.left, bf16[2048,128]{1,0:T(8,128)(2,1)S(1)} %get-tuple-element.45.right, bf16[1,32,4096]{2,1,0:T(8,128)(2,1)S(1)} %copy-done.1), custom_call_target="tpu_custom_call" | custom-call | tf_op jit(solution)/shard_map/pallas_call | solution.py:555
  58.2 0.0 collective-permute-done.6.recv
  58.2 3.3 %shard_map.151 = (f32[1,1,4096]{2,1,0:T(1,128)}, f32[1,1,4096]{2,1,0:T(1,128)}) custom-call(f32[64,128]{1,0:T(8,128)S(1)} %shard_map.150.high), custom_call_target="tpu_custom_call" | custom-call | tf_op jit(solution)/shard_map/pallas_call | solution.py:595
  (1 shorter events, 0.0 us)
Async XLA Ops:
  5.7 5.4 %collective-permute-start = (f32[128,128]{1,0:T(8,128)S(1)}, f32[128,128]{1,0:T(8,128)S(1)}, u32[]{:S(2)}, u32[]{:S(2)}) collective-permute-start(f32[128,128]{1,0:T(8,128)S(1)} %get-tuple-element.31.own), channel_id=1, source_target_pairs={{0,8},{8,0},{16,24},{24,16},{1,9},{9,1},{17,25},{25,17},{2,10},{10... | collective-permute-start | bytes 196616 | tf_op jit(solution)/shard_map/ppermute | solution.py:460
  11.5 5.3 %collective-permute-start.1 = (f32[128,128]{1,0:T(8,128)S(1)}, f32[128,128]{1,0:T(8,128)S(1)}, u32[]{:S(2)}, u32[]{:S(2)}) collective-permute-start(f32[128,128]{1,0:T(8,128)S(1)} %get-tuple-element.33.own), channel_id=1, source_target_pairs={{0,16},{8,24},{16,0},{24,8},{1,17},{9,25},{17,1},{25,9},{2,18},{10... | collective-permute-start | bytes 196616 | tf_op jit(solution)/shard_map/ppermute | solution.py:460
  17.3 1.4 %collective-permute-start.2 = (f32[192,128]{1,0:T(8,128)S(1)}, f32[192,128]{1,0:T(8,128)S(1)}, u32[]{:S(2)}, u32[]{:S(2)}) collective-permute-start(f32[192,128]{1,0:T(8,128)S(1)} %get-tuple-element.36.own), channel_id=1, source_target_pairs={{0,1},{1,0},{2,3},{3,2},{4,5},{5,4},{6,7},{7,6},{8,9},{9,8},{10,11... | collective-permute-start | bytes 294920 | tf_op jit(solution)/shard_map/ppermute | solution.py:460
  19.2 5.0 %collective-permute-start.3 = (f32[192,128]{1,0:T(8,128)S(1)}, f32[192,128]{1,0:T(8,128)S(1)}, u32[]{:S(2)}, u32[]{:S(2)}) collective-permute-start(f32[192,128]{1,0:T(8,128)S(1)} %get-tuple-element.38.own), channel_id=1, source_target_pairs={{0,2},{1,3},{2,0},{3,1},{4,6},{5,7},{6,4},{7,5},{8,10},{9,11},{10,... | collective-permute-start | bytes 294920 | tf_op jit(solution)/shard_map/ppermute | solution.py:460
  24.2 18.8 %copy-start = (bf16[1,64,4096]{2,1,0:T(8,128)(2,1)S(1)}, bf16[1,64,4096]{2,1,0:T(8,128)(2,1)}, u32[]{:S(2)}) copy-start(bf16[1,64,4096]{2,1,0:T(8,128)(2,1)} %blocks.4) | copy-start | bytes 1572868
  24.7 5.0 %collective-permute-start.4 = (f32[256,128]{1,0:T(8,128)S(1)}, f32[256,128]{1,0:T(8,128)S(1)}, u32[]{:S(2)}, u32[]{:S(2)}) collective-permute-start(f32[256,128]{1,0:T(8,128)S(1)} %get-tuple-element.40.own), channel_id=1, source_target_pairs={{0,4},{1,5},{2,6},{3,7},{4,0},{5,1},{6,2},{7,3},{8,12},{9,13},{10,... | collective-permute-start | bytes 393224 | tf_op jit(solution)/shard_map/ppermute | solution.py:460
  30.2 4.0 %collective-permute-start.5 = (f32[64,128]{1,0:T(8,128)S(1)}, f32[64,128]{1,0:T(8,128)S(1)}, u32[]{:S(2)}, u32[]{:S(2)}) collective-permute-start(f32[64,128]{1,0:T(8,128)S(1)} %get-tuple-element.46.own), channel_id=1, source_target_pairs={{0,8},{8,0},{16,24},{24,16},{1,9},{9,1},{17,25},{25,17},{2,10},{10... | collective-permute-start | bytes 98312 | tf_op jit(solution)/shard_map/ppermute | solution.py:460
  34.6 23.6 %collective-permute-start.6 = (f32[64,128]{1,0:T(8,128)S(1)}, f32[64,128]{1,0:T(8,128)S(1)}, u32[]{:S(2)}, u32[]{:S(2)}) collective-permute-start(f32[64,128]{1,0:T(8,128)S(1)} %get-tuple-element.48.own), channel_id=1, source_target_pairs={{0,16},{8,24},{16,0},{24,8},{1,17},{9,25},{17,1},{25,9},{2,18},{10... | collective-permute-start | bytes 98312 | tf_op jit(solution)/shard_map/ppermute | solution.py:460
  43.0 0.7 %copy-start.2 = (s32[1,2,64]{2,1,0:T(2,128)S(1)}, s32[1,2,64]{2,1,0:T(2,128)}, u32[]{:S(2)}) copy-start(s32[1,2,64]{2,1,0:T(2,128)} %right_pick.4) | copy-start | bytes 1540
  46.5 8.2 %copy-start.1 = (bf16[1,32,4096]{2,1,0:T(8,128)(2,1)S(1)}, bf16[1,32,4096]{2,1,0:T(8,128)(2,1)}, u32[]{:S(2)}) copy-start(bf16[1,32,4096]{2,1,0:T(8,128)(2,1)} %blocks.5) | copy-start | bytes 786436
  54.7 0.7 %copy-start.3 = (s32[1,1,32]{2,1,0:T(1,128)S(1)}, s32[1,1,32]{2,1,0:T(1,128)}, u32[]{:S(2)}) copy-start(s32[1,1,32]{2,1,0:T(1,128)} %left_pick.5) | copy-start | bytes 388
  54.7 0.7 %copy-start.4 = (s32[1,1,32]{2,1,0:T(1,128)S(1)}, s32[1,1,32]{2,1,0:T(1,128)}, u32[]{:S(2)}) copy-start(s32[1,1,32]{2,1,0:T(1,128)} %right_pick.5) | copy-start | bytes 388

commit v5 on v4

--- a/solution.py
+++ b/solution.py
@@ -117,20 +117,22 @@
     col_bases_in,
     row_transfer_in,
     col_transfer_in,
-    leaf_gram,
-    row_pay,
-    col_pay,
-    high,
-    row_bases,
-    col_bases,
-    row_transfer,
-    col_transfer,
-    row_order,
-    col_order,
-    basis,
-    trans,
-    sems,
+    *refs,
 ):
+    picks_in, refs = refs[:3], refs[3:]
+    leaf_gram, row_pay, col_pay, high = refs[:4]
+    picks, refs = refs[4:7], refs[7:]
+    (
+        row_bases,
+        col_bases,
+        row_transfer,
+        col_transfer,
+        row_order,
+        col_order,
+        basis,
+        trans,
+        sems,
+    ) = refs
     copies = [
         pltpu.make_async_copy(source, target, sems.at[n])
         for n, (source, target) in enumerate(
@@ -141,6 +143,7 @@
                 (col_transfer_in, col_transfer),
                 (row_order_in, row_order),
                 (col_order_in, col_order),
+                *zip(picks_in, picks),
             )
         )
     ]
@@ -154,7 +157,7 @@
         leaf_gram[leaf * RANK : (leaf + 1) * RANK, :] = dot_both(
             jnp.concatenate([u, u], axis=0).T, u
         )
-    for copy in copies[2:]:
+    for copy in copies[2:6]:
         copy.wait()
     unpack_trees(row_transfer, col_transfer, trans, 2 * count)
     nodes = []
@@ -185,6 +188,8 @@
     row_pay[RANK:WIDE, :] = gram
     col_pay[0:RANK, :] = beside(swapped(term), first)
     col_pay[RANK:WIDE, :] = swapped(gram)
+    for copy in copies[6:]:
+        copy.wait()
 
 
 def step_kernel(levels, top, sizes, held, apart, extra, own, recv, high_in, *refs):
@@ -297,54 +302,61 @@
                     beyond(p, list(range(q, min(q + 2, NB))))
 
 
-def put_row(a_ref, i, rows):
-    b0 = SUB * (i // SUB)
-    t = rows.T
-    a_ref[i, b0:RANK, 0 : 2 * rows.shape[0]] = jnp.concatenate([t[b0:RANK], t[RANK + b0 :]], axis=1)
-
-
-def get_row(r_ref, i, count):
-    b0 = SUB * (i // SUB)
-    parts = []
+CELL = WIDE // SUB
+
+
+def load_slots(slots, a_ref):
+    cell = lax.broadcasted_iota(jnp.int32, (RANK, WIDE), 1) % SUB
+    for q in range(NB):
+        b0 = SUB * q
+        turned = []
+        for g in range(0, len(slots), CELL):
+            group = slots[g : g + CELL]
+            group = group + [group[-1]] * (CELL - len(group))
+            tiles = [ref[s * RANK + b0 : s * RANK + b0 + SUB, :] for ref, s in group]
+            t = jnp.concatenate(tiles, axis=0).T
+            turned += [t[b0:RANK], t[RANK + b0 :]]
+        for r in range(SUB):
+            value = None
+            for offset, t in enumerate(turned):
+                t = pltpu.roll(t, (offset - r) % WIDE, 1) if offset != r else t
+                value = t if value is None else jnp.where(cell[b0:] == offset, t, value)
+            a_ref[b0 + r, b0:RANK, :] = value
+
+
+def factor_tiles(r_ref, q, group):
+    cell = lax.broadcasted_iota(jnp.int32, (SUB, WIDE), 1) % SUB
+    columns = []
     for half in range(2):
-        if b0:
-            parts.append(jnp.zeros((b0, count), F32))
-        parts.append(r_ref[i, b0:RANK, half * count : (half + 1) * count])
-    return jnp.concatenate(parts, axis=0).T
-
-
-def chol_table_kernel(count, shapes, *refs):
-    inputs = refs[: len(shapes)]
-    left, right, a_ref, r_ref, scale_ref = refs[len(shapes) : len(shapes) + 5]
+        offset = 2 * group + half
+        for p in range(NB):
+            tile = jnp.zeros((SUB, WIDE), F32)
+            for r in range(SUB if p >= q else 0):
+                v = r_ref[SUB * q + r, eight(p), :]
+                v = pltpu.roll(v, (r - offset) % WIDE, 1) if offset != r else v
+                tile = jnp.where(cell == r, v, tile)
+            columns.append(tile)
+    return jnp.concatenate(columns, axis=0).T
+
+
+def chol_kernel(*refs):
+    *inputs, r_ref, a_ref, scale_ref = refs
     slots = [(ref, s) for ref in inputs for s in range(ref.shape[0] // RANK)]
-    slots += [slots[-1]] * (count - len(slots))
-    for q in range(NB):
-        groups = []
-        for g in range(count // SUB):
-            groups.append(
-                swap8(
-                    [
-                        ref[s * RANK + SUB * q : s * RANK + SUB * (q + 1), :]
-                        for ref, s in slots[SUB * g : SUB * (g + 1)]
-                    ]
-                )
-            )
-        for r in range(SUB):
-            put_row(a_ref, SUB * q + r, jnp.concatenate([tiles[r] for tiles in groups], axis=0))
+    load_slots(slots, a_ref)
     chol_lanes(a_ref, r_ref, scale_ref)
+
+
+def table_kernel(count, r_ref, left, right):
     keep = lane_half(2 * SUB)
     for q in range(0, NB, 2):
-        rows = [get_row(r_ref, SUB * q + r, count) for r in range(2 * SUB)]
-        for g in range(count // SUB):
-            upper = swap8([row[eight(g)] for row in rows[:SUB]])
-            lower = swap8([row[eight(g)] for row in rows[SUB:]])
-            for b in range(SUB):
-                both = jnp.concatenate([upper[b], lower[b]], axis=0)
+        for g in range(-(-count // CELL)):
+            upper = factor_tiles(r_ref, q, g)
+            lower = factor_tiles(r_ref, q + 1, g)
+            for b in range(min(CELL, count - CELL * g)):
+                both = jnp.concatenate([upper[eight(b)], lower[eight(b)]], axis=0)
                 other = swapped(both)
-                for n, here, there in (
-                    (SUB * g + b, both, other),
-                    (count + SUB * g + b, other, both),
-                ):
+                s = CELL * g + b
+                for n, here, there in ((s, both, other), (count + s, other, both)):
                     at = n * WIDE + SUB * q
                     for table, value in (
                         (left, jnp.where(keep, here, 0.0)),
@@ -478,17 +490,28 @@
     lr, lc = nr.bit_length() - 1, nc.bit_length() - 1
     top = lr + lc - 1
 
-    leaf_gram, row_pay, col_pay, high = call(
+    leaf_gram, row_pay, col_pay, high, leaf_pattern, root_rows, root_cols = call(
         functools.partial(tree_kernel, count),
-        [shape(count * RANK, WIDE), shape(WIDE, WIDE), shape(WIDE, WIDE), shape(RANK, WIDE)],
-        [HBM] * 6,
+        [shape(count * RANK, WIDE), shape(WIDE, WIDE), shape(WIDE, WIDE), shape(RANK, WIDE)]
+        + [jax.ShapeDtypeStruct(x.shape, x.dtype) for x in (leaf_pattern, root_rows, root_cols)],
+        [HBM] * 9,
         [pltpu.VMEM(x.shape, F32) for x in (row_bases, col_bases, row_transfer, col_transfer)]
         + [pltpu.SMEM(x.shape, jnp.int32) for x in (row_order, col_order)]
-        + [scratch(count * RANK), scratch(2 * count * RANK), pltpu.SemaphoreType.DMA((6,))],
+        + [scratch(count * RANK), scratch(2 * count * RANK), pltpu.SemaphoreType.DMA((9,))],
     )(
         *(
             pltpu.with_memory_space_constraint(x, pltpu.HBM)
-            for x in (row_order, col_order, row_bases, col_bases, row_transfer, col_transfer)
+            for x in (
+                row_order,
+                col_order,
+                row_bases,
+                col_bases,
+                row_transfer,
+                col_transfer,
+                leaf_pattern,
+                root_rows,
+                root_cols,
+            )
         )
     )
 
@@ -538,14 +561,13 @@
     big = [pltpu.VMEM((RANK, RANK, WIDE), F32)] * 2 + [pltpu.VMEM((RANK, SUB, WIDE), F32)]
 
     def tables(count, *sources):
+        factors = call(
+            chol_kernel, shape(RANK, RANK, WIDE), [VMEM] * len(sources), big[1:]
+        )(*sources)
         out = jax.ShapeDtypeStruct((2 * count * WIDE, WIDE), BF16)
         return call(
-            functools.partial(chol_table_kernel, count, [x.shape for x in sources]),
-            [out, out],
-            [VMEM] * len(sources),
-            big,
-            limit=5 + count // 3,
-        )(*sources)
+            functools.partial(table_kernel, count), [out, out], [VMEM], limit=5 + count // 4
+        )(factors)
 
     def couple(parts, left_of, right_of, left_pick, right_pick, factors, blocks):
         result, first = [], 0
@@ -582,7 +604,7 @@
         leaf_blocks,
     )
     row_slots, col_slots = nc // 2, nr // 2
-    slots = -(-(row_slots + col_slots) // SUB) * SUB
+    slots = row_slots + col_slots
     root_coupled = couple(
         (root_groups,),
         lambda ref, b: (ref[0, 0, b] & 1) * slots + (ref[0, 0, b] >> 1),

time: 61.7 us -> 58 us (0.940)
  Pallas kernels: 30.3 us -> 27.9 us
  local copies, waits for them, and re-layouts: 1.32 us -> 0.01 us
    pallas_call x2 -> x4, Pallas kernels: 10.6 us -> 8.16 us  [the longest x2 5.5 us: tables(): call(chol_kernel, shape(RANK, RANK, WIDE), [VMEM] * len(sources), big[1:])]
    unnamed x10 -> x4, local copies, waits for them, and re-layouts: 1.32 us -> 0.01 us
  transfers between devices with their start and end apart: 7 -> 7, of which waited for: 6 -> 6; matrix products, arithmetic and copies ran while one was open for 0% -> 0% of each run, Pallas kernels for 31% -> 29%
where the time goes in v5:
time: 58 us; the launch traced here: 57.8 us
  Pallas kernels  27.9 us (48%)
  starting transfers between devices  14.9 us (26%)
  waiting for transfers between devices  14.2 us (24%)
  between operations  0.8 us (1%)
    ppermute x7, starting transfers between devices, partner(): lax.ppermute(value, axis, [(i, i ^ 1 << bit) for i in range(lax.axis_size...  14.9 us
    ppermute x7, waiting for transfers between devices, partner(): lax.ppermute(value, axis, [(i, i ^ 1 << bit) for i in range(lax.axis_size...  14.2 us
    pallas_call x3, Pallas kernels, couple(): pl.pallas_call(functools.partial(couple_kernel, first, groups, left_of, r...  8.49 us
    pallas_call x2, Pallas kernels, tables(): call(chol_kernel, shape(RANK, RANK, WIDE), [VMEM] * len(sources), big[1:])  5.5 us
    pallas_call x1, Pallas kernels, body(): call(functools.partial(tree_kernel, count), [shape(count * RANK, WIDE), s...  5.1 us
    pallas_call x1, Pallas kernels, body(): call(final_kernel, [shape(1, 1, RANK * RANK), shape(1, 1, RANK * RANK)],...  3.33 us
    pallas_call x7, Pallas kernels, step(): call(functools.partial(step_kernel, levels, top, (nr, nc), held, apart, e...  2.8 us
    pallas_call x2, Pallas kernels, tables(): call(functools.partial(table_kernel, count), [out, out], [VMEM], limit=5...  2.66 us
  transfers between devices with their start and end apart: 7, of which 6 were waited for; matrix products, arithmetic and copies ran while one was open for 0% of the time, Pallas kernels for 29%

profile of v5, /device:TPU:0, one launch (start us, length us, event | category | flops | bytes accessed | tf_op | source)
XLA Modules:
  0.0 57.8 jit_solution(14309931220737050872)
XLA Ops:
  0.6 5.1 %shard_map.138 = (f32[1024,128]{1,0:T(8,128)S(1)}, f32[128,128]{1,0:T(8,128)S(1)}, f32[128,128]{1,0:T(8,128)S(1)}, f32[64,128]{1,0:T(8,128)S(1)}, s32[1,2,64]{2,...) custom-call(s32[1,1,16]{2,1,0:T(1,128)} %row_order_in.1, s32[1,1,16]{2,1,0:T(1,128)} %col_order_in.1, ...), custom_call_target="tpu_custom_call" | custom-call | tf_op jit(solution)/shard_map/pallas_call | solution.py:493
  5.7 3.1 %collective-permute-start = (f32[128,128]{1,0:T(8,128)S(1)}, f32[128,128]{1,0:T(8,128)S(1)}, u32[]{:S(2)}, u32[]{:S(2)}) collective-permute-start(f32[128,128]{1,0:T(8,128)S(1)} %get-tuple-element.37.own), channel_id=1, source_target_pairs={{0,8},{8,0},{16,24},{24,16},{1,9},{9,1},{17,25},{25,17},{2,10},{10... | collective-permute-start | bytes 196616 | tf_op jit(solution)/shard_map/ppermute | solution.py:472
  8.9 2.2 %collective-permute-done.recv = f32[128,128]{1,0:T(8,128)S(1)} collective-permute-done((f32[128,128]{1,0:T(8,128)S(1)}, f32[128,128]{1,0:T(8,128)S(1)}, u32[]{:S(2)}, u32[]{:S(2)}) %collective-permute-start) | collective-permute-done | bytes 65568 | tf_op jit(solution)/shard_map/ppermute | solution.py:472
  11.1 0.5 shard_map.143
  11.6 3.1 %collective-permute-start.1 = (f32[128,128]{1,0:T(8,128)S(1)}, f32[128,128]{1,0:T(8,128)S(1)}, u32[]{:S(2)}, u32[]{:S(2)}) collective-permute-start(f32[128,128]{1,0:T(8,128)S(1)} %get-tuple-element.39.own), channel_id=1, source_target_pairs={{0,16},{8,24},{16,0},{24,8},{1,17},{9,25},{17,1},{25,9},{2,18},{10... | collective-permute-start | bytes 196616 | tf_op jit(solution)/shard_map/ppermute | solution.py:472
  14.7 2.2 %collective-permute-done.1.recv = f32[128,128]{1,0:T(8,128)S(1)} collective-permute-done((f32[128,128]{1,0:T(8,128)S(1)}, f32[128,128]{1,0:T(8,128)S(1)}, u32[]{:S(2)}, u32[]{:S(2)}) %collective-permute-start.1) | collective-permute-done | bytes 65568 | tf_op jit(solution)/shard_map/ppermute | solution.py:472
  16.9 0.5 shard_map.144
  17.4 0.1 collective-permute-start.2
  17.4 1.3 %collective-permute-done.2.recv = f32[192,128]{1,0:T(8,128)S(1)} collective-permute-done((f32[192,128]{1,0:T(8,128)S(1)}, f32[192,128]{1,0:T(8,128)S(1)}, u32[]{:S(2)}, u32[]{:S(2)}) %collective-permute-start.2) | collective-permute-done | bytes 98336 | tf_op jit(solution)/shard_map/ppermute | solution.py:472
  18.7 0.5 shard_map.145
  19.2 1.9 %collective-permute-start.3 = (f32[192,128]{1,0:T(8,128)S(1)}, f32[192,128]{1,0:T(8,128)S(1)}, u32[]{:S(2)}, u32[]{:S(2)}) collective-permute-start(f32[192,128]{1,0:T(8,128)S(1)} %get-tuple-element.44.own), channel_id=1, source_target_pairs={{0,2},{1,3},{2,0},{3,1},{4,6},{5,7},{6,4},{7,5},{8,10},{9,11},{10,... | collective-permute-start | bytes 294920 | tf_op jit(solution)/shard_map/ppermute | solution.py:472
  21.1 3.1 %collective-permute-done.3.recv = f32[192,128]{1,0:T(8,128)S(1)} collective-permute-done((f32[192,128]{1,0:T(8,128)S(1)}, f32[192,128]{1,0:T(8,128)S(1)}, u32[]{:S(2)}, u32[]{:S(2)}) %collective-permute-start.3) | collective-permute-done | bytes 98336 | tf_op jit(solution)/shard_map/ppermute | solution.py:472
  24.2 0.5 shard_map.146
  24.7 1.8 %collective-permute-start.4 = (f32[256,128]{1,0:T(8,128)S(1)}, f32[256,128]{1,0:T(8,128)S(1)}, u32[]{:S(2)}, u32[]{:S(2)}) collective-permute-start(f32[256,128]{1,0:T(8,128)S(1)} %get-tuple-element.46.own), channel_id=1, source_target_pairs={{0,4},{1,5},{2,6},{3,7},{4,0},{5,1},{6,2},{7,3},{8,12},{9,13},{10,... | collective-permute-start | bytes 393224 | tf_op jit(solution)/shard_map/ppermute | solution.py:472
  26.5 3.2 %collective-permute-done.4.recv = f32[256,128]{1,0:T(8,128)S(1)} collective-permute-done((f32[256,128]{1,0:T(8,128)S(1)}, f32[256,128]{1,0:T(8,128)S(1)}, u32[]{:S(2)}, u32[]{:S(2)}) %collective-permute-start.4) | collective-permute-done | bytes 131104 | tf_op jit(solution)/shard_map/ppermute | solution.py:472
  29.7 0.5 shard_map.147
  30.2 1.9 %collective-permute-start.5 = (f32[64,128]{1,0:T(8,128)S(1)}, f32[64,128]{1,0:T(8,128)S(1)}, u32[]{:S(2)}, u32[]{:S(2)}) collective-permute-start(f32[64,128]{1,0:T(8,128)S(1)} %get-tuple-element.52.own), channel_id=1, source_target_pairs={{0,8},{8,0},{16,24},{24,16},{1,9},{9,1},{17,25},{25,17},{2,10},{10... | collective-permute-start | bytes 98312 | tf_op jit(solution)/shard_map/ppermute | solution.py:472
  32.1 2.1 %collective-permute-done.5.recv = f32[64,128]{1,0:T(8,128)S(1)} collective-permute-done((f32[64,128]{1,0:T(8,128)S(1)}, f32[64,128]{1,0:T(8,128)S(1)}, u32[]{:S(2)}, u32[]{:S(2)}) %collective-permute-start.5) | collective-permute-done | bytes 32800 | tf_op jit(solution)/shard_map/ppermute | solution.py:472
  34.2 0.5 shard_map.151
  34.7 3.0 %collective-permute-start.6 = (f32[64,128]{1,0:T(8,128)S(1)}, f32[64,128]{1,0:T(8,128)S(1)}, u32[]{:S(2)}, u32[]{:S(2)}) collective-permute-start(f32[64,128]{1,0:T(8,128)S(1)} %get-tuple-element.54.own), channel_id=1, source_target_pairs={{0,16},{8,24},{16,0},{24,8},{1,17},{9,25},{17,1},{25,9},{2,18},{10... | collective-permute-start | bytes 98312 | tf_op jit(solution)/shard_map/ppermute | solution.py:472
  37.7 0.0 copy-start
  37.7 2.7 %shard_map.139.r_ref = f32[64,64,128]{2,1,0:T(8,128)S(1)} custom-call(f32[1024,128]{1,0:T(8,128)S(1)} %get-tuple-element.32.refs_0_), custom_call_target="tpu_custom_call" | custom-call | tf_op jit(solution)/shard_map/pallas_call | solution.py:564
  40.4 1.4 %shard_map.140 = (bf16[4096,128]{1,0:T(8,128)(2,1)S(1)}, bf16[4096,128]{1,0:T(8,128)(2,1)S(1)}) custom-call(f32[64,64,128]{2,1,0:T(8,128)S(1)} %shard_map.139.r_ref), custom_call_target="tpu_custom_call" | custom-call | tf_op jit(solution)/shard_map/pallas_call | solution.py:568
  41.8 0.0 copy-done
  41.8 2.8 %shard_map.141.refs_0_ = f32[1,64,4096]{2,1,0:T(8,128)} custom-call(s32[1,2,64]{2,1,0:T(2,128)S(1)} %get-tuple-element.31.left_pick.right_pick, s32[1,2,64]{2,1,0:T(2,128)S(1)} %get-tuple-element.31.left_pick.right_pick, bf16[4096,128]{1,0:T(8,128)(2,1)S(1)} %get-tuple-element.33.left, bf16[4096,128]{1,0:T(8,128)(2,1)S(1)} %get-tuple-element.34.right, ...), custom_call_target="tpu_custom_call" | custom-call | tf_op jit(solution)/shard_map/pallas_call | solution.py:577
  44.6 2.8 %shard_map.142 = f32[1,64,4096]{2,1,0:T(8,128)} custom-call(s32[1,2,64]{2,1,0:T(2,128)S(1)} %get-tuple-element.31.left_pick.right_pick, s32[1,2,64]{2,1,0:T(2,128)S(1)} %get-tuple-element.31.left_pick.right_pick, bf16[4096,128]{1,0:T(8,128)(2,1)S(1)} %get-tuple-element.33.left, ...), custom_call_target="tpu_custom_call", output_to_operand_aliasing={{}: (5, {})} | custom-call | tf_op jit(solution)/shard_map/pallas_call | solution.py:577
  47.5 0.0 copy-start.1
  47.5 2.8 %shard_map.148.r_ref = f32[64,64,128]{2,1,0:T(8,128)S(1)} custom-call(f32[256,128]{1,0:T(8,128)S(1)} %get-tuple-element.48.refs_0_, f32[128,128]{1,0:T(8,128)S(1)} %get-tuple-element.49.refs_1_), custom_call_target="tpu_custom_call" | custom-call | tf_op jit(solution)/shard_map/pallas_call | solution.py:564
  50.3 1.3 %shard_map.149 = (bf16[1536,128]{1,0:T(8,128)(2,1)S(1)}, bf16[1536,128]{1,0:T(8,128)(2,1)S(1)}) custom-call(f32[64,64,128]{2,1,0:T(8,128)S(1)} %shard_map.148.r_ref), custom_call_target="tpu_custom_call" | custom-call | tf_op jit(solution)/shard_map/pallas_call | solution.py:568
  51.6 0.0 copy-done.1
  51.6 2.8 %shard_map.150 = f32[1,32,4096]{2,1,0:T(8,128)} custom-call(s32[1,1,32]{2,1,0:T(1,128)S(1)} %get-tuple-element.35.left_pick, s32[1,1,32]{2,1,0:T(1,128)S(1)} %get-tuple-element.36.right_pick, bf16[1536,128]{1,0:T(8,128)(2,1)S(1)} %get-tuple-element.50.left, bf16[1536,128]{1,0:T(8,128)(2,1)S(1)} %get-tuple-element.51.right, bf16[1,32,4096]{2,1,0:T(8,128)(2,1)S(1)} %copy-done.1), custom_call_target="tpu_custom_call" | custom-call | tf_op jit(solution)/shard_map/pallas_call | solution.py:577
  54.4 0.0 collective-permute-done.6.recv
  54.5 3.3 %shard_map.153 = (f32[1,1,4096]{2,1,0:T(1,128)}, f32[1,1,4096]{2,1,0:T(1,128)}) custom-call(f32[64,128]{1,0:T(8,128)S(1)} %shard_map.152.high), custom_call_target="tpu_custom_call" | custom-call | tf_op jit(solution)/shard_map/pallas_call | solution.py:617
  (1 shorter events, 0.0 us)
Async XLA Ops:
  5.7 5.4 %collective-permute-start = (f32[128,128]{1,0:T(8,128)S(1)}, f32[128,128]{1,0:T(8,128)S(1)}, u32[]{:S(2)}, u32[]{:S(2)}) collective-permute-start(f32[128,128]{1,0:T(8,128)S(1)} %get-tuple-element.37.own), channel_id=1, source_target_pairs={{0,8},{8,0},{16,24},{24,16},{1,9},{9,1},{17,25},{25,17},{2,10},{10... | collective-permute-start | bytes 196616 | tf_op jit(solution)/shard_map/ppermute | solution.py:472
  11.6 5.3 %collective-permute-start.1 = (f32[128,128]{1,0:T(8,128)S(1)}, f32[128,128]{1,0:T(8,128)S(1)}, u32[]{:S(2)}, u32[]{:S(2)}) collective-permute-start(f32[128,128]{1,0:T(8,128)S(1)} %get-tuple-element.39.own), channel_id=1, source_target_pairs={{0,16},{8,24},{16,0},{24,8},{1,17},{9,25},{17,1},{25,9},{2,18},{10... | collective-permute-start | bytes 196616 | tf_op jit(solution)/shard_map/ppermute | solution.py:472
  17.4 1.4 %collective-permute-start.2 = (f32[192,128]{1,0:T(8,128)S(1)}, f32[192,128]{1,0:T(8,128)S(1)}, u32[]{:S(2)}, u32[]{:S(2)}) collective-permute-start(f32[192,128]{1,0:T(8,128)S(1)} %get-tuple-element.42.own), channel_id=1, source_target_pairs={{0,1},{1,0},{2,3},{3,2},{4,5},{5,4},{6,7},{7,6},{8,9},{9,8},{10,11... | collective-permute-start | bytes 294920 | tf_op jit(solution)/shard_map/ppermute | solution.py:472
  19.2 5.0 %collective-permute-start.3 = (f32[192,128]{1,0:T(8,128)S(1)}, f32[192,128]{1,0:T(8,128)S(1)}, u32[]{:S(2)}, u32[]{:S(2)}) collective-permute-start(f32[192,128]{1,0:T(8,128)S(1)} %get-tuple-element.44.own), channel_id=1, source_target_pairs={{0,2},{1,3},{2,0},{3,1},{4,6},{5,7},{6,4},{7,5},{8,10},{9,11},{10,... | collective-permute-start | bytes 294920 | tf_op jit(solution)/shard_map/ppermute | solution.py:472
  24.7 5.0 %collective-permute-start.4 = (f32[256,128]{1,0:T(8,128)S(1)}, f32[256,128]{1,0:T(8,128)S(1)}, u32[]{:S(2)}, u32[]{:S(2)}) collective-permute-start(f32[256,128]{1,0:T(8,128)S(1)} %get-tuple-element.46.own), channel_id=1, source_target_pairs={{0,4},{1,5},{2,6},{3,7},{4,0},{5,1},{6,2},{7,3},{8,12},{9,13},{10,... | collective-permute-start | bytes 393224 | tf_op jit(solution)/shard_map/ppermute | solution.py:472
  30.2 4.0 %collective-permute-start.5 = (f32[64,128]{1,0:T(8,128)S(1)}, f32[64,128]{1,0:T(8,128)S(1)}, u32[]{:S(2)}, u32[]{:S(2)}) collective-permute-start(f32[64,128]{1,0:T(8,128)S(1)} %get-tuple-element.52.own), channel_id=1, source_target_pairs={{0,8},{8,0},{16,24},{24,16},{1,9},{9,1},{17,25},{25,17},{2,10},{10... | collective-permute-start | bytes 98312 | tf_op jit(solution)/shard_map/ppermute | solution.py:472
  34.7 19.8 %collective-permute-start.6 = (f32[64,128]{1,0:T(8,128)S(1)}, f32[64,128]{1,0:T(8,128)S(1)}, u32[]{:S(2)}, u32[]{:S(2)}) collective-permute-start(f32[64,128]{1,0:T(8,128)S(1)} %get-tuple-element.54.own), channel_id=1, source_target_pairs={{0,16},{8,24},{16,0},{24,8},{1,17},{9,25},{17,1},{25,9},{2,18},{10... | collective-permute-start | bytes 98312 | tf_op jit(solution)/shard_map/ppermute | solution.py:472
  37.7 4.1 %copy-start = (bf16[1,64,4096]{2,1,0:T(8,128)(2,1)S(1)}, bf16[1,64,4096]{2,1,0:T(8,128)(2,1)}, u32[]{:S(2)}) copy-start(bf16[1,64,4096]{2,1,0:T(8,128)(2,1)} %blocks.4) | copy-start | bytes 1572868
  47.5 4.1 %copy-start.1 = (bf16[1,32,4096]{2,1,0:T(8,128)(2,1)S(1)}, bf16[1,32,4096]{2,1,0:T(8,128)(2,1)}, u32[]{:S(2)}) copy-start(bf16[1,32,4096]{2,1,0:T(8,128)(2,1)} %blocks.5) | copy-start | bytes 786436

commit v6 on v5

--- a/solution.py
+++ b/solution.py
@@ -247,7 +247,7 @@
             roots_out[rows : 2 * rows, :] = jnp.where(upper, mine, theirs)
 
 
-def chol_lanes(a_ref, r_ref, scale_ref):
+def chol_lanes(a_ref, r_ref, scale_ref, begin=-1, end=NB - 1):
     sub = lax.broadcasted_iota(jnp.int32, (SUB, WIDE), 0)
     here = lax.axis_index("row") >= 0
 
@@ -290,7 +290,7 @@
                 for q in qs:
                     acc[r2, q] = less(acc[r2, q], f, acc[r, q])
 
-    for p in range(-1, NB - 1):
+    for p in range(begin, end):
 
         @pl.when(here)
         def _():
@@ -303,6 +303,7 @@
 
 
 CELL = WIDE // SUB
+CUT = NB // 2
 
 
 def load_slots(slots, a_ref):
@@ -344,6 +345,23 @@
     slots = [(ref, s) for ref in inputs for s in range(ref.shape[0] // RANK)]
     load_slots(slots, a_ref)
     chol_lanes(a_ref, r_ref, scale_ref)
+
+
+def chol_first_kernel(gram, r_ref, a_ref, scale_ref):
+    slots = [(gram, s) for s in range(gram.shape[0] // RANK)]
+    load_slots(slots, a_ref)
+    chol_lanes(a_ref, r_ref, scale_ref, -1, CUT)
+
+
+def chol_second_kernel(count, r_in, a_ref, scale_in, left, right, r_ref, scale_ref):
+    for k in range(SUB * (CUT + 1)):
+        last = CUT + 1 if k >= SUB * CUT else NB
+        at = slice(SUB * (k // SUB), SUB * last)
+        r_ref[k, at, :] = r_in[k, at, :]
+    for k in range(SUB * CUT, SUB * (CUT + 1)):
+        scale_ref[k] = scale_in[k]
+    chol_lanes(a_ref, r_ref, scale_ref, CUT, NB - 1)
+    table_kernel(count, r_ref, left, right)
 
 
 def table_kernel(count, r_ref, left, right):
@@ -398,7 +416,7 @@
         to = pl.ds(pl.multiple_of((first_group + g) * 2 * SUB, 2 * SUB), 2 * SUB)
         return pltpu.make_async_copy(out.at[at, :], target.at[0, to, :], sem.at[g])
 
-    def group(g, carry):
+    def group(g, s_ref, y_ref):
         local = pl.multiple_of(g * 2 * SUB, 2 * SUB)
         start = pl.multiple_of((first_group + g) * 2 * SUB, 2 * SUB)
 
@@ -442,9 +460,9 @@
                     swapped(even), odd
                 )
         copy(g).start()
-        return carry
-
-    lax.fori_loop(0, groups, group, 0)
+
+    for g in range(groups):
+        group(g, s_ref.at[g % 2], y_ref.at[g % 2])
     for g in range(groups):
         copy(g).wait()
 
@@ -560,7 +578,22 @@
 
     big = [pltpu.VMEM((RANK, RANK, WIDE), F32)] * 2 + [pltpu.VMEM((RANK, SUB, WIDE), F32)]
 
-    def tables(count, *sources):
+    def leaf_tables(count, gram):
+        parts = call(
+            chol_first_kernel,
+            [
+                shape(RANK, RANK, WIDE),
+                shape(RANK, RANK, WIDE),
+                shape(RANK, SUB, WIDE),
+            ],
+            [VMEM],
+        )(gram)
+        out = jax.ShapeDtypeStruct((2 * count * WIDE, WIDE), BF16)
+        return call(
+            functools.partial(chol_second_kernel, count), [out, out], [VMEM] * 3, big[1:], limit=12
+        )(*parts)
+
+    def root_tables(count, *sources):
         factors = call(
             chol_kernel, shape(RANK, RANK, WIDE), [VMEM] * len(sources), big[1:]
         )(*sources)
@@ -580,8 +613,8 @@
                     in_specs=[SMEM, SMEM, VMEM, VMEM, VMEM] + [HBM] * len(result),
                     out_specs=HBM,
                     scratch_shapes=[
-                        scratch(SUB * RANK),
-                        scratch(SUB * RANK),
+                        pltpu.VMEM((2, SUB * RANK, WIDE), F32),
+                        pltpu.VMEM((2, SUB * RANK, WIDE), F32),
                         scratch(pairs, RANK * RANK),
                         pltpu.SemaphoreType.DMA((groups,)),
                     ],
@@ -600,7 +633,7 @@
         lambda ref, b: ref[0, 1, b] + count,
         leaf_pattern,
         leaf_pattern,
-        tables(count, leaf_gram),
+        leaf_tables(count, leaf_gram),
         leaf_blocks,
     )
     row_slots, col_slots = nc // 2, nr // 2
@@ -611,7 +644,7 @@
         lambda ref, b: (ref[0, 0, b] & 1) * slots + (ref[0, 0, b] >> 1) + row_slots,
         root_rows,
         root_cols,
-        tables(slots, row_roots, col_roots),
+        root_tables(slots, row_roots, col_roots),
         root_blocks,
     )
     row_upper_r, col_upper_r = call(

time: 58 us -> 56.6 us (0.976)
  Pallas kernels: 27.9 us -> 26.5 us
    pallas_call x3, Pallas kernels: 8.49 us -> 7.02 us  [couple(): pl.pallas_call(functools.partial(couple_kernel, first, groups, left_of, r...]
  transfers between devices with their start and end apart: 7 -> 7, of which waited for: 6 -> 6; matrix products, arithmetic and copies ran while one was open for 0% -> 0% of each run, Pallas kernels for 29% -> 27%
where the time goes in v6:
time: 56.6 us; the launch traced here: 56.4 us
  Pallas kernels  26.5 us (47%)
  starting transfers between devices  14.9 us (26%)
  waiting for transfers between devices  14.2 us (25%)
  between operations  0.8 us (1%)
    ppermute x7, starting transfers between devices, partner(): lax.ppermute(value, axis, [(i, i ^ 1 << bit) for i in range(lax.axis_size...  14.9 us
    ppermute x7, waiting for transfers between devices, partner(): lax.ppermute(value, axis, [(i, i ^ 1 << bit) for i in range(lax.axis_size...  14.2 us
    pallas_call x3, Pallas kernels, couple(): pl.pallas_call(functools.partial(couple_kernel, first, groups, left_of, r...  7.02 us
    pallas_call x1, Pallas kernels, body(): call(functools.partial(tree_kernel, count), [shape(count * RANK, WIDE), s...  5.1 us
    pallas_call x1, Pallas kernels, body(): call(final_kernel, [shape(1, 1, RANK * RANK), shape(1, 1, RANK * RANK)],...  3.33 us
    pallas_call x1, Pallas kernels, root_tables(): call(chol_kernel, shape(RANK, RANK, WIDE), [VMEM] * len(sources), big[1:])  2.84 us
    pallas_call x7, Pallas kernels, step(): call(functools.partial(step_kernel, levels, top, (nr, nc), held, apart, e...  2.8 us
    pallas_call x1, Pallas kernels, leaf_tables(): call(functools.partial(chol_second_kernel, count), [out, out], [VMEM] * 3...  2.38 us
  transfers between devices with their start and end apart: 7, of which 6 were waited for; matrix products, arithmetic and copies ran while one was open for 0% of the time, Pallas kernels for 27%

profile of v6, /device:TPU:0, one launch (start us, length us, event | category | flops | bytes accessed | tf_op | source)
XLA Modules:
  0.0 56.4 jit_solution(11358468693156386145)
XLA Ops:
  0.6 5.1 %shard_map.138 = (f32[1024,128]{1,0:T(8,128)S(1)}, f32[128,128]{1,0:T(8,128)S(1)}, f32[128,128]{1,0:T(8,128)S(1)}, f32[64,128]{1,0:T(8,128)S(1)}, s32[1,2,64]{2,...) custom-call(s32[1,1,16]{2,1,0:T(1,128)} %row_order_in.1, s32[1,1,16]{2,1,0:T(1,128)} %col_order_in.1, ...), custom_call_target="tpu_custom_call" | custom-call | tf_op jit(solution)/shard_map/pallas_call | solution.py:511
  5.7 3.1 %collective-permute-start = (f32[128,128]{1,0:T(8,128)S(1)}, f32[128,128]{1,0:T(8,128)S(1)}, u32[]{:S(2)}, u32[]{:S(2)}) collective-permute-start(f32[128,128]{1,0:T(8,128)S(1)} %get-tuple-element.43.own), channel_id=1, source_target_pairs={{0,8},{8,0},{16,24},{24,16},{1,9},{9,1},{17,25},{25,17},{2,10},{10... | collective-permute-start | bytes 196616 | tf_op jit(solution)/shard_map/ppermute | solution.py:490
  8.9 2.2 %collective-permute-done.recv = f32[128,128]{1,0:T(8,128)S(1)} collective-permute-done((f32[128,128]{1,0:T(8,128)S(1)}, f32[128,128]{1,0:T(8,128)S(1)}, u32[]{:S(2)}, u32[]{:S(2)}) %collective-permute-start) | collective-permute-done | bytes 65568 | tf_op jit(solution)/shard_map/ppermute | solution.py:490
  11.1 0.5 shard_map.143
  11.6 3.1 %collective-permute-start.1 = (f32[128,128]{1,0:T(8,128)S(1)}, f32[128,128]{1,0:T(8,128)S(1)}, u32[]{:S(2)}, u32[]{:S(2)}) collective-permute-start(f32[128,128]{1,0:T(8,128)S(1)} %get-tuple-element.45.own), channel_id=1, source_target_pairs={{0,16},{8,24},{16,0},{24,8},{1,17},{9,25},{17,1},{25,9},{2,18},{10... | collective-permute-start | bytes 196616 | tf_op jit(solution)/shard_map/ppermute | solution.py:490
  14.7 2.2 %collective-permute-done.1.recv = f32[128,128]{1,0:T(8,128)S(1)} collective-permute-done((f32[128,128]{1,0:T(8,128)S(1)}, f32[128,128]{1,0:T(8,128)S(1)}, u32[]{:S(2)}, u32[]{:S(2)}) %collective-permute-start.1) | collective-permute-done | bytes 65568 | tf_op jit(solution)/shard_map/ppermute | solution.py:490
  16.9 0.5 shard_map.144
  17.4 0.1 collective-permute-start.2
  17.4 1.3 %collective-permute-done.2.recv = f32[192,128]{1,0:T(8,128)S(1)} collective-permute-done((f32[192,128]{1,0:T(8,128)S(1)}, f32[192,128]{1,0:T(8,128)S(1)}, u32[]{:S(2)}, u32[]{:S(2)}) %collective-permute-start.2) | collective-permute-done | bytes 98336 | tf_op jit(solution)/shard_map/ppermute | solution.py:490
  18.7 0.5 shard_map.145
  19.2 1.9 %collective-permute-start.3 = (f32[192,128]{1,0:T(8,128)S(1)}, f32[192,128]{1,0:T(8,128)S(1)}, u32[]{:S(2)}, u32[]{:S(2)}) collective-permute-start(f32[192,128]{1,0:T(8,128)S(1)} %get-tuple-element.50.own), channel_id=1, source_target_pairs={{0,2},{1,3},{2,0},{3,1},{4,6},{5,7},{6,4},{7,5},{8,10},{9,11},{10,... | collective-permute-start | bytes 294920 | tf_op jit(solution)/shard_map/ppermute | solution.py:490
  21.1 3.1 %collective-permute-done.3.recv = f32[192,128]{1,0:T(8,128)S(1)} collective-permute-done((f32[192,128]{1,0:T(8,128)S(1)}, f32[192,128]{1,0:T(8,128)S(1)}, u32[]{:S(2)}, u32[]{:S(2)}) %collective-permute-start.3) | collective-permute-done | bytes 98336 | tf_op jit(solution)/shard_map/ppermute | solution.py:490
  24.2 0.5 shard_map.146
  24.7 1.8 %collective-permute-start.4 = (f32[256,128]{1,0:T(8,128)S(1)}, f32[256,128]{1,0:T(8,128)S(1)}, u32[]{:S(2)}, u32[]{:S(2)}) collective-permute-start(f32[256,128]{1,0:T(8,128)S(1)} %get-tuple-element.52.own), channel_id=1, source_target_pairs={{0,4},{1,5},{2,6},{3,7},{4,0},{5,1},{6,2},{7,3},{8,12},{9,13},{10,... | collective-permute-start | bytes 393224 | tf_op jit(solution)/shard_map/ppermute | solution.py:490
  26.5 3.2 %collective-permute-done.4.recv = f32[256,128]{1,0:T(8,128)S(1)} collective-permute-done((f32[256,128]{1,0:T(8,128)S(1)}, f32[256,128]{1,0:T(8,128)S(1)}, u32[]{:S(2)}, u32[]{:S(2)}) %collective-permute-start.4) | collective-permute-done | bytes 131104 | tf_op jit(solution)/shard_map/ppermute | solution.py:490
  29.7 0.5 shard_map.147
  30.2 1.9 %collective-permute-start.5 = (f32[64,128]{1,0:T(8,128)S(1)}, f32[64,128]{1,0:T(8,128)S(1)}, u32[]{:S(2)}, u32[]{:S(2)}) collective-permute-start(f32[64,128]{1,0:T(8,128)S(1)} %get-tuple-element.58.own), channel_id=1, source_target_pairs={{0,8},{8,0},{16,24},{24,16},{1,9},{9,1},{17,25},{25,17},{2,10},{10... | collective-permute-start | bytes 98312 | tf_op jit(solution)/shard_map/ppermute | solution.py:490
  32.1 2.1 %collective-permute-done.5.recv = f32[64,128]{1,0:T(8,128)S(1)} collective-permute-done((f32[64,128]{1,0:T(8,128)S(1)}, f32[64,128]{1,0:T(8,128)S(1)}, u32[]{:S(2)}, u32[]{:S(2)}) %collective-permute-start.5) | collective-permute-done | bytes 32800 | tf_op jit(solution)/shard_map/ppermute | solution.py:490
  34.2 0.5 shard_map.151
  34.7 3.0 %collective-permute-start.6 = (f32[64,128]{1,0:T(8,128)S(1)}, f32[64,128]{1,0:T(8,128)S(1)}, u32[]{:S(2)}, u32[]{:S(2)}) collective-permute-start(f32[64,128]{1,0:T(8,128)S(1)} %get-tuple-element.60.own), channel_id=1, source_target_pairs={{0,16},{8,24},{16,0},{24,8},{1,17},{9,25},{17,1},{25,9},{2,18},{10... | collective-permute-start | bytes 98312 | tf_op jit(solution)/shard_map/ppermute | solution.py:490
  37.7 1.8 %shard_map.139 = (f32[64,64,128]{2,1,0:T(8,128)S(1)}, f32[64,64,128]{2,1,0:T(8,128)S(1)}, f32[64,8,128]{2,1,0:T(8,128)S(1)}) custom-call(f32[1024,128]{1,0:T(8,128)S(1)} %get-tuple-element.35.gram), custom_call_target="tpu_custom_call" | custom-call | tf_op jit(solution)/shard_map/pallas_call | solution.py:582
  39.5 0.0 copy-start
  39.5 2.4 %shard_map.140 = (bf16[4096,128]{1,0:T(8,128)(2,1)S(1)}, bf16[4096,128]{1,0:T(8,128)(2,1)S(1)}) custom-call(f32[64,64,128]{2,1,0:T(8,128)S(1)} %get-tuple-element.36.r_in, f32[64,64,128]{2,1,0:T(8,128)S(1)} %get-tuple-element.37.a_ref, f32[64,8,128]{2,1,0:T(8,128)S(1)} %get-tuple-element.38.scale_in), custom_call_target="tpu_custom_call" | custom-call | tf_op jit(solution)/shard_map/pallas_call | solution.py:592
  41.8 0.0 copy-done
  41.9 2.3 %shard_map.141.refs_0_ = f32[1,64,4096]{2,1,0:T(8,128)} custom-call(s32[1,2,64]{2,1,0:T(2,128)S(1)} %get-tuple-element.34.left_pick.right_pick, s32[1,2,64]{2,1,0:T(2,128)S(1)} %get-tuple-element.34.left_pick.right_pick, bf16[4096,128]{1,0:T(8,128)(2,1)S(1)} %get-tuple-element.39.left, bf16[4096,128]{1,0:T(8,128)(2,1)S(1)} %get-tuple-element.40.right, ...), custom_call_target="tpu_custom_call" | custom-call | tf_op jit(solution)/shard_map/pallas_call | solution.py:610
  44.2 2.3 %shard_map.142 = f32[1,64,4096]{2,1,0:T(8,128)} custom-call(s32[1,2,64]{2,1,0:T(2,128)S(1)} %get-tuple-element.34.left_pick.right_pick, s32[1,2,64]{2,1,0:T(2,128)S(1)} %get-tuple-element.34.left_pick.right_pick, bf16[4096,128]{1,0:T(8,128)(2,1)S(1)} %get-tuple-element.39.left, ...), custom_call_target="tpu_custom_call", output_to_operand_aliasing={{}: (5, {})} | custom-call | tf_op jit(solution)/shard_map/pallas_call | solution.py:610
  46.6 0.0 copy-start.1
  46.6 2.8 %shard_map.148.r_ref = f32[64,64,128]{2,1,0:T(8,128)S(1)} custom-call(f32[256,128]{1,0:T(8,128)S(1)} %get-tuple-element.54.refs_0_, f32[128,128]{1,0:T(8,128)S(1)} %get-tuple-element.55.refs_1_), custom_call_target="tpu_custom_call" | custom-call | tf_op jit(solution)/shard_map/pallas_call | solution.py:597
  49.4 1.3 %shard_map.149 = (bf16[1536,128]{1,0:T(8,128)(2,1)S(1)}, bf16[1536,128]{1,0:T(8,128)(2,1)S(1)}) custom-call(f32[64,64,128]{2,1,0:T(8,128)S(1)} %shard_map.148.r_ref), custom_call_target="tpu_custom_call" | custom-call | tf_op jit(solution)/shard_map/pallas_call | solution.py:601
  50.7 0.0 copy-done.1
  50.7 2.3 %shard_map.150 = f32[1,32,4096]{2,1,0:T(8,128)} custom-call(s32[1,1,32]{2,1,0:T(1,128)S(1)} %get-tuple-element.41.left_pick, s32[1,1,32]{2,1,0:T(1,128)S(1)} %get-tuple-element.42.right_pick, bf16[1536,128]{1,0:T(8,128)(2,1)S(1)} %get-tuple-element.56.left, bf16[1536,128]{1,0:T(8,128)(2,1)S(1)} %get-tuple-element.57.right, bf16[1,32,4096]{2,1,0:T(8,128)(2,1)S(1)} %copy-done.1), custom_call_target="tpu_custom_call" | custom-call | tf_op jit(solution)/shard_map/pallas_call | solution.py:610
  53.1 0.0 collective-permute-done.6.recv
  53.1 3.3 %shard_map.153 = (f32[1,1,4096]{2,1,0:T(1,128)}, f32[1,1,4096]{2,1,0:T(1,128)}) custom-call(f32[64,128]{1,0:T(8,128)S(1)} %shard_map.152.high), custom_call_target="tpu_custom_call" | custom-call | tf_op jit(solution)/shard_map/pallas_call | solution.py:650
  (1 shorter events, 0.0 us)
Async XLA Ops:
  5.7 5.4 %collective-permute-start = (f32[128,128]{1,0:T(8,128)S(1)}, f32[128,128]{1,0:T(8,128)S(1)}, u32[]{:S(2)}, u32[]{:S(2)}) collective-permute-start(f32[128,128]{1,0:T(8,128)S(1)} %get-tuple-element.43.own), channel_id=1, source_target_pairs={{0,8},{8,0},{16,24},{24,16},{1,9},{9,1},{17,25},{25,17},{2,10},{10... | collective-permute-start | bytes 196616 | tf_op jit(solution)/shard_map/ppermute | solution.py:490
  11.6 5.3 %collective-permute-start.1 = (f32[128,128]{1,0:T(8,128)S(1)}, f32[128,128]{1,0:T(8,128)S(1)}, u32[]{:S(2)}, u32[]{:S(2)}) collective-permute-start(f32[128,128]{1,0:T(8,128)S(1)} %get-tuple-element.45.own), channel_id=1, source_target_pairs={{0,16},{8,24},{16,0},{24,8},{1,17},{9,25},{17,1},{25,9},{2,18},{10... | collective-permute-start | bytes 196616 | tf_op jit(solution)/shard_map/ppermute | solution.py:490
  17.4 1.4 %collective-permute-start.2 = (f32[192,128]{1,0:T(8,128)S(1)}, f32[192,128]{1,0:T(8,128)S(1)}, u32[]{:S(2)}, u32[]{:S(2)}) collective-permute-start(f32[192,128]{1,0:T(8,128)S(1)} %get-tuple-element.48.own), channel_id=1, source_target_pairs={{0,1},{1,0},{2,3},{3,2},{4,5},{5,4},{6,7},{7,6},{8,9},{9,8},{10,11... | collective-permute-start | bytes 294920 | tf_op jit(solution)/shard_map/ppermute | solution.py:490
  19.2 5.0 %collective-permute-start.3 = (f32[192,128]{1,0:T(8,128)S(1)}, f32[192,128]{1,0:T(8,128)S(1)}, u32[]{:S(2)}, u32[]{:S(2)}) collective-permute-start(f32[192,128]{1,0:T(8,128)S(1)} %get-tuple-element.50.own), channel_id=1, source_target_pairs={{0,2},{1,3},{2,0},{3,1},{4,6},{5,7},{6,4},{7,5},{8,10},{9,11},{10,... | collective-permute-start | bytes 294920 | tf_op jit(solution)/shard_map/ppermute | solution.py:490
  24.7 5.0 %collective-permute-start.4 = (f32[256,128]{1,0:T(8,128)S(1)}, f32[256,128]{1,0:T(8,128)S(1)}, u32[]{:S(2)}, u32[]{:S(2)}) collective-permute-start(f32[256,128]{1,0:T(8,128)S(1)} %get-tuple-element.52.own), channel_id=1, source_target_pairs={{0,4},{1,5},{2,6},{3,7},{4,0},{5,1},{6,2},{7,3},{8,12},{9,13},{10,... | collective-permute-start | bytes 393224 | tf_op jit(solution)/shard_map/ppermute | solution.py:490
  30.2 4.0 %collective-permute-start.5 = (f32[64,128]{1,0:T(8,128)S(1)}, f32[64,128]{1,0:T(8,128)S(1)}, u32[]{:S(2)}, u32[]{:S(2)}) collective-permute-start(f32[64,128]{1,0:T(8,128)S(1)} %get-tuple-element.58.own), channel_id=1, source_target_pairs={{0,8},{8,0},{16,24},{24,16},{1,9},{9,1},{17,25},{25,17},{2,10},{10... | collective-permute-start | bytes 98312 | tf_op jit(solution)/shard_map/ppermute | solution.py:490
  34.7 18.4 %collective-permute-start.6 = (f32[64,128]{1,0:T(8,128)S(1)}, f32[64,128]{1,0:T(8,128)S(1)}, u32[]{:S(2)}, u32[]{:S(2)}) collective-permute-start(f32[64,128]{1,0:T(8,128)S(1)} %get-tuple-element.60.own), channel_id=1, source_target_pairs={{0,16},{8,24},{16,0},{24,8},{1,17},{9,25},{17,1},{25,9},{2,18},{10... | collective-permute-start | bytes 98312 | tf_op jit(solution)/shard_map/ppermute | solution.py:490
  39.5 2.4 %copy-start = (bf16[1,64,4096]{2,1,0:T(8,128)(2,1)S(1)}, bf16[1,64,4096]{2,1,0:T(8,128)(2,1)}, u32[]{:S(2)}) copy-start(bf16[1,64,4096]{2,1,0:T(8,128)(2,1)} %blocks.4) | copy-start | bytes 1572868
  46.6 4.1 %copy-start.1 = (bf16[1,32,4096]{2,1,0:T(8,128)(2,1)S(1)}, bf16[1,32,4096]{2,1,0:T(8,128)(2,1)}, u32[]{:S(2)}) copy-start(bf16[1,32,4096]{2,1,0:T(8,128)(2,1)} %blocks.5) | copy-start | bytes 786436

commit v7 on v6

--- a/solution.py
+++ b/solution.py
@@ -310,6 +310,14 @@
     cell = lax.broadcasted_iota(jnp.int32, (RANK, WIDE), 1) % SUB
     for q in range(NB):
         b0 = SUB * q
+        if len(slots) <= SUB:
+            group = slots + [slots[-1]] * (SUB - len(slots))
+            tiles = [ref[s * RANK + b0 : s * RANK + b0 + SUB, :] for ref, s in group]
+            t = jnp.concatenate(tiles, axis=0).T
+            value = jnp.concatenate([t[b0:RANK], t[RANK + b0 :]], axis=1)
+            for r in range(SUB):
+                a_ref[b0 + r, b0:RANK, :] = pltpu.roll(value, WIDE - r, 1) if r else value
+            continue
         turned = []
         for g in range(0, len(slots), CELL):
             group = slots[g : g + CELL]
@@ -329,7 +337,10 @@
     cell = lax.broadcasted_iota(jnp.int32, (SUB, WIDE), 1) % SUB
     columns = []
     for half in range(2):
-        offset = 2 * group + half
+        offset = 0 if group is None else 2 * group + half
+        if group is None and half:
+            columns += columns
+            break
         for p in range(NB):
             tile = jnp.zeros((SUB, WIDE), F32)
             for r in range(SUB if p >= q else 0):
@@ -367,6 +378,22 @@
 def table_kernel(count, r_ref, left, right):
     keep = lane_half(2 * SUB)
     for q in range(0, NB, 2):
+        if count <= SUB:
+            upper = factor_tiles(r_ref, q, None)
+            lower = factor_tiles(r_ref, q + 1, None)
+            for half in range(2):
+                for s in range(count):
+                    rows = eight(SUB * half + s)
+                    both = jnp.concatenate([upper[rows], lower[rows]], axis=0)
+                    at = (half * count + s) * WIDE + SUB * q
+                    for table, value in (
+                        (left, jnp.where(keep, both, 0.0)),
+                        (right, jnp.where(keep, 0.0, both)),
+                    ):
+                        high, low = split(value)
+                        table[at : at + 2 * SUB, :] = high
+                        table[at + RANK : at + RANK + 2 * SUB, :] = low
+            continue
         for g in range(-(-count // CELL)):
             upper = factor_tiles(r_ref, q, g)
             lower = factor_tiles(r_ref, q + 1, g)

time: 56.6 us -> 55.9 us (0.988)
  Pallas kernels: 26.5 us -> 25.9 us
    pallas_call x1, Pallas kernels: 1.28 us -> 0.52 us  [root_tables(): call(functools.partial(table_kernel, count), [out, out], [VMEM], limit=5...]
  transfers between devices with their start and end apart: 7 -> 7, of which waited for: 6 -> 6; matrix products, arithmetic and copies ran while one was open for 0% -> 0% of each run, Pallas kernels for 27% -> 26%
where the time goes in v7:
time: 55.9 us; the launch traced here: 55.8 us
  Pallas kernels  25.9 us (46%)
  starting transfers between devices  14.9 us (27%)
  waiting for transfers between devices  14.2 us (25%)
  between operations  0.8 us (1%)
    ppermute x7, starting transfers between devices, partner(): lax.ppermute(value, axis, [(i, i ^ 1 << bit) for i in range(lax.axis_size...  14.9 us
    ppermute x7, waiting for transfers between devices, partner(): lax.ppermute(value, axis, [(i, i ^ 1 << bit) for i in range(lax.axis_size...  14.2 us
    pallas_call x3, Pallas kernels, couple(): pl.pallas_call(functools.partial(couple_kernel, first, groups, left_of, r...  7.02 us
    pallas_call x1, Pallas kernels, body(): call(functools.partial(tree_kernel, count), [shape(count * RANK, WIDE), s...  5.1 us
    pallas_call x1, Pallas kernels, body(): call(final_kernel, [shape(1, 1, RANK * RANK), shape(1, 1, RANK * RANK)],...  3.33 us
    pallas_call x1, Pallas kernels, root_tables(): call(chol_kernel, shape(RANK, RANK, WIDE), [VMEM] * len(sources), big[1:])  2.96 us
    pallas_call x7, Pallas kernels, step(): call(functools.partial(step_kernel, levels, top, (nr, nc), held, apart, e...  2.8 us
    pallas_call x1, Pallas kernels, leaf_tables(): call(functools.partial(chol_second_kernel, count), [out, out], [VMEM] * 3...  2.38 us
  transfers between devices with their start and end apart: 7, of which 6 were waited for; matrix products, arithmetic and copies ran while one was open for 0% of the time, Pallas kernels for 26%

profile of v7, /device:TPU:0, one launch (start us, length us, event | category | flops | bytes accessed | tf_op | source)
XLA Modules:
  0.0 55.8 jit_solution(17771176425769536224)
XLA Ops:
  0.6 5.1 %shard_map.138 = (f32[1024,128]{1,0:T(8,128)S(1)}, f32[128,128]{1,0:T(8,128)S(1)}, f32[128,128]{1,0:T(8,128)S(1)}, f32[64,128]{1,0:T(8,128)S(1)}, s32[1,2,64]{2,...) custom-call(s32[1,1,16]{2,1,0:T(1,128)} %row_order_in.1, s32[1,1,16]{2,1,0:T(1,128)} %col_order_in.1, ...), custom_call_target="tpu_custom_call" | custom-call | tf_op jit(solution)/shard_map/pallas_call | solution.py:538
  5.7 3.1 %collective-permute-start = (f32[128,128]{1,0:T(8,128)S(1)}, f32[128,128]{1,0:T(8,128)S(1)}, u32[]{:S(2)}, u32[]{:S(2)}) collective-permute-start(f32[128,128]{1,0:T(8,128)S(1)} %get-tuple-element.43.own), channel_id=1, source_target_pairs={{0,8},{8,0},{16,24},{24,16},{1,9},{9,1},{17,25},{25,17},{2,10},{10... | collective-permute-start | bytes 196616 | tf_op jit(solution)/shard_map/ppermute | solution.py:517
  8.9 2.2 %collective-permute-done.recv = f32[128,128]{1,0:T(8,128)S(1)} collective-permute-done((f32[128,128]{1,0:T(8,128)S(1)}, f32[128,128]{1,0:T(8,128)S(1)}, u32[]{:S(2)}, u32[]{:S(2)}) %collective-permute-start) | collective-permute-done | bytes 65568 | tf_op jit(solution)/shard_map/ppermute | solution.py:517
  11.1 0.5 shard_map.143
  11.6 3.1 %collective-permute-start.1 = (f32[128,128]{1,0:T(8,128)S(1)}, f32[128,128]{1,0:T(8,128)S(1)}, u32[]{:S(2)}, u32[]{:S(2)}) collective-permute-start(f32[128,128]{1,0:T(8,128)S(1)} %get-tuple-element.45.own), channel_id=1, source_target_pairs={{0,16},{8,24},{16,0},{24,8},{1,17},{9,25},{17,1},{25,9},{2,18},{10... | collective-permute-start | bytes 196616 | tf_op jit(solution)/shard_map/ppermute | solution.py:517
  14.7 2.2 %collective-permute-done.1.recv = f32[128,128]{1,0:T(8,128)S(1)} collective-permute-done((f32[128,128]{1,0:T(8,128)S(1)}, f32[128,128]{1,0:T(8,128)S(1)}, u32[]{:S(2)}, u32[]{:S(2)}) %collective-permute-start.1) | collective-permute-done | bytes 65568 | tf_op jit(solution)/shard_map/ppermute | solution.py:517
  16.9 0.5 shard_map.144
  17.4 0.1 collective-permute-start.2
  17.4 1.3 %collective-permute-done.2.recv = f32[192,128]{1,0:T(8,128)S(1)} collective-permute-done((f32[192,128]{1,0:T(8,128)S(1)}, f32[192,128]{1,0:T(8,128)S(1)}, u32[]{:S(2)}, u32[]{:S(2)}) %collective-permute-start.2) | collective-permute-done | bytes 98336 | tf_op jit(solution)/shard_map/ppermute | solution.py:517
  18.7 0.5 shard_map.145
  19.2 1.9 %collective-permute-start.3 = (f32[192,128]{1,0:T(8,128)S(1)}, f32[192,128]{1,0:T(8,128)S(1)}, u32[]{:S(2)}, u32[]{:S(2)}) collective-permute-start(f32[192,128]{1,0:T(8,128)S(1)} %get-tuple-element.50.own), channel_id=1, source_target_pairs={{0,2},{1,3},{2,0},{3,1},{4,6},{5,7},{6,4},{7,5},{8,10},{9,11},{10,... | collective-permute-start | bytes 294920 | tf_op jit(solution)/shard_map/ppermute | solution.py:517
  21.1 3.1 %collective-permute-done.3.recv = f32[192,128]{1,0:T(8,128)S(1)} collective-permute-done((f32[192,128]{1,0:T(8,128)S(1)}, f32[192,128]{1,0:T(8,128)S(1)}, u32[]{:S(2)}, u32[]{:S(2)}) %collective-permute-start.3) | collective-permute-done | bytes 98336 | tf_op jit(solution)/shard_map/ppermute | solution.py:517
  24.2 0.5 shard_map.146
  24.7 1.8 %collective-permute-start.4 = (f32[256,128]{1,0:T(8,128)S(1)}, f32[256,128]{1,0:T(8,128)S(1)}, u32[]{:S(2)}, u32[]{:S(2)}) collective-permute-start(f32[256,128]{1,0:T(8,128)S(1)} %get-tuple-element.52.own), channel_id=1, source_target_pairs={{0,4},{1,5},{2,6},{3,7},{4,0},{5,1},{6,2},{7,3},{8,12},{9,13},{10,... | collective-permute-start | bytes 393224 | tf_op jit(solution)/shard_map/ppermute | solution.py:517
  26.5 3.2 %collective-permute-done.4.recv = f32[256,128]{1,0:T(8,128)S(1)} collective-permute-done((f32[256,128]{1,0:T(8,128)S(1)}, f32[256,128]{1,0:T(8,128)S(1)}, u32[]{:S(2)}, u32[]{:S(2)}) %collective-permute-start.4) | collective-permute-done | bytes 131104 | tf_op jit(solution)/shard_map/ppermute | solution.py:517
  29.7 0.5 shard_map.147
  30.2 1.9 %collective-permute-start.5 = (f32[64,128]{1,0:T(8,128)S(1)}, f32[64,128]{1,0:T(8,128)S(1)}, u32[]{:S(2)}, u32[]{:S(2)}) collective-permute-start(f32[64,128]{1,0:T(8,128)S(1)} %get-tuple-element.58.own), channel_id=1, source_target_pairs={{0,8},{8,0},{16,24},{24,16},{1,9},{9,1},{17,25},{25,17},{2,10},{10... | collective-permute-start | bytes 98312 | tf_op jit(solution)/shard_map/ppermute | solution.py:517
  32.1 2.1 %collective-permute-done.5.recv = f32[64,128]{1,0:T(8,128)S(1)} collective-permute-done((f32[64,128]{1,0:T(8,128)S(1)}, f32[64,128]{1,0:T(8,128)S(1)}, u32[]{:S(2)}, u32[]{:S(2)}) %collective-permute-start.5) | collective-permute-done | bytes 32800 | tf_op jit(solution)/shard_map/ppermute | solution.py:517
  34.2 0.5 shard_map.151
  34.7 3.0 %collective-permute-start.6 = (f32[64,128]{1,0:T(8,128)S(1)}, f32[64,128]{1,0:T(8,128)S(1)}, u32[]{:S(2)}, u32[]{:S(2)}) collective-permute-start(f32[64,128]{1,0:T(8,128)S(1)} %get-tuple-element.60.own), channel_id=1, source_target_pairs={{0,16},{8,24},{16,0},{24,8},{1,17},{9,25},{17,1},{25,9},{2,18},{10... | collective-permute-start | bytes 98312 | tf_op jit(solution)/shard_map/ppermute | solution.py:517
  37.7 1.8 %shard_map.139 = (f32[64,64,128]{2,1,0:T(8,128)S(1)}, f32[64,64,128]{2,1,0:T(8,128)S(1)}, f32[64,8,128]{2,1,0:T(8,128)S(1)}) custom-call(f32[1024,128]{1,0:T(8,128)S(1)} %get-tuple-element.35.gram), custom_call_target="tpu_custom_call" | custom-call | tf_op jit(solution)/shard_map/pallas_call | solution.py:609
  39.5 0.0 copy-start
  39.5 2.4 %shard_map.140 = (bf16[4096,128]{1,0:T(8,128)(2,1)S(1)}, bf16[4096,128]{1,0:T(8,128)(2,1)S(1)}) custom-call(f32[64,64,128]{2,1,0:T(8,128)S(1)} %get-tuple-element.36.r_in, f32[64,64,128]{2,1,0:T(8,128)S(1)} %get-tuple-element.37.a_ref, f32[64,8,128]{2,1,0:T(8,128)S(1)} %get-tuple-element.38.scale_in), custom_call_target="tpu_custom_call" | custom-call | tf_op jit(solution)/shard_map/pallas_call | solution.py:619
  41.8 0.0 copy-done
  41.9 2.3 %shard_map.141.refs_0_ = f32[1,64,4096]{2,1,0:T(8,128)} custom-call(s32[1,2,64]{2,1,0:T(2,128)S(1)} %get-tuple-element.34.left_pick.right_pick, s32[1,2,64]{2,1,0:T(2,128)S(1)} %get-tuple-element.34.left_pick.right_pick, bf16[4096,128]{1,0:T(8,128)(2,1)S(1)} %get-tuple-element.39.left, bf16[4096,128]{1,0:T(8,128)(2,1)S(1)} %get-tuple-element.40.right, ...), custom_call_target="tpu_custom_call" | custom-call | tf_op jit(solution)/shard_map/pallas_call | solution.py:637
  44.2 2.3 %shard_map.142 = f32[1,64,4096]{2,1,0:T(8,128)} custom-call(s32[1,2,64]{2,1,0:T(2,128)S(1)} %get-tuple-element.34.left_pick.right_pick, s32[1,2,64]{2,1,0:T(2,128)S(1)} %get-tuple-element.34.left_pick.right_pick, bf16[4096,128]{1,0:T(8,128)(2,1)S(1)} %get-tuple-element.39.left, ...), custom_call_target="tpu_custom_call", output_to_operand_aliasing={{}: (5, {})} | custom-call | tf_op jit(solution)/shard_map/pallas_call | solution.py:637
  46.6 0.0 copy-start.1
  46.6 3.0 %shard_map.148.r_ref = f32[64,64,128]{2,1,0:T(8,128)S(1)} custom-call(f32[256,128]{1,0:T(8,128)S(1)} %get-tuple-element.54.refs_0_, f32[128,128]{1,0:T(8,128)S(1)} %get-tuple-element.55.refs_1_), custom_call_target="tpu_custom_call" | custom-call | tf_op jit(solution)/shard_map/pallas_call | solution.py:624
  49.5 0.5 shard_map.149
  50.1 0.0 copy-done.1
  50.1 2.3 %shard_map.150 = f32[1,32,4096]{2,1,0:T(8,128)} custom-call(s32[1,1,32]{2,1,0:T(1,128)S(1)} %get-tuple-element.41.left_pick, s32[1,1,32]{2,1,0:T(1,128)S(1)} %get-tuple-element.42.right_pick, bf16[1536,128]{1,0:T(8,128)(2,1)S(1)} %get-tuple-element.56.left, bf16[1536,128]{1,0:T(8,128)(2,1)S(1)} %get-tuple-element.57.right, bf16[1,32,4096]{2,1,0:T(8,128)(2,1)S(1)} %copy-done.1), custom_call_target="tpu_custom_call" | custom-call | tf_op jit(solution)/shard_map/pallas_call | solution.py:637
  52.4 0.0 collective-permute-done.6.recv
  52.5 3.3 %shard_map.153 = (f32[1,1,4096]{2,1,0:T(1,128)}, f32[1,1,4096]{2,1,0:T(1,128)}) custom-call(f32[64,128]{1,0:T(8,128)S(1)} %shard_map.152.high), custom_call_target="tpu_custom_call" | custom-call | tf_op jit(solution)/shard_map/pallas_call | solution.py:677
  (1 shorter events, 0.0 us)
Async XLA Ops:
  5.7 5.4 %collective-permute-start = (f32[128,128]{1,0:T(8,128)S(1)}, f32[128,128]{1,0:T(8,128)S(1)}, u32[]{:S(2)}, u32[]{:S(2)}) collective-permute-start(f32[128,128]{1,0:T(8,128)S(1)} %get-tuple-element.43.own), channel_id=1, source_target_pairs={{0,8},{8,0},{16,24},{24,16},{1,9},{9,1},{17,25},{25,17},{2,10},{10... | collective-permute-start | bytes 196616 | tf_op jit(solution)/shard_map/ppermute | solution.py:517
  11.6 5.3 %collective-permute-start.1 = (f32[128,128]{1,0:T(8,128)S(1)}, f32[128,128]{1,0:T(8,128)S(1)}, u32[]{:S(2)}, u32[]{:S(2)}) collective-permute-start(f32[128,128]{1,0:T(8,128)S(1)} %get-tuple-element.45.own), channel_id=1, source_target_pairs={{0,16},{8,24},{16,0},{24,8},{1,17},{9,25},{17,1},{25,9},{2,18},{10... | collective-permute-start | bytes 196616 | tf_op jit(solution)/shard_map/ppermute | solution.py:517
  17.4 1.4 %collective-permute-start.2 = (f32[192,128]{1,0:T(8,128)S(1)}, f32[192,128]{1,0:T(8,128)S(1)}, u32[]{:S(2)}, u32[]{:S(2)}) collective-permute-start(f32[192,128]{1,0:T(8,128)S(1)} %get-tuple-element.48.own), channel_id=1, source_target_pairs={{0,1},{1,0},{2,3},{3,2},{4,5},{5,4},{6,7},{7,6},{8,9},{9,8},{10,11... | collective-permute-start | bytes 294920 | tf_op jit(solution)/shard_map/ppermute | solution.py:517
  19.2 5.0 %collective-permute-start.3 = (f32[192,128]{1,0:T(8,128)S(1)}, f32[192,128]{1,0:T(8,128)S(1)}, u32[]{:S(2)}, u32[]{:S(2)}) collective-permute-start(f32[192,128]{1,0:T(8,128)S(1)} %get-tuple-element.50.own), channel_id=1, source_target_pairs={{0,2},{1,3},{2,0},{3,1},{4,6},{5,7},{6,4},{7,5},{8,10},{9,11},{10,... | collective-permute-start | bytes 294920 | tf_op jit(solution)/shard_map/ppermute | solution.py:517
  24.7 5.0 %collective-permute-start.4 = (f32[256,128]{1,0:T(8,128)S(1)}, f32[256,128]{1,0:T(8,128)S(1)}, u32[]{:S(2)}, u32[]{:S(2)}) collective-permute-start(f32[256,128]{1,0:T(8,128)S(1)} %get-tuple-element.52.own), channel_id=1, source_target_pairs={{0,4},{1,5},{2,6},{3,7},{4,0},{5,1},{6,2},{7,3},{8,12},{9,13},{10,... | collective-permute-start | bytes 393224 | tf_op jit(solution)/shard_map/ppermute | solution.py:517
  30.2 4.0 %collective-permute-start.5 = (f32[64,128]{1,0:T(8,128)S(1)}, f32[64,128]{1,0:T(8,128)S(1)}, u32[]{:S(2)}, u32[]{:S(2)}) collective-permute-start(f32[64,128]{1,0:T(8,128)S(1)} %get-tuple-element.58.own), channel_id=1, source_target_pairs={{0,8},{8,0},{16,24},{24,16},{1,9},{9,1},{17,25},{25,17},{2,10},{10... | collective-permute-start | bytes 98312 | tf_op jit(solution)/shard_map/ppermute | solution.py:517
  34.7 17.8 %collective-permute-start.6 = (f32[64,128]{1,0:T(8,128)S(1)}, f32[64,128]{1,0:T(8,128)S(1)}, u32[]{:S(2)}, u32[]{:S(2)}) collective-permute-start(f32[64,128]{1,0:T(8,128)S(1)} %get-tuple-element.60.own), channel_id=1, source_target_pairs={{0,16},{8,24},{16,0},{24,8},{1,17},{9,25},{17,1},{25,9},{2,18},{10... | collective-permute-start | bytes 98312 | tf_op jit(solution)/shard_map/ppermute | solution.py:517
  39.5 2.4 %copy-start = (bf16[1,64,4096]{2,1,0:T(8,128)(2,1)S(1)}, bf16[1,64,4096]{2,1,0:T(8,128)(2,1)}, u32[]{:S(2)}) copy-start(bf16[1,64,4096]{2,1,0:T(8,128)(2,1)} %blocks.4) | copy-start | bytes 1572868
  46.6 3.5 %copy-start.1 = (bf16[1,32,4096]{2,1,0:T(8,128)(2,1)S(1)}, bf16[1,32,4096]{2,1,0:T(8,128)(2,1)}, u32[]{:S(2)}) copy-start(bf16[1,32,4096]{2,1,0:T(8,128)(2,1)} %blocks.5) | copy-start | bytes 786436

commit v8 on v7

--- a/solution.py
+++ b/solution.py
@@ -433,6 +433,22 @@
             out[0, 0:1, lanes_of(k)] = beside(half[2 * k : 2 * k + 1], half[2 * k + 1 : 2 * k + 2])
 
 
+def unpack_blocks(blocks, start, s_ref):
+    def slab(k):
+        return blocks[0, pl.ds(start, 2 * SUB), lanes_of(k)].astype(F32)
+
+    def keep(b, q, tile):
+        s_ref[b * RANK + SUB * q : b * RANK + SUB * (q + 1), :] = tile
+
+    unpack_both(lambda k: slab(k)[:SUB], lambda k: slab(k)[SUB:], keep)
+
+
+def unpack_kernel(groups, blocks, out, s_ref):
+    for g in range(groups):
+        unpack_blocks(blocks, g * 2 * SUB, s_ref.at[g % 2])
+        out[g * SUB * RANK : (g + 1) * SUB * RANK, :] = s_ref[g % 2].astype(BF16)
+
+
 def couple_kernel(
     first_group, groups, left_of, right_of, left_pick, right_pick, left, right, blocks, *refs
 ):
@@ -447,19 +463,18 @@
         local = pl.multiple_of(g * 2 * SUB, 2 * SUB)
         start = pl.multiple_of((first_group + g) * 2 * SUB, 2 * SUB)
 
-        def slab(k):
-            return blocks[0, pl.ds(start, 2 * SUB), lanes_of(k)].astype(F32)
-
-        def keep(b, q, tile):
-            s_ref[b * RANK + SUB * q : b * RANK + SUB * (q + 1), :] = tile
-
-        unpack_both(lambda k: slab(k)[:SUB], lambda k: slab(k)[SUB:], keep)
+        if blocks.ndim == 3:
+            unpack_blocks(blocks, start, s_ref)
 
         def entry(table, pick, ref, b):
             return table[pl.ds(pl.multiple_of(pick(ref, start + b) * WIDE, WIDE), WIDE), :]
 
         for b in range(SUB):
-            block = s_ref[b * RANK : (b + 1) * RANK, :].astype(BF16)
+            if blocks.ndim == 3:
+                block = s_ref[b * RANK : (b + 1) * RANK, :].astype(BF16)
+            else:
+                at = ((first_group + g) * SUB + b) * RANK
+                block = blocks[at : at + RANK, :]
             rows = jnp.concatenate(
                 [entry(left, left_of, left_pick, n)[:, :RANK] for n in (b, b + SUB)], axis=0
             )
@@ -636,7 +651,7 @@
             result = [
                 pl.pallas_call(
                     functools.partial(couple_kernel, first, groups, left_of, right_of),
-                    out_shape=shape(1, blocks.shape[1], RANK * RANK),
+                    out_shape=shape(1, sum(parts) * 2 * SUB, RANK * RANK),
                     in_specs=[SMEM, SMEM, VMEM, VMEM, VMEM] + [HBM] * len(result),
                     out_specs=HBM,
                     scratch_shapes=[
@@ -665,6 +680,13 @@
     )
     row_slots, col_slots = nc // 2, nr // 2
     slots = row_slots + col_slots
+    root_squares = call(
+        functools.partial(unpack_kernel, root_groups),
+        jax.ShapeDtypeStruct((root_groups * SUB * RANK, WIDE), BF16),
+        [VMEM],
+        [pltpu.VMEM((2, SUB * RANK, WIDE), F32)],
+        limit=4,
+    )(root_blocks)
     root_coupled = couple(
         (root_groups,),
         lambda ref, b: (ref[0, 0, b] & 1) * slots + (ref[0, 0, b] >> 1),
@@ -672,7 +694,7 @@
         root_rows,
         root_cols,
         root_tables(slots, row_roots, col_roots),
-        root_blocks,
+        root_squares,
     )
     row_upper_r, col_upper_r = call(
         final_kernel, [shape(1, 1, RANK * RANK), shape(1, 1, RANK * RANK)], [VMEM], big

time: 55.9 us -> 56.1 us (level)
  no operation moved by 1% of the time
where the time goes in v8:
time: 56.1 us; the launch traced here: 55.9 us
  Pallas kernels  26 us (46%)
  starting transfers between devices  14.9 us (27%)
  waiting for transfers between devices  14.2 us (25%)
  between operations  0.8 us (1%)
    ppermute x7, starting transfers between devices, partner(): lax.ppermute(value, axis, [(i, i ^ 1 << bit) for i in range(lax.axis_size...  14.9 us
    ppermute x7, waiting for transfers between devices, partner(): lax.ppermute(value, axis, [(i, i ^ 1 << bit) for i in range(lax.axis_size...  14.2 us
    pallas_call x3, Pallas kernels, couple(): pl.pallas_call(functools.partial(couple_kernel, first, groups, left_of, r...  6.9 us
    pallas_call x1, Pallas kernels, body(): call(functools.partial(tree_kernel, count), [shape(count * RANK, WIDE), s...  5.1 us
    pallas_call x1, Pallas kernels, body(): call(final_kernel, [shape(1, 1, RANK * RANK), shape(1, 1, RANK * RANK)],...  3.33 us
    pallas_call x1, Pallas kernels, root_tables(): call(chol_kernel, shape(RANK, RANK, WIDE), [VMEM] * len(sources), big[1:])  2.96 us
    pallas_call x7, Pallas kernels, step(): call(functools.partial(step_kernel, levels, top, (nr, nc), held, apart, e...  2.8 us
    pallas_call x1, Pallas kernels, leaf_tables(): call(functools.partial(chol_second_kernel, count), [out, out], [VMEM] * 3...  2.38 us
  transfers between devices with their start and end apart: 7, of which 6 were waited for; matrix products, arithmetic and copies ran while one was open for 0% of the time, Pallas kernels for 26%

profile of v8, /device:TPU:0, one launch (start us, length us, event | category | flops | bytes accessed | tf_op | source)
XLA Modules:
  0.0 55.9 jit_solution(6371859553101779195)
XLA Ops:
  0.6 5.1 %shard_map.138 = (f32[1024,128]{1,0:T(8,128)S(1)}, f32[128,128]{1,0:T(8,128)S(1)}, f32[128,128]{1,0:T(8,128)S(1)}, f32[64,128]{1,0:T(8,128)S(1)}, s32[1,2,64]{2,...) custom-call(s32[1,1,16]{2,1,0:T(1,128)} %row_order_in.1, s32[1,1,16]{2,1,0:T(1,128)} %col_order_in.1, ...), custom_call_target="tpu_custom_call" | custom-call | tf_op jit(solution)/shard_map/pallas_call | solution.py:553
  5.7 3.1 %collective-permute-start = (f32[128,128]{1,0:T(8,128)S(1)}, f32[128,128]{1,0:T(8,128)S(1)}, u32[]{:S(2)}, u32[]{:S(2)}) collective-permute-start(f32[128,128]{1,0:T(8,128)S(1)} %get-tuple-element.43.own), channel_id=1, source_target_pairs={{0,8},{8,0},{16,24},{24,16},{1,9},{9,1},{17,25},{25,17},{2,10},{10... | collective-permute-start | bytes 196616 | tf_op jit(solution)/shard_map/ppermute | solution.py:532
  8.9 2.2 %collective-permute-done.recv = f32[128,128]{1,0:T(8,128)S(1)} collective-permute-done((f32[128,128]{1,0:T(8,128)S(1)}, f32[128,128]{1,0:T(8,128)S(1)}, u32[]{:S(2)}, u32[]{:S(2)}) %collective-permute-start) | collective-permute-done | bytes 65568 | tf_op jit(solution)/shard_map/ppermute | solution.py:532
  11.1 0.5 shard_map.143
  11.6 3.1 %collective-permute-start.1 = (f32[128,128]{1,0:T(8,128)S(1)}, f32[128,128]{1,0:T(8,128)S(1)}, u32[]{:S(2)}, u32[]{:S(2)}) collective-permute-start(f32[128,128]{1,0:T(8,128)S(1)} %get-tuple-element.45.own), channel_id=1, source_target_pairs={{0,16},{8,24},{16,0},{24,8},{1,17},{9,25},{17,1},{25,9},{2,18},{10... | collective-permute-start | bytes 196616 | tf_op jit(solution)/shard_map/ppermute | solution.py:532
  14.7 2.2 %collective-permute-done.1.recv = f32[128,128]{1,0:T(8,128)S(1)} collective-permute-done((f32[128,128]{1,0:T(8,128)S(1)}, f32[128,128]{1,0:T(8,128)S(1)}, u32[]{:S(2)}, u32[]{:S(2)}) %collective-permute-start.1) | collective-permute-done | bytes 65568 | tf_op jit(solution)/shard_map/ppermute | solution.py:532
  16.9 0.5 shard_map.144
  17.4 0.1 collective-permute-start.2
  17.4 1.3 %collective-permute-done.2.recv = f32[192,128]{1,0:T(8,128)S(1)} collective-permute-done((f32[192,128]{1,0:T(8,128)S(1)}, f32[192,128]{1,0:T(8,128)S(1)}, u32[]{:S(2)}, u32[]{:S(2)}) %collective-permute-start.2) | collective-permute-done | bytes 98336 | tf_op jit(solution)/shard_map/ppermute | solution.py:532
  18.7 0.5 shard_map.145
  19.2 1.9 %collective-permute-start.3 = (f32[192,128]{1,0:T(8,128)S(1)}, f32[192,128]{1,0:T(8,128)S(1)}, u32[]{:S(2)}, u32[]{:S(2)}) collective-permute-start(f32[192,128]{1,0:T(8,128)S(1)} %get-tuple-element.50.own), channel_id=1, source_target_pairs={{0,2},{1,3},{2,0},{3,1},{4,6},{5,7},{6,4},{7,5},{8,10},{9,11},{10,... | collective-permute-start | bytes 294920 | tf_op jit(solution)/shard_map/ppermute | solution.py:532
  21.1 3.1 %collective-permute-done.3.recv = f32[192,128]{1,0:T(8,128)S(1)} collective-permute-done((f32[192,128]{1,0:T(8,128)S(1)}, f32[192,128]{1,0:T(8,128)S(1)}, u32[]{:S(2)}, u32[]{:S(2)}) %collective-permute-start.3) | collective-permute-done | bytes 98336 | tf_op jit(solution)/shard_map/ppermute | solution.py:532
  24.2 0.5 shard_map.146
  24.7 1.8 %collective-permute-start.4 = (f32[256,128]{1,0:T(8,128)S(1)}, f32[256,128]{1,0:T(8,128)S(1)}, u32[]{:S(2)}, u32[]{:S(2)}) collective-permute-start(f32[256,128]{1,0:T(8,128)S(1)} %get-tuple-element.52.own), channel_id=1, source_target_pairs={{0,4},{1,5},{2,6},{3,7},{4,0},{5,1},{6,2},{7,3},{8,12},{9,13},{10,... | collective-permute-start | bytes 393224 | tf_op jit(solution)/shard_map/ppermute | solution.py:532
  26.5 3.2 %collective-permute-done.4.recv = f32[256,128]{1,0:T(8,128)S(1)} collective-permute-done((f32[256,128]{1,0:T(8,128)S(1)}, f32[256,128]{1,0:T(8,128)S(1)}, u32[]{:S(2)}, u32[]{:S(2)}) %collective-permute-start.4) | collective-permute-done | bytes 131104 | tf_op jit(solution)/shard_map/ppermute | solution.py:532
  29.7 0.5 shard_map.147
  30.2 1.9 %collective-permute-start.5 = (f32[64,128]{1,0:T(8,128)S(1)}, f32[64,128]{1,0:T(8,128)S(1)}, u32[]{:S(2)}, u32[]{:S(2)}) collective-permute-start(f32[64,128]{1,0:T(8,128)S(1)} %get-tuple-element.58.own), channel_id=1, source_target_pairs={{0,8},{8,0},{16,24},{24,16},{1,9},{9,1},{17,25},{25,17},{2,10},{10... | collective-permute-start | bytes 98312 | tf_op jit(solution)/shard_map/ppermute | solution.py:532
  32.1 2.1 %collective-permute-done.5.recv = f32[64,128]{1,0:T(8,128)S(1)} collective-permute-done((f32[64,128]{1,0:T(8,128)S(1)}, f32[64,128]{1,0:T(8,128)S(1)}, u32[]{:S(2)}, u32[]{:S(2)}) %collective-permute-start.5) | collective-permute-done | bytes 32800 | tf_op jit(solution)/shard_map/ppermute | solution.py:532
  34.2 0.5 shard_map.152
  34.7 3.0 %collective-permute-start.6 = (f32[64,128]{1,0:T(8,128)S(1)}, f32[64,128]{1,0:T(8,128)S(1)}, u32[]{:S(2)}, u32[]{:S(2)}) collective-permute-start(f32[64,128]{1,0:T(8,128)S(1)} %get-tuple-element.60.own), channel_id=1, source_target_pairs={{0,16},{8,24},{16,0},{24,8},{1,17},{9,25},{17,1},{25,9},{2,18},{10... | collective-permute-start | bytes 98312 | tf_op jit(solution)/shard_map/ppermute | solution.py:532
  37.7 1.8 %shard_map.139 = (f32[64,64,128]{2,1,0:T(8,128)S(1)}, f32[64,64,128]{2,1,0:T(8,128)S(1)}, f32[64,8,128]{2,1,0:T(8,128)S(1)}) custom-call(f32[1024,128]{1,0:T(8,128)S(1)} %get-tuple-element.35.gram), custom_call_target="tpu_custom_call" | custom-call | tf_op jit(solution)/shard_map/pallas_call | solution.py:624
  39.5 0.0 copy-start
  39.5 2.4 %shard_map.140 = (bf16[4096,128]{1,0:T(8,128)(2,1)S(1)}, bf16[4096,128]{1,0:T(8,128)(2,1)S(1)}) custom-call(f32[64,64,128]{2,1,0:T(8,128)S(1)} %get-tuple-element.36.r_in, f32[64,64,128]{2,1,0:T(8,128)S(1)} %get-tuple-element.37.a_ref, f32[64,8,128]{2,1,0:T(8,128)S(1)} %get-tuple-element.38.scale_in), custom_call_target="tpu_custom_call" | custom-call | tf_op jit(solution)/shard_map/pallas_call | solution.py:634
  41.8 0.0 copy-done
  41.9 2.3 %shard_map.141.refs_0_ = f32[1,64,4096]{2,1,0:T(8,128)} custom-call(s32[1,2,64]{2,1,0:T(2,128)S(1)} %get-tuple-element.34.left_pick.right_pick, s32[1,2,64]{2,1,0:T(2,128)S(1)} %get-tuple-element.34.left_pick.right_pick, bf16[4096,128]{1,0:T(8,128)(2,1)S(1)} %get-tuple-element.39.left, bf16[4096,128]{1,0:T(8,128)(2,1)S(1)} %get-tuple-element.40.right, ...), custom_call_target="tpu_custom_call" | custom-call | tf_op jit(solution)/shard_map/pallas_call | solution.py:652
  44.2 0.0 copy-start.1
  44.2 2.3 %shard_map.142 = f32[1,64,4096]{2,1,0:T(8,128)} custom-call(s32[1,2,64]{2,1,0:T(2,128)S(1)} %get-tuple-element.34.left_pick.right_pick, s32[1,2,64]{2,1,0:T(2,128)S(1)} %get-tuple-element.34.left_pick.right_pick, bf16[4096,128]{1,0:T(8,128)(2,1)S(1)} %get-tuple-element.39.left, ...), custom_call_target="tpu_custom_call", output_to_operand_aliasing={{}: (5, {})} | custom-call | tf_op jit(solution)/shard_map/pallas_call | solution.py:652
  46.6 0.0 copy-done.1
  46.6 0.2 shard_map.150.blocks
  46.8 3.0 %shard_map.148.r_ref = f32[64,64,128]{2,1,0:T(8,128)S(1)} custom-call(f32[256,128]{1,0:T(8,128)S(1)} %get-tuple-element.54.refs_0_, f32[128,128]{1,0:T(8,128)S(1)} %get-tuple-element.55.refs_1_), custom_call_target="tpu_custom_call" | custom-call | tf_op jit(solution)/shard_map/pallas_call | solution.py:639
  49.8 0.5 shard_map.149
  50.3 2.2 %shard_map.151 = f32[1,32,4096]{2,1,0:T(8,128)} custom-call(s32[1,1,32]{2,1,0:T(1,128)S(1)} %get-tuple-element.41.left_pick, s32[1,1,32]{2,1,0:T(1,128)S(1)} %get-tuple-element.42.right_pick, bf16[1536,128]{1,0:T(8,128)(2,1)S(1)} %get-tuple-element.56.left, bf16[1536,128]{1,0:T(8,128)(2,1)S(1)} %get-tuple-element.57.right, ...), custom_call_target="tpu_custom_call" | custom-call | tf_op jit(solution)/shard_map/pallas_call | solution.py:652
  52.5 0.0 collective-permute-done.6.recv
  52.6 3.3 %shard_map.154 = (f32[1,1,4096]{2,1,0:T(1,128)}, f32[1,1,4096]{2,1,0:T(1,128)}) custom-call(f32[64,128]{1,0:T(8,128)S(1)} %shard_map.153.high), custom_call_target="tpu_custom_call" | custom-call | tf_op jit(solution)/shard_map/pallas_call | solution.py:699
  (1 shorter events, 0.0 us)
Async XLA Ops:
  5.7 5.4 %collective-permute-start = (f32[128,128]{1,0:T(8,128)S(1)}, f32[128,128]{1,0:T(8,128)S(1)}, u32[]{:S(2)}, u32[]{:S(2)}) collective-permute-start(f32[128,128]{1,0:T(8,128)S(1)} %get-tuple-element.43.own), channel_id=1, source_target_pairs={{0,8},{8,0},{16,24},{24,16},{1,9},{9,1},{17,25},{25,17},{2,10},{10... | collective-permute-start | bytes 196616 | tf_op jit(solution)/shard_map/ppermute | solution.py:532
  11.6 5.3 %collective-permute-start.1 = (f32[128,128]{1,0:T(8,128)S(1)}, f32[128,128]{1,0:T(8,128)S(1)}, u32[]{:S(2)}, u32[]{:S(2)}) collective-permute-start(f32[128,128]{1,0:T(8,128)S(1)} %get-tuple-element.45.own), channel_id=1, source_target_pairs={{0,16},{8,24},{16,0},{24,8},{1,17},{9,25},{17,1},{25,9},{2,18},{10... | collective-permute-start | bytes 196616 | tf_op jit(solution)/shard_map/ppermute | solution.py:532
  17.4 1.4 %collective-permute-start.2 = (f32[192,128]{1,0:T(8,128)S(1)}, f32[192,128]{1,0:T(8,128)S(1)}, u32[]{:S(2)}, u32[]{:S(2)}) collective-permute-start(f32[192,128]{1,0:T(8,128)S(1)} %get-tuple-element.48.own), channel_id=1, source_target_pairs={{0,1},{1,0},{2,3},{3,2},{4,5},{5,4},{6,7},{7,6},{8,9},{9,8},{10,11... | collective-permute-start | bytes 294920 | tf_op jit(solution)/shard_map/ppermute | solution.py:532
  19.2 5.0 %collective-permute-start.3 = (f32[192,128]{1,0:T(8,128)S(1)}, f32[192,128]{1,0:T(8,128)S(1)}, u32[]{:S(2)}, u32[]{:S(2)}) collective-permute-start(f32[192,128]{1,0:T(8,128)S(1)} %get-tuple-element.50.own), channel_id=1, source_target_pairs={{0,2},{1,3},{2,0},{3,1},{4,6},{5,7},{6,4},{7,5},{8,10},{9,11},{10,... | collective-permute-start | bytes 294920 | tf_op jit(solution)/shard_map/ppermute | solution.py:532
  24.7 5.0 %collective-permute-start.4 = (f32[256,128]{1,0:T(8,128)S(1)}, f32[256,128]{1,0:T(8,128)S(1)}, u32[]{:S(2)}, u32[]{:S(2)}) collective-permute-start(f32[256,128]{1,0:T(8,128)S(1)} %get-tuple-element.52.own), channel_id=1, source_target_pairs={{0,4},{1,5},{2,6},{3,7},{4,0},{5,1},{6,2},{7,3},{8,12},{9,13},{10,... | collective-permute-start | bytes 393224 | tf_op jit(solution)/shard_map/ppermute | solution.py:532
  30.2 4.0 %collective-permute-start.5 = (f32[64,128]{1,0:T(8,128)S(1)}, f32[64,128]{1,0:T(8,128)S(1)}, u32[]{:S(2)}, u32[]{:S(2)}) collective-permute-start(f32[64,128]{1,0:T(8,128)S(1)} %get-tuple-element.58.own), channel_id=1, source_target_pairs={{0,8},{8,0},{16,24},{24,16},{1,9},{9,1},{17,25},{25,17},{2,10},{10... | collective-permute-start | bytes 98312 | tf_op jit(solution)/shard_map/ppermute | solution.py:532
  34.7 17.9 %collective-permute-start.6 = (f32[64,128]{1,0:T(8,128)S(1)}, f32[64,128]{1,0:T(8,128)S(1)}, u32[]{:S(2)}, u32[]{:S(2)}) collective-permute-start(f32[64,128]{1,0:T(8,128)S(1)} %get-tuple-element.60.own), channel_id=1, source_target_pairs={{0,16},{8,24},{16,0},{24,8},{1,17},{9,25},{17,1},{25,9},{2,18},{10... | collective-permute-start | bytes 98312 | tf_op jit(solution)/shard_map/ppermute | solution.py:532
  39.5 2.4 %copy-start = (bf16[1,64,4096]{2,1,0:T(8,128)(2,1)S(1)}, bf16[1,64,4096]{2,1,0:T(8,128)(2,1)}, u32[]{:S(2)}) copy-start(bf16[1,64,4096]{2,1,0:T(8,128)(2,1)} %blocks.4) | copy-start | bytes 1572868
  44.2 2.4 %copy-start.1 = (bf16[1,32,4096]{2,1,0:T(8,128)(2,1)S(1)}, bf16[1,32,4096]{2,1,0:T(8,128)(2,1)}, u32[]{:S(2)}) copy-start(bf16[1,32,4096]{2,1,0:T(8,128)(2,1)} %blocks.5) | copy-start | bytes 786436
